TPU v7x, 32 devices: a whole 2x2x4 slice. The times are simulated.
32 devices in a mesh: dp: 8 (over z, y), tensor: 4 (over x, core).
Axes of the slice: x: 2, y: 2, z: 4, core: 2. Of those that a mesh axis runs over, the one named last changes fastest.
Arguments:
- tokens: bfloat16 [16384, 768], P(('dp', 'tensor')), may hold values from -6 to 6
- grad_out: bfloat16 [16384, 768], P(('dp', 'tensor')), may hold values from -6 to 6
- seg_ids: int32 [16, 1024], P('dp'), may hold values from 0 to 5, never falling along the last dimension, each value on 1 to 800 neighbouring positions
- w_qkv: bfloat16 [3, 768, 768], P(None, 'dp', 'tensor'), may hold values from -0.21875 to 0.21875
- b_qv: bfloat16 [2, 768], P(None, ('tensor', 'dp')), may hold values from -3 to 3
- w_out: bfloat16 [768, 768], P('tensor', 'dp'), may hold values from -1.75 to 1.75
- w_up: bfloat16 [768, 3072], P('dp', 'tensor'), may hold values from -0.21875 to 0.21875
- b_up: bfloat16 [3072], P(('tensor', 'dp')), may hold values from -3 to 3
- w_down: bfloat16 [3072, 768], P('tensor', 'dp'), may hold values from -0.21875 to 0.21875
- b_out: float32 [768], P(('dp', 'tensor')), may hold values from -2 to 2
- b_down: float32 [768], P(('dp', 'tensor')), may hold values from -2 to 2
- g_one: float32 [768], P(('dp', 'tensor')), may hold values from 0.5 to 1.5
- s_one: float32 [768], P(('dp', 'tensor')), may hold values from -2 to 2
- g_two: float32 [768], P(('dp', 'tensor')), may hold values from 0.5 to 1.5
- s_two: float32 [768], P(('dp', 'tensor')), may hold values from -2 to 2
Outputs:
- layer_out: bfloat16 [16384, 768], P(('dp', 'tensor'))
- input_grad: bfloat16 [16384, 768], P(('dp', 'tensor'))
- grad_qkv: float32 [3, 768, 768], P(None, 'dp', 'tensor')
- grad_bias_qv: float32 [2, 768], P(None, ('tensor', 'dp'))
- grad_out_proj: float32 [768, 768], P('tensor', 'dp')
- grad_up: float32 [768, 3072], P('dp', 'tensor')
- grad_bias_up: float32 [3072], P(('tensor', 'dp'))
- grad_down: float32 [3072, 768], P('tensor', 'dp')
- grad_bias_out: float32 [768], P(('dp', 'tensor'))
- grad_bias_down: float32 [768], P(('dp', 'tensor'))
- grad_gain_one: float32 [768], P(('dp', 'tensor'))
- grad_shift_one: float32 [768], P(('dp', 'tensor'))
- grad_gain_two: float32 [768], P(('dp', 'tensor'))
- grad_shift_two: float32 [768], P(('dp', 'tensor'))
Inputs may be any that keep to these rules, and one draw needn't show every extreme that they name: `seg_ids`: within a sequence the ids never fall; each document spans 1 to 800 tokens, and the longest one of a draw spans exactly 800.
All inputs are finite; a program needn't handle non-finite values.
Results may differ from a plain program's by a relative error of at most 0.024.
Values may be sent and summed in bfloat16 or wider, within the bound.
No kernel may reach another device: no remote copies, remote signals or barrier semaphores. Data moves between devices by JAX's collectives and lax.ppermute only.
A program may use at most 128 MiB of HBM per device.

v0:
```python
import functools

import jax
import jax.numpy as jnp
from jax import lax
from jax.experimental import pallas as pl
from jax.experimental.pallas import tpu as pltpu
from jax.sharding import Mesh, PartitionSpec as P

HD = 64
LANES = 128
EPSILON = 1e-05
ROOT_HALF = 0.7071067811865476
INV_ROOT_TWO_PI = 0.3989422804014327
F32 = jnp.float32
BF16 = jnp.bfloat16


def dot(a, b, dims):
    return lax.dot_general(a, b, (dims, ((), ())), preferred_element_type=F32)


def dot_nn(a, b):
    return dot(a, b, ((1,), (0,)))


def dot_nt(a, b):
    return dot(a, b, ((1,), (1,)))


def dot_tn(a, b):
    return dot(a, b, ((0,), (0,)))


CHEAP = pl.CostEstimate(flops=1000, bytes_accessed=1000, transcendentals=0)


def attention_forward_kernel(width, seg_q_ref, seg_k_ref, q_ref, k_ref, v_ref, *refs):
    ctx_ref, lse_ref = refs[-2:]
    lane = lax.broadcasted_iota(jnp.int32, (1, LANES), 1)
    bias = jnp.where(seg_q_ref[...] == seg_k_ref[...], 0.0, -1000000000.0)
    block = q_ref.shape[0]

    stats = jnp.zeros((block, LANES), F32)
    for tile in range(width // LANES):
        cols = slice(tile * LANES, (tile + 1) * LANES)
        q2 = q_ref[:, cols] * jnp.asarray(0.125, BF16)
        k2 = k_ref[:, cols]
        v2 = v_ref[:, cols]
        outs = []
        for half in range(2):
            qm = jnp.where((lane // HD) == half, q2, jnp.zeros_like(q2))
            s = dot_nt(qm, k2) + bias
            top = jnp.max(s, axis=-1, keepdims=True)
            e = jnp.exp(s - top)
            total = jnp.sum(e, axis=-1, keepdims=True)
            outs.append(dot_nn(e.astype(BF16), v2) * (1.0 / total))
            stats = jnp.where(lane == 2 * tile + half, top + jnp.log(total), stats)
        ctx_ref[:, cols] = jnp.where(lane < HD, outs[0], outs[1]).astype(BF16)
    lse_ref[...] = stats.T[: lse_ref.shape[0], :]


def attention_forward(qkv, seg_col, seg_row, block, first, count, made):
    rows, triple = qkv.shape
    width = triple // 3
    return pl.pallas_call(
        functools.partial(attention_forward_kernel, width),
        grid=(count,),
        in_specs=[
            pl.BlockSpec((block, 1), lambda i: (first + i, 0)),
            pl.BlockSpec((1, rows), lambda i: (0, 0)),
            pl.BlockSpec((block, width), lambda i: (first + i, 0)),
            pl.BlockSpec((rows, width), lambda i: (0, 1)),
            pl.BlockSpec((rows, width), lambda i: (0, 2)),
        ]
        + [pl.BlockSpec(memory_space=pl.ANY)] * len(made),
        out_specs=[
            pl.BlockSpec((block, width), lambda i: (first + i, 0)),
            pl.BlockSpec((8, block), lambda i: (0, first + i)),
        ],
        out_shape=[
            jax.ShapeDtypeStruct((rows, width), BF16),
            jax.ShapeDtypeStruct((8, rows), F32),
        ],
        input_output_aliases={5 + i: i for i in range(len(made))},
        cost_estimate=CHEAP,
        name="attention_forward",
    )(seg_col, seg_row, qkv, qkv, qkv, *made)


def split_specs(block, columns, halves):
    return [
        pl.BlockSpec((block, columns), lambda i, *_: (jnp.minimum(i, halves - 1), 0)),
        pl.BlockSpec((block, columns), lambda i, *_: (jnp.maximum(i - halves, 0), 0)),
    ]


def either(step, halves, own_ref, other_ref):
    return jnp.where(step < halves, own_ref[...], other_ref[...])


def attention_backward_kernel(
    width, halves, seg_k_ref, seg_q_ref, q_ref, k_ref, v_ref, ctx_ref, lse_ref, own_ref, other_ref, out_ref, sum_ref, dk_ref, dv_ref
):
    step = pl.program_id(0)
    block = q_ref.shape[0]
    lane = lax.broadcasted_iota(jnp.int32, (1, LANES), 1)

    @pl.when(step == 0)
    def _():
        dk_ref[...] = jnp.zeros_like(dk_ref)
        dv_ref[...] = jnp.zeros_like(dv_ref)
        sum_ref[...] = jnp.zeros_like(sum_ref)

    bias = jnp.where(seg_k_ref[...] == seg_q_ref[...], 0.0, -1000000000.0)
    for pair in range(width // LANES):
        cols = slice(pair * LANES, (pair + 1) * LANES)
        q2 = q_ref[:, cols] * jnp.asarray(0.125, BF16)
        k2 = k_ref[:, cols]
        v2 = v_ref[:, cols]
        d2 = jnp.where(step < halves, own_ref[:, cols], other_ref[:, cols])
        prod = (d2.astype(F32) * ctx_ref[:, cols].astype(F32)).T
        kt = (k2 * jnp.asarray(0.125, BF16)).T
        row = lax.broadcasted_iota(jnp.int32, (LANES, 1), 0)
        dq = None
        dk = None
        dv = None
        for half in range(2):
            mine = (lane // HD) == half
            qm = jnp.where(mine, q2, jnp.zeros_like(q2))
            dm = jnp.where(mine, d2, jnp.zeros_like(d2))
            ktm = jnp.where((row // HD) == half, kt, jnp.zeros_like(kt))
            inner = jnp.sum(prod[half * HD : (half + 1) * HD, :], axis=0, keepdims=True)
            lse = lse_ref[2 * pair + half : 2 * pair + half + 1, :]
            p = jnp.exp(dot_nt(k2, qm) + bias - lse)
            dp = dot_nt(v2, dm)
            ds = (p * (dp - inner)).astype(BF16)
            dv_h = dot_nn(p.astype(BF16), dm)
            dk_h = dot_nn(ds, qm)
            dq_h = dot_nn(ktm, ds)
            dv = dv_h if dv is None else dv + dv_h
            dk = dk_h if dk is None else dk + dk_h
            dq = dq_h if dq is None else dq + dq_h
        dk_ref[:, cols] += dk
        dv_ref[:, cols] += dv
        dq = dq.T.astype(BF16)
        out_ref[pl.ds(pl.multiple_of(step * block, block), block), cols] = dq
        sum_ref[:, cols] += jnp.sum(dq.astype(F32), axis=0, keepdims=True)

    @pl.when(step == pl.num_programs(0) - 1)
    def _():
        out_ref[:, width : 2 * width] = dk_ref[...].astype(BF16)
        dv = dv_ref[...].astype(BF16)
        out_ref[:, 2 * width : 3 * width] = dv
        sum_ref[:, width : 2 * width] = jnp.sum(dv.astype(F32), axis=0, keepdims=True)


def attention_backward(qkv, ctx, lse, d_own, d_other, seg_col, seg_row, block):
    rows, triple = qkv.shape
    width = triple // 3
    halves = rows // block // 2
    return pl.pallas_call(
        functools.partial(attention_backward_kernel, width, halves),
        grid=(rows // block,),
        in_specs=[
            pl.BlockSpec((rows, 1), lambda i: (0, 0)),
            pl.BlockSpec((1, block), lambda i: (0, i)),
            pl.BlockSpec((block, width), lambda i: (i, 0)),
            pl.BlockSpec((rows, width), lambda i: (0, 1)),
            pl.BlockSpec((rows, width), lambda i: (0, 2)),
            pl.BlockSpec((block, width), lambda i: (i, 0)),
            pl.BlockSpec((8, block), lambda i: (0, i)),
            *split_specs(block, width, halves),
        ],
        out_specs=[pl.BlockSpec((rows, triple), lambda i: (0, 0)), pl.BlockSpec((1, 2 * width), lambda i: (0, 0))],
        out_shape=[jax.ShapeDtypeStruct((rows, triple), BF16), jax.ShapeDtypeStruct((1, 2 * width), F32)],
        scratch_shapes=[pltpu.VMEM((rows, width), F32), pltpu.VMEM((rows, width), F32)],
        cost_estimate=CHEAP,
        name="attention_backward",
    )(seg_col, seg_row, qkv, qkv, qkv, ctx, lse, d_own, d_other)


def input_kernel(halves, d_ref, first_ref, w_ref, keep_ref, send_ref):
    step = pl.program_id(0)
    part = dot_nt(d_ref[...], w_ref[...])

    @pl.when(step < halves)
    def _():
        keep_ref[...] = first_ref[...] + part

    @pl.when(step >= halves)
    def _():
        send_ref[...] = part.astype(BF16)


def input_gradient(d_qkv, d_first, w_all, block):
    rows, model = d_first.shape
    width = d_qkv.shape[1]
    halves = rows // block
    by_row = pl.BlockSpec((block, width), lambda i: (i, 0))
    own = pl.BlockSpec((block, model), lambda i: (jnp.minimum(i, halves - 1), 0))
    return pl.pallas_call(
        functools.partial(input_kernel, halves),
        grid=(2 * halves,),
        in_specs=[by_row, own, pl.BlockSpec(w_all.shape, lambda i: (0, 0))],
        out_specs=split_specs(block, model, halves),
        out_shape=[jax.ShapeDtypeStruct((rows, model), F32), jax.ShapeDtypeStruct((rows, model), BF16)],
        cost_estimate=CHEAP,
        name="input_gradient",
    )(d_qkv, d_first, w_all)


def normalize(r):
    mean = jnp.mean(r, axis=-1, keepdims=True)
    cent = r - mean
    var = jnp.mean(cent * cent, axis=-1, keepdims=True)
    inv = lax.rsqrt(var + EPSILON)
    return cent * inv, inv


def normalize_back(hat, inv, gain, d_out):
    d_hat = d_out * gain
    first = jnp.mean(d_hat, axis=-1, keepdims=True)
    second = jnp.mean(d_hat * hat, axis=-1, keepdims=True)
    return inv * (d_hat - first - hat * second)


def swap(a):
    return lax.ppermute(a, "c", [(0, 1), (1, 0)])


def flip(a, axis, bit):
    n = lax.axis_size(axis)
    return lax.ppermute(a, axis, [(i, i ^ bit) for i in range(n)])


def turn(a, level):
    n, nx = lax.axis_size("dp"), lax.axis_size("x")
    pairs = []
    for d in range(n):
        for x in range(nx):
            for c in range(2):
                other = (d * nx + (x ^ 1)) if (c + level) % 2 == 0 else ((d ^ 1) * nx + x)
                pairs.append(((d * nx + x) * 2 + c, other * 2 + c))
    return lax.ppermute(a, ("dp", "x", "c"), pairs)


def tie(*values):
    return lax.optimization_barrier(values)


def add(*terms):
    return sum(t.astype(F32) for t in terms).astype(BF16)


def outer_bits():
    return lax.axis_size("dp").bit_length() - 2


def gather_far(near):
    parts = [near]
    for k in range(1, outer_bits()):
        held = jnp.concatenate(parts) if len(parts) > 1 else near
        parts.append(flip(held, "dp", 2 << k))
    return jnp.concatenate(parts[1:]) if len(parts) > 2 else parts[1]


OPT = {'bc': None, 'bn1': 'qkv', 'bz2': 'qkv', 'bf1': 'ctx', 'bn2': 'ctx', 'bf2': 'attn', 'c1': 'P3', 'c2': 'P4', 'b1': 'P3', 'b2': 'P4', 'c3': 'P5', 'b3': 'P6', 'an2': 'f1', 'bz1': 'f1'}


def stage(name, *values, **items):
    keys = [k for k in items if OPT.get(k) == name]
    extra, spans = [], []
    for k in keys:
        v = getattr(*items[k])
        many = isinstance(v, list)
        spans.append((k, len(v) if many else 1, many))
        extra += v if many else [v]
    if len(values) + len(extra) > 1:
        out = list(tie(*values, *extra))
    else:
        out = [*values, *extra]
    res, at = out[: len(values)], len(values)
    for k, n, many in spans:
        setattr(*items[k], out[at : at + n] if many else out[at])
        at += n
    return res if len(res) > 1 else (res[0] if res else None)


class Spread:
    def __init__(self, units, outer):
        self.units, self.outer = units, outer

    def first(self):
        self.one = turn(self.units, 0)

    def second(self):
        self.two = turn(jnp.concatenate([self.units, self.one]), 1)

    def pieces(self):
        n = self.units.shape[0]
        index = [(0, u, self.outer + u, 0, 0) for u in range(n)]
        index += [(1, u, self.outer + u, 1, 0) for u in range(n)]
        index += [(2, a * n + u, self.outer + u, a, 1) for a in range(2) for u in range(n)]
        return [self.units, self.one, self.two], index


def joined(spreads):
    arrays, index = [], []
    for s in spreads:
        more, at = s.pieces()
        index += [(i + len(arrays), *rest) for i, *rest in at]
        arrays += more
    return arrays, index


def put_units(index, moves, where_ref, ins, outs, each=None):
    dp = where_ref[0]
    for parity in range(2):

        @pl.when(where_ref[1] == parity)
        def _():
            for array, unit, outer, first, second in index:
                rx, ry = (second, first) if parity else (first, second)
                to = jnp.bitwise_xor(dp, 2 * outer + ry)
                for lead, rows, col, cols, target, at in moves:
                    value = ins[array][(unit, *lead, slice(0, rows), slice(col, col + cols))]
                    outs[target][pl.ds(pl.multiple_of(to * rows, 16), rows), at[rx] : at[rx] + cols] = value
                if each is not None:
                    each(ins[array], unit, to, rx)


def prepare_kernel(piece, dp_ref, qkv_ref, out_ref, up_ref, down_ref, qv_ref, *refs):
    vectors, (a_ref, bc_ref, row_ref) = refs[:-3], refs[-3:]
    part = qkv_ref.shape[2]
    for j in range(3):
        a_ref[:piece, j * part : (j + 1) * part] = qkv_ref[j]
    a_ref[:piece, 3 * part :] = out_ref[...].T
    row_ref[...] = jnp.zeros_like(row_ref)
    at = 0
    for v in vectors:
        n = v.shape[1]
        row_ref[0:1, at : at + n] = v[...].astype(F32)
        at += n
    n = qv_ref.shape[1]
    lane = lax.broadcasted_iota(jnp.int32, (n, part), 1)
    spot = (lane == lax.broadcasted_iota(jnp.int32, (n, part), 0) + n * dp_ref[0]).astype(BF16)
    both = dot_nn(qv_ref[...], spot)
    row_ref[1:2, :part] = both[0:1]
    row_ref[1:2, part : 2 * part] = both[1:2]
    exact = row_ref[0:1, :]
    high = exact.astype(BF16).astype(F32)
    middle = (exact - high).astype(BF16).astype(F32)
    low = exact - high - middle
    line = lax.broadcasted_iota(jnp.int32, (8, 1), 0)
    rows = jnp.where(line == 0, high, 0.0) + jnp.where(line == 1, middle, 0.0)
    rows += jnp.where(line == 2, low, 0.0) + jnp.where(line == 3, row_ref[1:2, :], 0.0)
    a_ref[piece:, :] = rows.astype(BF16)
    bc_ref[0] = up_ref[...]
    bc_ref[1] = down_ref[...].T


def prepare(w_qkv, w_out, w_up, w_down, b_qv, vectors):
    piece, part = w_qkv.shape[1:]
    model = w_up.shape[1]
    dp = lax.axis_index("dp").astype(jnp.int32)
    if piece % 16 == 0:

        def whole(s):
            return pl.BlockSpec(s, lambda i, d: (0,) * len(s))

        given = [w_qkv, w_out, w_up, w_down, b_qv, *[v[None] for v in vectors]]
        shapes = [(piece + 8, model), (2, piece, model)]
        return pl.pallas_call(
            functools.partial(prepare_kernel, piece),
            grid_spec=pltpu.PrefetchScalarGridSpec(
                num_scalar_prefetch=1,
                grid=(1,),
                in_specs=[whole(v.shape) for v in given],
                out_specs=[whole(s) for s in shapes],
                scratch_shapes=[pltpu.VMEM((8, model), F32)],
            ),
            out_shape=[jax.ShapeDtypeStruct(s, BF16) for s in shapes],
            cost_estimate=CHEAP,
            name="prepare_units",
        )(dp[None], *given)
    row = jnp.concatenate([v.astype(F32) for v in vectors])
    row = jnp.pad(row, (0, model - row.shape[0]))
    high = row.astype(BF16)
    middle = (row - high.astype(F32)).astype(BF16)
    low = (row - high.astype(F32) - middle.astype(F32)).astype(BF16)
    keep = lax.broadcasted_iota(jnp.int32, (1, part // b_qv.shape[1], 1), 1) == dp
    spot = jnp.where(keep, b_qv[:, None, :], jnp.zeros((), BF16)).reshape(-1)
    spot = jnp.pad(spot, (0, model - spot.shape[0]))
    tail = jnp.pad(jnp.stack([high, middle, low, spot]), ((0, 4), (0, 0)))
    unit = jnp.concatenate([w_qkv[0], w_qkv[1], w_qkv[2], w_out.T], axis=1)
    return jnp.concatenate([unit, tail], axis=0), jnp.stack([w_up, w_down.T])


def project_kernel(index, moves, piece, part, halves, where_ref, own_ref, other_ref, *refs):
    ins, (out_ref, w_ref, o_ref, ext_ref, bias_ref) = refs[:-5], refs[-5:]
    width = 2 * part

    @pl.when(pl.program_id(0) == 0)
    def _():
        bias_ref[...] = jnp.zeros_like(bias_ref)

        def each(source, unit, to, rx):
            value = source[unit, piece:, : 2 * part]
            ext_ref[to, :, 2 * part * rx : 2 * part * (rx + 1)] = value
            value = value.astype(F32)[3:4]
            bias_ref[0:1, rx * part : (rx + 1) * part] += value[:, :part]
            at = 2 * width + rx * part
            bias_ref[0:1, at : at + part] += value[:, part:]

        put_units(index, moves, where_ref, ins, (w_ref, o_ref), each)

    x = either(pl.program_id(0), halves, own_ref, other_ref)
    out_ref[...] = (dot_nn(x, w_ref[...]) + bias_ref[0:1, :]).astype(BF16)


def feed_kernel(index, moves, halves, where_ref, own_ref, other_ref, bias_ref, *refs):
    ins, (hidden_ref, slope_ref, keep_ref, send_ref, b_ref, c_ref) = refs[:-6], refs[-6:]
    step = pl.program_id(0)

    @pl.when(step == 0)
    def _():
        put_units(index, moves, where_ref, ins, (b_ref, c_ref))

    x = either(step, halves, own_ref, other_ref)
    hidden, slope = gelu_both(dot_nn(x, b_ref[...]) + bias_ref[...])
    hidden_ref[...] = hidden
    slope_ref[...] = slope
    part = dot_nt(hidden, c_ref[...])

    @pl.when(step < halves)
    def _():
        keep_ref[...] = part

    @pl.when(step >= halves)
    def _():
        send_ref[...] = part.astype(BF16)


def chunks(n, size=512):
    return [slice(at, min(at + size, n)) for at in range(0, n, size)]


def gelu_both(up):
    cdf = 0.5 * (1.0 + lax.erf(up * ROOT_HALF))
    slope = cdf + up * (jnp.exp(-0.5 * up * up) * INV_ROOT_TWO_PI)
    return (up * cdf).astype(BF16), slope.astype(BF16)


def feed_back_kernel(size, piece, where_ref, *refs):
    own_ref, other_ref, n_own_ref, n_other_ref, slope_ref, hidden_ref, c_ref, b_ref = refs[:8]
    keep_ref, send_ref, sum_ref, c_keep, c_send, b_keep, b_send = refs[8:15]
    d_ref, d_turned, n_turned, acc_ref, c_grad, b_grad = refs[15:]
    step, dp = pl.program_id(0), where_ref[0]
    half, model = own_ref.shape
    outer = c_keep.shape[0] // 2

    @pl.when(step == 0)
    def _():
        for at, d, n in ((0, own_ref, n_own_ref), (half, other_ref, n_other_ref)):
            d_ref[at : at + half, :] = d[...]
            d_turned[:, at : at + half] = d[...].T
            n_turned[:, at : at + half] = n[...].T

    d_up = (dot_nn(d_ref[...], c_ref[...]) * slope_ref[...].astype(F32)).astype(BF16)
    sum_ref[...] = jnp.sum(d_up.astype(F32), axis=0, keepdims=True)
    part = dot_nt(d_up, b_ref[...])

    @pl.when(step == 0)
    def _():
        acc_ref[...] = part

    @pl.when(step > 0)
    def _():
        acc_ref[...] += part

    c_grad[...] = dot_nn(d_turned[...], hidden_ref[...]).astype(BF16)
    b_grad[...] = dot_nn(n_turned[...], d_up).astype(BF16)
    width = c_ref.shape[1]
    for s in range(2 * model // width):
        for at in range(0, width, size):
            rx, to = divmod(s * width + at, model)
            for parity in range(2):

                @pl.when((step == s) & (where_ref[1] == parity))
                def _():
                    for ry in range(2):
                        first, second = (ry, rx) if parity else (rx, ry)
                        outs = ((c_send, b_send) if first else (c_keep, b_keep))

                        def move(z, carry):
                            rows = pl.ds(pl.multiple_of(jnp.bitwise_xor(dp, 2 * z + ry) * piece, 16), piece)
                            for out, grad in zip(outs, (c_grad, b_grad)):
                                out[second * outer + z, :, to : to + size] = grad[rows, at : at + size]
                            return carry

                        lax.fori_loop(0, outer, move, 0)

    @pl.when(step == pl.num_programs(0) - 1)
    def _():
        keep_ref[...] = acc_ref[:half, :]
        send_ref[...] = acc_ref[half:, :].astype(BF16)


def feed_back(d_own, d_other, n_own, n_other, slope, hidden, c, b, piece):
    rows, model = d_own.shape
    wide = b.shape[1]
    ndp = model // piece
    if piece % 16:
        d, n = jnp.concatenate([d_own, d_other]), jnp.concatenate([n_own, n_other])
        d_up = (dot_nn(d, c) * slope.astype(F32)).astype(BF16)
        part = dot_nt(d_up, b)
        sums = jnp.sum(d_up.astype(F32), axis=0, keepdims=True)
        wide_part = [((0, 1), 2, model, 0, True)]
        c_pair = summed([d_own, d_other, hidden], wide_part)
        b_pair = summed([n_own, n_other, d_up], wide_part)
        return part[:rows], part[rows:].astype(BF16), sums, *c_pair, *b_pair

    def whole(s):
        return pl.BlockSpec(s, lambda i, w: (0,) * len(s))

    def columns(n):
        return pl.BlockSpec((n, 512), lambda i, w: (0, i))

    units = (ndp, piece, model)
    return pl.pallas_call(
        functools.partial(feed_back_kernel, 256, piece),
        grid_spec=pltpu.PrefetchScalarGridSpec(
            num_scalar_prefetch=1,
            grid=(wide // 512,),
            in_specs=[whole((rows, model))] * 4 + [columns(2 * rows)] * 2 + [columns(model)] * 2,
            out_specs=[whole((rows, model))] * 2 + [columns(1)] + [whole(units)] * 4,
            scratch_shapes=[
                pltpu.VMEM((2 * rows, model), BF16),
                pltpu.VMEM((model, 2 * rows), BF16),
                pltpu.VMEM((model, 2 * rows), BF16),
                pltpu.VMEM((2 * rows, model), F32),
                pltpu.VMEM((model, 512), BF16),
                pltpu.VMEM((model, 512), BF16),
            ],
        ),
        out_shape=[
            jax.ShapeDtypeStruct((rows, model), F32),
            jax.ShapeDtypeStruct((rows, model), BF16),
            jax.ShapeDtypeStruct((1, wide), F32),
        ]
        + [jax.ShapeDtypeStruct(units, BF16)] * 4,
        cost_estimate=CHEAP,
        name="feed_back",
    )(where(), d_own, d_other, n_own, n_other, slope, hidden, c, b)


def ordered(spreads, moves):
    arrays, index = joined(spreads)
    order = jnp.bitwise_xor(jnp.arange(lax.axis_size("dp")), lax.axis_index("dp"))
    made = {}
    for lead, rows, col, cols, target, at in moves:
        for rx in range(2):
            both = []
            for swapped in range(2):
                units = {}
                for array, unit, outer, first, second in index:
                    x, y = (second, first) if swapped else (first, second)
                    if x == rx:
                        units[2 * outer + y] = arrays[array][(unit, *lead)][rows, col : col + cols]
                both.append(jnp.stack([units[k] for k in sorted(units)]))
            stack = jnp.take(jnp.where(lax.axis_index("c") == 0, both[0], both[1]), order, axis=0)
            made.setdefault(target, []).append((at[rx], stack))
    return [jnp.concatenate([m for _, m in sorted(made[t], key=lambda p: p[0])], axis=-1) for t in sorted(made)]


def project(spreads, own, other, piece, part, block):
    width = 2 * part
    rows, model = own.shape
    halves = rows // block
    moves = [((), piece, j * part, part, 0, (j * width, j * width + part)) for j in range(3)]
    moves.append(((), piece, 3 * part, part, 1, (0, part)))
    if piece % 16 == 0:
        arrays, index = joined(spreads)

        def whole(s):
            return pl.BlockSpec(s, lambda i, d: (0,) * len(s))

        shapes = [(model, 3 * width), (model, width), (model // piece, 8, 2 * width)]
        return pl.pallas_call(
            functools.partial(project_kernel, index, moves, piece, part, halves),
            grid_spec=pltpu.PrefetchScalarGridSpec(
                num_scalar_prefetch=1,
                grid=(2 * halves,),
                in_specs=split_specs(block, model, halves) + [whole(a.shape) for a in arrays],
                out_specs=[pl.BlockSpec((block, 3 * width), lambda i, d: (i, 0))] + [whole(s) for s in shapes],
                scratch_shapes=[pltpu.VMEM((8, 3 * width), F32)],
            ),
            out_shape=[jax.ShapeDtypeStruct(s, BF16) for s in [(2 * rows, 3 * width), *shapes]],
            cost_estimate=CHEAP,
            name="project_kernel",
        )(where(), own, other, *arrays)
    slices = [(lead, slice(0, n), *rest) for lead, n, *rest in moves]
    slices.append(((), slice(piece, piece + 8), 0, 2 * part, 2, (0, 2 * part)))
    w, o, ext = ordered(spreads, slices)
    bias = jnp.sum(ext[:, 3].astype(F32), axis=0).reshape(2, 2, part)
    bias = jnp.concatenate([bias[:, 0].reshape(-1), jnp.zeros((width,), F32), bias[:, 1].reshape(-1)])
    w, o = w.reshape(model, -1), o.reshape(model, -1)
    return (dot_nn(jnp.concatenate([own, other]), w) + bias[None]).astype(BF16), w, o, ext


def feed(spreads, own, other, bias, piece, block):
    rows, model = own.shape
    halves = rows // block
    moves = [((k,), piece, 0, model, k, (0, model)) for k in range(2)]
    if piece % 16 == 0:
        arrays, index = joined(spreads)

        def whole(s):
            return pl.BlockSpec(s, lambda i, d: (0,) * len(s))

        wide = pl.BlockSpec((block, 2 * model), lambda i, d: (i, 0))
        return pl.pallas_call(
            functools.partial(feed_kernel, index, moves, halves),
            grid_spec=pltpu.PrefetchScalarGridSpec(
                num_scalar_prefetch=1,
                grid=(2 * halves,),
                in_specs=split_specs(block, model, halves) + [whole(a.shape) for a in [bias, *arrays]],
                out_specs=[wide, wide, *split_specs(block, model, halves)] + [whole((model, 2 * model))] * 2,
            ),
            out_shape=[jax.ShapeDtypeStruct((2 * rows, 2 * model), BF16)] * 2
            + [jax.ShapeDtypeStruct((rows, model), F32), jax.ShapeDtypeStruct((rows, model), BF16)]
            + [jax.ShapeDtypeStruct((model, 2 * model), BF16)] * 2,
            cost_estimate=CHEAP,
            name="feed_kernel",
        )(where(), own, other, bias, *arrays)
    b, c = ordered(spreads, [(lead, slice(0, n), *rest) for lead, n, *rest in moves])
    b, c = b.reshape(model, -1), c.reshape(model, -1)
    hidden, slope = gelu_both(dot_nn(jnp.concatenate([own, other]), b) + bias)
    part = dot_nt(hidden, c)
    return hidden, slope, part[:rows], part[rows:].astype(BF16), b, c


def pull(own, other, slope, c, b, block):
    rows, model = own.shape
    wide = b.shape[1]
    halves = rows // block

    def whole(s):
        return pl.BlockSpec(s, lambda i: (0, 0))

    by_row = pl.BlockSpec((block, wide), lambda i: (i, 0))
    return pl.pallas_call(
        functools.partial(pull_kernel, halves),
        grid=(2 * halves,),
        in_specs=[*split_specs(block, model, halves), by_row, whole(c.shape), whole(b.shape)],
        out_specs=[by_row, *split_specs(block, model, halves), whole((1, wide))],
        out_shape=[
            jax.ShapeDtypeStruct((2 * rows, wide), BF16),
            jax.ShapeDtypeStruct((rows, model), F32),
            jax.ShapeDtypeStruct((rows, model), BF16),
            jax.ShapeDtypeStruct((1, wide), F32),
        ],
        cost_estimate=CHEAP,
        name="pull_kernel",
    )(own, other, slope, c, b)


def where():
    return jnp.stack([lax.axis_index("dp"), lax.axis_index("c")]).astype(jnp.int32)


def sum_kernel(parts, piece, extra, part, where_ref, *refs):
    count = 1 + max(max(*p[0], p[1]) for p in parts)
    ins = refs[:count]
    scratch = refs[count + (2 if extra else 0) :]
    outs, left_ref, acc, ext_ref = scratch[:2], scratch[2], scratch[3], scratch[4]
    dp, step = where_ref[0], pl.program_id(0)
    outer = outs[0].shape[0] // 2
    blocked = parts[0][4]
    if extra:
        lines_ref, bias_ref = refs[count : count + 2]
        ext_ref[...] = lines_ref[...].astype(F32)
        for rx in range(2):
            for k in range(2):
                ext_ref[rx, extra - 1 : extra, k * part : (k + 1) * part] = bias_ref[
                    0:1, (2 * k + rx) * part : (2 * k + rx + 1) * part
                ]

    def turned(own, other):
        half = ins[own].shape[0]
        left_ref[:, :half] = ins[own][...].T
        left_ref[:, half:] = ins[other][...].T

    for k, ((own, other), right, width, at, by_block) in enumerate(parts):
        if by_block:

            @pl.when(step == 0)
            def _():
                turned(own, other)

            for lanes in chunks(width, 256):
                acc[:, lanes] = dot_nn(left_ref[...], ins[right][:, lanes]).astype(BF16)
        else:

            @pl.when(step == 0)
            def _():
                if k == 0 or parts[k - 1][0] != (own, other):
                    turned(own, other)
                for j in range(ins[right].shape[1] // (2 * width)):
                    both = dot_nn(left_ref[...], ins[right][:, 2 * j * width : 2 * (j + 1) * width]).astype(BF16)
                    for rx in range(2):
                        lanes = slice(rx * acc.shape[1] // 2 + at + j * width, rx * acc.shape[1] // 2 + at + (j + 1) * width)
                        acc[:, lanes] = both[:, rx * width : (rx + 1) * width]

    span = outs[0].shape[2]

    def put(rx):
        lanes = slice(0, span) if blocked else slice(rx * span, (rx + 1) * span)
        for parity in range(2):

            @pl.when(where_ref[1] == parity)
            def _():
                for ry in range(2):
                    first, second = (ry, rx) if parity else (rx, ry)

                    def move(z, carry):
                        rows = pl.ds(pl.multiple_of(jnp.bitwise_xor(dp, 2 * z + ry) * piece, 16), piece)
                        outs[first][second * outer + z, :piece, :] = acc[rows, lanes]
                        if extra:
                            outs[first][second * outer + z, piece:, :] = ext_ref[rx].astype(BF16)
                        return carry

                    lax.fori_loop(0, outer, move, 0)

    for rx in range(2):
        if blocked:
            pl.when(step == rx)(functools.partial(put, rx))
        else:
            put(rx)


def summed(arrays, parts, ext=None, bias=None):
    ndp = lax.axis_size("dp")
    model = arrays[0].shape[1]
    piece = model // ndp
    blocked = parts[0][4]
    width = sum(p[2] if p[4] else arrays[p[1]].shape[1] // 2 for p in parts)
    extra = 0 if ext is None else ext.shape[1]
    if piece % 16 == 0:

        def whole(s):
            return pl.BlockSpec(s, lambda i, d: (0,) * len(s))

        given = list(arrays) + ([] if ext is None else [ext, bias])
        specs = [whole(a.shape) for a in given]
        if blocked:
            right = parts[0][1]
            specs[right] = pl.BlockSpec((arrays[right].shape[0], width), lambda i, d: (0, i))
        shape = (ndp, piece + extra, width)
        return pl.pallas_call(
            functools.partial(sum_kernel, parts, piece, extra, 0 if bias is None else bias.shape[1] // 4),
            grid_spec=pltpu.PrefetchScalarGridSpec(
                num_scalar_prefetch=1,
                grid=(2 if blocked else 1,),
                in_specs=specs,
                out_specs=[whole(shape)] * 2,
                scratch_shapes=[
                    pltpu.VMEM((model, 2 * arrays[0].shape[0]), BF16),
                    pltpu.VMEM((model, width if blocked else 2 * width), BF16),
                    pltpu.VMEM((2, max(extra, 8), width), F32),
                ],
            ),
            out_shape=[jax.ShapeDtypeStruct(shape, BF16)] * 2,
            cost_estimate=CHEAP,
            name="sum_units",
        )(where(), *given)
    order = jnp.bitwise_xor(jnp.arange(ndp), lax.axis_index("dp"))
    sides = []
    if extra:
        line = jnp.transpose(bias.reshape(2, 2, -1), (1, 0, 2)).reshape(2, -1)
        line = jnp.pad(line, ((0, 0), (0, width - line.shape[1]))).astype(BF16)
        ext = jnp.concatenate([ext[:, :-1], line[:, None]], axis=1)
    for rx in range(2):
        g = []
        for (own, other), right, cols, _, by_block in parts:
            left = jnp.concatenate([arrays[own], arrays[other]])
            for j in range(1 if by_block else arrays[right].shape[1] // (2 * cols)):
                at = (2 * j + rx) * cols
                g.append(dot_tn(left, arrays[right][:, at : at + cols]).astype(BF16))
        g = jnp.concatenate(g, axis=1).reshape(ndp, piece, width)
        if extra:
            g = jnp.concatenate([g, jnp.broadcast_to(ext[rx][None], (ndp, extra, width))], axis=1)
        g = jnp.take(g, order, axis=0).reshape(ndp // 2, 2, piece + extra, width)
        sides.append(jnp.moveaxis(g, 1, 0))
    g = jnp.stack(sides)
    g = jnp.where(lax.axis_index("c") == 0, g, jnp.swapaxes(g, 0, 1))
    return g[0].reshape(ndp, piece + extra, width), g[1].reshape(ndp, piece + extra, width)


class Scatter:
    def __init__(self, pair):
        self.keep, self.send = pair

    def first(self):
        self.one = turn(self.send, 0)

    def second(self):
        half = self.keep.shape[0] // 2
        self.kept = add(self.keep[:half], self.one[:half])
        self.two = turn(add(self.keep[half:], self.one[half:]), 1)

    def third(self):
        total = add(self.kept, self.two)
        outer = total.shape[0]
        if outer <= 4:
            self.last = [total[0]]
            self.three = [flip(total[k], "dp", 2 * k) for k in range(1, outer)]
            return
        for k in reversed(range(outer_bits())):
            half = total.shape[0] // 2
            total = add(total[:half], flip(total[half:], "dp", 2 << k))
        self.last, self.three = [total[0]], []

    def result(self):
        return sum(t.astype(F32) for t in self.last + self.three)


def local(
    tokens, grad_out, seg_ids, w_qkv, b_qv, w_out, w_up, b_up, w_down, b_out, b_down, g_one, s_one, g_two, s_two
):
    ndp = lax.axis_size("dp")
    nx = lax.axis_size("x")
    parity = lax.axis_index("c")
    which = lax.axis_index("x")
    place_dp = lax.axis_index("dp")
    rows, model = tokens.shape
    piece = model // ndp
    part = w_qkv.shape[2]
    width = nx * part
    slim = model // (ndp * nx * 2)
    qv = part // ndp
    extra = 8
    block = 256
    tall = 512

    unit_a, unit_bc = prepare(
        w_qkv, w_out, w_up, w_down, b_qv, [b_out, b_down, g_one, s_one, g_two, s_two, b_up]
    )
    a_near = Spread(jnp.stack([unit_a, flip(unit_a, "dp", 2)]), 0)

    class Box:
        pass

    box = Box()
    box.bc = unit_bc
    a_near.units = stage("z1", a_near.units, bc=(box, "bc"))
    a_far = Spread(gather_far(a_near.units), 2)
    a_near.first()
    a_near.one = stage("n1", a_near.one, bc=(box, "bc"), az=(a_far, "units"))
    a_near.second()
    a_far.units = stage("z2", a_far.units, bc=(box, "bc"), an2=(a_near, "two"))
    a_far.first()
    bc_near = Spread(jnp.stack([box.bc, flip(box.bc, "dp", 2)]), 0)
    a_far.one = stage("f1", a_far.one, bz1=(bc_near, "units"), an2=(a_near, "two"))
    a_far.second()
    bc_far = Spread(gather_far(bc_near.units), 2)
    bc_items = lambda: dict(bn1=(bc_near, "one"), bz2=(bc_far, "units"), bn2=(bc_near, "two"), bf1=(bc_far, "one"), bf2=(bc_far, "two"))
    done = set()

    def advance(name, *values):
        res = stage(name, *values, **{k: v for k, v in bc_items().items() if hasattr(*v)})
        order = ["z2", "f1", "f2", "qkv", "ctx", "attn", "normed", "feed"]
        at = order.index(name)
        ready = lambda k: k is None or order.index(OPT.get(k, "feed")) <= at
        if "n1" not in done and order.index(OPT.get("rn1", "z2")) <= at:
            bc_near.first()
            done.add("n1")
        if "n2" not in done and "n1" in done and (ready("bn1") or name == "feed"):
            bc_near.second()
            done.add("n2")
        if "f1" not in done and (ready("bz2") or name == "feed"):
            bc_far.first()
            done.add("f1")
        if "f2" not in done and "f1" in done and (ready("bf1") or name == "feed"):
            bc_far.second()
            done.add("f2")
        return res

    advance("z2")
    a_far.two = advance("f2", a_far.two)

    seg = lax.dynamic_index_in_dim(seg_ids, which, 0, keepdims=False).reshape(2, rows)
    seg_rel = jnp.concatenate(
        [
            lax.dynamic_index_in_dim(seg, parity, 0, keepdims=False),
            lax.dynamic_index_in_dim(seg, 1 - parity, 0, keepdims=False),
        ]
    )
    seg_col = seg_rel[:, None]
    seg_row = seg_rel[None, :]
    x_other = swap(tokens)

    qkv, w_all, o_t, ext = project([a_near, a_far], tokens, x_other, piece, part, block)
    ext = ext[:, :3].astype(F32)
    ext = (ext[:, 0] + ext[:, 1] + ext[:, 2]).reshape(ndp, nx, 2 * part)
    bias_up = jnp.transpose(ext[:, :, 6 * slim : 6 * slim + piece], (1, 0, 2)).reshape(1, nx * model)
    six = ext[:, :, : 6 * slim]
    six = jnp.stack([six, swap(six)], axis=2)
    six = jnp.where(lax.broadcasted_iota(jnp.int32, (1, 1, 2, 1), 2) == parity, six[:, :, :1], six[:, :, 1:])
    six = jnp.where(which == 0, six, six[:, ::-1]).reshape(ndp * nx * 2, 6, slim)
    vectors = jnp.transpose(six, (1, 0, 2)).reshape(6, model)
    bout_f, bdown_f, gone_f, sone_f, gtwo_f, stwo_f = [vectors[i : i + 1] for i in range(6)]

    qkv = advance("qkv", qkv)
    ctx, lse = attention_forward(qkv, seg_col, seg_row, tall, 0, 2 * rows // tall, ())
    ctx = advance("ctx", ctx)
    attn_send = dot_nt(ctx[rows:], o_t).astype(BF16)
    attn = dot_nt(ctx[:rows], o_t) + swap(attn_send).astype(F32)
    attn = advance("attn", attn)
    first = tokens.astype(F32) + attn + bout_f
    hat_one, inv_one = normalize(first)
    normed = hat_one * gone_f + sone_f
    normed_low = advance("normed", normed.astype(BF16))
    normed_other = swap(normed_low)
    normed_other = advance("feed", normed_other)
    hidden, slope, keep, send, b_all, c_all = feed([bc_near, bc_far], normed_low, normed_other, bias_up, piece, block)
    branch = keep + swap(send).astype(F32)
    second = normed + branch + bdown_f
    hat_two, inv_two = normalize(second)
    layer_out = (hat_two * gtwo_f + stwo_f).astype(BF16)

    g_in = grad_out.astype(F32)
    d_gain_two = jnp.sum(g_in * hat_two, axis=0)
    d_shift_two = jnp.sum(g_in, axis=0)
    d_second = normalize_back(hat_two, inv_two, gtwo_f, g_in)
    d_branch = d_second.astype(BF16)
    d_bias_down = jnp.sum(d_branch.astype(F32), axis=0)
    db_other = swap(d_branch)

    sc = sb = sa = None
    order = ["P0", "P1", "P2", "P3", "P4", "P5", "P6", "P7"]
    sent = set()

    def go(name, *values):
        items = {}
        for k, s in (("c", sc), ("b", sb)):
            if s is not None:
                for n, f in (("1", "one"), ("2", "two"), ("3", "three")):
                    if hasattr(s, f):
                        items[k + n] = (s, f)
        res = stage(name, *values, **items)
        at = order.index(name)
        for k, s in (("c", sc), ("b", sb)):
            if s is None:
                continue
            for n, need, f in ((1, None, "first"), (2, "1", "second"), (3, "2", "third")):
                if k + str(n) in sent or (n > 1 and k + str(n - 1) not in sent):
                    continue
                if n == 1 or order.index(OPT.get(k + need, "P7")) <= at:
                    getattr(s, f)()
                    sent.add(k + str(n))
        return res

    keep, send, d_bias_up, *pairs = feed_back(
        d_branch, db_other, normed_low, normed_other, slope, hidden, c_all, b_all, piece
    )
    sc, sb = Scatter(pairs[:2]), Scatter(pairs[2:])
    go("P0")
    d_normed = d_second + keep + swap(send).astype(F32)
    d_normed = go("P1", d_normed)
    d_gain_one = jnp.sum(d_normed * hat_one, axis=0)
    d_shift_one = jnp.sum(d_normed, axis=0)
    d_first = normalize_back(hat_one, inv_one, gone_f, d_normed)
    d_attn = d_first.astype(BF16)
    d_bias_out = jnp.sum(d_attn.astype(F32), axis=0)
    da_other = swap(d_attn)
    d_ctx = dot_nn(d_attn, o_t).astype(BF16)
    sums = jnp.stack([d_bias_out, d_bias_down, d_gain_one, d_shift_one, d_gain_two, d_shift_two])
    sums = sums + swap(sums)
    d_ctx_other = dot_nn(da_other, o_t).astype(BF16)
    spread = jnp.concatenate([d_bias_up.reshape(nx, model), jnp.broadcast_to(sums.reshape(1, -1), (nx, 6 * model))], axis=1)
    spread = jnp.pad(spread.reshape(nx, 7, model), ((0, 0), (0, 1), (0, 0))).astype(BF16)
    d_ctx_other, spread = go("P2", d_ctx_other, spread)
    d_qkv, bias = attention_backward(qkv, ctx, lse, d_ctx, d_ctx_other, seg_col, seg_row, block)
    d_qkv = go("P3", d_qkv)
    attention_parts = [((0, 1), 2, part, 0, False), ((3, 4), 5, part, 3 * part, False)]
    given = [tokens, x_other, d_qkv, d_attn, da_other, ctx]
    sa = Scatter(summed(given, attention_parts, spread, bias))
    d_qkv, sa.send = go("P4", d_qkv, sa.send)
    sa.first()
    keep, send = input_gradient(d_qkv, d_first, w_all, block)
    sa.one, keep, send = go("P5", sa.one, keep, send)
    sa.second()
    input_grad = keep + swap(send).astype(F32)
    sa.two, input_grad = go("P6", sa.two, input_grad)
    sa.third()
    go("P7")
    input_grad = input_grad.astype(BF16)
    gc = sc.result()
    gb = sb.result()
    ga = sa.result()
    g_qkv = jnp.stack([ga[:piece, j * part : (j + 1) * part] for j in range(3)])
    tail = ga[piece:]
    g_bqv = lax.dynamic_slice_in_dim(tail[7, : 2 * part].reshape(2, part), place_dp * qv, qv, axis=1)
    g_bup = lax.dynamic_slice_in_dim(tail[0], place_dp * piece, piece)
    six = lax.dynamic_slice_in_dim(tail[1:7], ((place_dp * nx + which) * 2 + parity) * slim, slim, axis=1)
    return (
        layer_out,
        input_grad,
        g_qkv,
        g_bqv,
        ga[:piece, 3 * part :].T,
        gb,
        g_bup,
        gc.T,
        *[six[i] for i in range(6)],
    )


def solution(mesh):
    ndp, nt = mesh.devices.shape
    fine = Mesh(mesh.devices.reshape(ndp, nt // 2, 2), ("dp", "x", "c"))
    tensor = ("x", "c")
    every = ("dp", "x", "c")
    row = P(every, None)
    vec = P(every)
    return jax.shard_map(
        local,
        mesh=fine,
        in_specs=(
            row,
            row,
            P("dp", None),
            P(None, "dp", tensor),
            P(None, ("x", "c", "dp")),
            P(tensor, "dp"),
            P("dp", tensor),
            P(("x", "c", "dp")),
            P(tensor, "dp"),
            vec,
            vec,
            vec,
            vec,
            vec,
            vec,
        ),
        out_specs=(
            row,
            row,
            P(None, "dp", tensor),
            P(None, ("x", "c", "dp")),
            P(tensor, "dp"),
            P("dp", tensor),
            P(("x", "c", "dp")),
            P(tensor, "dp"),
            vec,
            vec,
            vec,
            vec,
            vec,
            vec,
        ),
        check_vma=False,
    )
```

profile of v0, /device:TPU:0, one launch (start us, length us, event | category | flops | bytes accessed | tf_op | source)
XLA Modules:
  0.0 269.5 jit_solution(8190719070654033727)
XLA Ops:
  2.5 2.1 prepare_units.1
  4.6 3.0 %collective-permute-start.1 = (bf16[104,768]{1,0:T(8,128)(2,1)}, bf16[104,768]{1,0:T(8,128)(2,1)S(1)}, u32[]{:S(2)}, u32[]{:S(2)}) collective-permute-start(bf16[104,768]{1,0:T(8,128)(2,1)} %get-tuple-element.72), channel_id=1, source_target_pairs={{0,8},{4,12},{8,0},{12,4},{16,24},{20,28},{24,16},{28,20},{1,9},{5... | collective-permute-start | bytes 479240 | tf_op jit(solution)/shard_map/ppermute | solution.py:234
  7.6 4.3 %collective-permute-done.1 = bf16[104,768]{1,0:T(8,128)(2,1)S(1)} collective-permute-done((bf16[104,768]{1,0:T(8,128)(2,1)}, bf16[104,768]{1,0:T(8,128)(2,1)S(1)}, u32[]{:S(2)}, u32[]{:S(2)}) %collective-permute-start.1) | collective-permute-done | bytes 159776 | tf_op jit(solution)/shard_map/ppermute | solution.py:234
  14.6 2.6 collective-permute-start.3
  17.2 2.7 %collective-permute-done.2.refs_1_ = bf16[2,104,768]{2,1,0:T(8,128)(2,1)S(1)} collective-permute-done((bf16[2,104,768]{2,1,0:T(8,128)(2,1)S(1)}, bf16[2,104,768]{2,1,0:T(8,128)(2,1)S(1)}, u32[]{:S(2)}, u32[]{:S(2)}) %collective-permute-start.2) | collective-permute-done | bytes 319520 | tf_op jit(solution)/shard_map/ppermute | solution.py:245
  24.4 6.2 %collective-permute-done.3.refs_3_ = bf16[2,104,768]{2,1,0:T(8,128)(2,1)S(1)} collective-permute-done((bf16[2,104,768]{2,1,0:T(8,128)(2,1)S(1)}, bf16[2,104,768]{2,1,0:T(8,128)(2,1)S(1)}, u32[]{:S(2)}, u32[]{:S(2)}) %collective-permute-start.3) | collective-permute-done | bytes 319520 | tf_op jit(solution)/shard_map/ppermute | solution.py:234
  32.1 3.1 %collective-permute-done.5 = bf16[2,96,768]{2,1,0:T(8,128)(2,1)S(1)} collective-permute-done((bf16[2,96,768]{2,1,0:T(8,128)(2,1)S(1)}, bf16[2,96,768]{2,1,0:T(8,128)(2,1)S(1)}, u32[]{:S(2)}, u32[]{:S(2)}) %collective-permute-start.5) | collective-permute-done | bytes 294944 | tf_op jit(solution)/shard_map/ppermute | solution.py:234
  35.3 2.3 collective-permute-done.4.refs_4_
  42.4 13.0 %collective-permute-done.7.refs_5_ = bf16[4,104,768]{2,1,0:T(8,128)(2,1)} collective-permute-done((bf16[4,104,768]{2,1,0:T(8,128)(2,1)}, bf16[4,104,768]{2,1,0:T(8,128)(2,1)}, u32[]{:S(2)}, u32[]{:S(2)}) %collective-permute-start.7) | collective-permute-done | bytes 639008 | tf_op jit(solution)/shard_map/ppermute | solution.py:245
  55.4 7.5 %project_kernel.1 = (bf16[1024,1152]{1,0:T(8,128)(2,1)}, bf16[768,1152]{1,0:T(8,128)(2,1)}, bf16[768,384]{1,0:T(8,128)(2,1)}, bf16[8,8,768]{2,1,0:T(8,128)(2,1)}) custom-call(s32[2]{0:T(128)} %pad_add_fusion.1.where_ref, bf16[512,768]{1,0:T(8,128)(2,1)} %refs_0_.1, bf16[512,768]{1,0:T(8,128)(2,1)} %copy-done.8, bf16[2,104,768]{2,1,0:T(8,128)(2,1)} %copy-done.21, ...), custom_call_target="tpu_custom_call" | custom-call | flops 1000 | bytes 1000 | tf_op jit(solution)/shard_map/project_kernel/pallas_call | solution.py:590
  62.9 3.9 %collective-permute-done.9.refs_3_ = bf16[2,2,96,768]{3,2,1,0:T(8,128)(2,1)S(1)} collective-permute-done((bf16[2,2,96,768]{3,2,1,0:T(8,128)(2,1)S(1)}, bf16[2,2,96,768]{3,2,1,0:T(8,128)(2,1)S(1)}, u32[]{:S(2)}, u32[]{:S(2)}) %collective-permute-start.9) | collective-permute-done | bytes 589856 | tf_op jit(solution)/shard_map/ppermute | solution.py:234
  70.7 12.9 %attention_forward.1 = (bf16[1024,384]{1,0:T(8,128)(2,1)}, f32[8,1024]{1,0:T(8,128)}) custom-call(s32[1024,1]{1,0:T(8,128)} %copy.33.seg_q_ref.seg_k_ref, s32[1,1024]{1,0:T(1,128)} %bitcast.93, bf16[1024,1152]{1,0:T(8,128)(2,1)} %get-tuple-element.78.q_ref.k_ref.v_ref, bf16[1024,1152]{1,0:T(8,128)(2,1)} %get-tuple-element.78.q_ref.k_ref.v_ref, ...), custom_call_target="tpu_custom_call" | custom-call | flops 1000 | bytes 1000 | tf_op jit(solution)/shard_map/attention_forward/pallas_call | solution.py:66
  85.3 2.6 collective-permute-done.10.refs_2_
  96.1 9.5 %collective-permute-done.13.refs_5_ = bf16[4,2,96,768]{3,2,1,0:T(8,128)(2,1)} collective-permute-done((bf16[4,2,96,768]{3,2,1,0:T(8,128)(2,1)}, bf16[4,2,96,768]{3,2,1,0:T(8,128)(2,1)}, u32[]{:S(2)}, u32[]{:S(2)}) %collective-permute-start.13) | collective-permute-done | bytes 1179680 | tf_op jit(solution)/shard_map/ppermute | solution.py:245
  109.8 13.7 %feed_kernel.1 = (bf16[1024,1536]{1,0:T(8,128)(2,1)}, bf16[1024,1536]{1,0:T(8,128)(2,1)}, f32[512,768]{1,0:T(8,128)}, bf16[512,768]{1,0:T(8,128)(2,1)}, bf16[768...) custom-call(s32[2]{0:T(128)} %pad_add_fusion.1.where_ref, bf16[512,768]{1,0:T(8,128)(2,1)} %copy-done.5, ...), custom_call_target="tpu_custom_call" | custom-call | flops 1000 | bytes 1000 | tf_op jit(solution)/shard_map/feed_kernel/pallas_call | solution.py:623
  123.8 2.2 collective-permute-done.16
  126.9 2.3 fusion.21
  132.7 2.1 collective-permute-done.17.refs_1_
  135.8 21.0 %feed_back.1 = (f32[512,768]{1,0:T(8,128)}, bf16[512,768]{1,0:T(8,128)(2,1)}, f32[1,1536]{1,0:T(1,128)}, bf16[8,96,768]{2,1,0:T(8,128)(2,1)}, bf16[8,96,768]{2,1...) custom-call(s32[2]{0:T(128)} %pad_add_fusion.1.where_ref, bf16[512,768]{1,0:T(8,128)(2,1)} %copy-done.9, ...), custom_call_target="tpu_custom_call" | custom-call | flops 1000 | bytes 1000 | tf_op jit(solution)/shard_map/feed_back/pallas_call | solution.py:531
  160.0 3.7 %multiply_reduce_fusion = (f32[768]{0:T(1024)S(1)}, f32[512]{0:T(512)S(1)}, f32[512]{0:T(512)S(1)}, f32[768]{0:T(1024)S(1)}, f32[512,768]{1,0:T(8,128)S(1)}, /*index=5*/bf16[512,768]{1,0:T(8,128)(2,1)}) fusion(f32[512,768]{1,0:T(8,128)S(1)} %get-tuple-element.181, f32[512]{0:T(512)S(1)} %add_rsqrt_fusion.1, f32[512]{0:T(512)S(1)} %broadcast_multiply_fusion.5, ...), kind=kLoop, calls=%fused_computation.11 | loop fusion | flops 9041408 | bytes 8682496 | tf_op jit(solution)/shard_map/reduce_sum | solution.py:972
  170.6 21.0 %attention_backward.1 = (bf16[1024,1152]{1,0:T(8,128)(2,1)}, f32[1,768]{1,0:T(1,128)}) custom-call(s32[1024,1]{1,0:T(8,128)} %copy.33.seg_q_ref.seg_k_ref, s32[1,1024]{1,0:T(1,128)} %bitcast.94, bf16[1024,1152]{1,0:T(8,128)(2,1)} %get-tuple-element.78.q_ref.k_ref.v_ref, bf16[1024,1152]{1,0:T(8,128)(2,1)} %get-tuple-element.78.q_ref.k_ref.v_ref, ...), custom_call_target="tpu_custom_call" | custom-call | flops 1000 | bytes 1000 | tf_op jit(solution)/shard_map/attention_backward/pallas_call | solution.py:162
  196.4 8.7 %sum_units.1 = (bf16[8,104,768]{2,1,0:T(8,128)(2,1)}, bf16[8,104,768]{2,1,0:T(8,128)(2,1)}) custom-call(s32[2]{0:T(128)} %pad_add_fusion.1.where_ref, bf16[512,768]{1,0:T(8,128)(2,1)} %refs_0_.1, bf16[512,768]{1,0:T(8,128)(2,1)} %copy-done.8, bf16[1024,1152]{1,0:T(8,128)(2,1)} %get-tuple-element.113.refs_2_.d_ref, bf16[512,768]{1,0:T(8,128)(2,1)} %copy-done.10, ...), custom_call_target="tpu_custom_call" | custom-call | flops 1000 | bytes 1000 | tf_op jit(solution)/shard_map/sum_units/pallas_call | solution.py:761
  205.1 4.3 %collective-permute-done.23 = bf16[4,96,768]{2,1,0:T(8,128)(2,1)} collective-permute-done((bf16[4,96,768]{2,1,0:T(8,128)(2,1)S(1)}, bf16[4,96,768]{2,1,0:T(8,128)(2,1)}, u32[]{:S(2)}, u32[]{:S(2)}) %collective-permute-start.23) | collective-permute-done | bytes 589856 | tf_op jit(solution)/shard_map/ppermute | solution.py:245
  213.4 4.7 %collective-permute-start.28 = (bf16[96,768]{1,0:T(8,128)(2,1)}, bf16[96,768]{1,0:T(8,128)(2,1)S(1)}, u32[]{:S(2)}, u32[]{:S(2)}) collective-permute-start(bf16[96,768]{1,0:T(8,128)(2,1)} %get-tuple-element.189), channel_id=1, source_target_pairs={{0,24},{4,28},{8,16},{12,20},{16,8},{20,12},{24,0},{28,4},{1,25},{... | collective-permute-start | bytes 442376 | tf_op jit(solution)/shard_map/ppermute | solution.py:234
  218.6 6.6 %input_gradient.1 = (f32[512,768]{1,0:T(8,128)}, bf16[512,768]{1,0:T(8,128)(2,1)}) custom-call(bf16[1024,1152]{1,0:T(8,128)(2,1)} %get-tuple-element.113.refs_2_.d_ref, f32[512,768]{1,0:T(8,128)} %get-tuple-element.176.first_ref, bf16[768,1152]{1,0:T(8,128)(2,1)} %get-tuple-element.114.w_ref), custom_call_target="tpu_custom_call" | custom-call | flops 1000 | bytes 1000 | tf_op jit(solution)/shard_map/input_gradient/pallas_call | solution.py:202
  225.2 4.3 %collective-permute-done.27 = bf16[96,768]{1,0:T(8,128)(2,1)S(1)} collective-permute-done((bf16[96,768]{1,0:T(8,128)(2,1)}, bf16[96,768]{1,0:T(8,128)(2,1)S(1)}, u32[]{:S(2)}, u32[]{:S(2)}) %collective-permute-start.27) | collective-permute-done | bytes 147488 | tf_op jit(solution)/shard_map/ppermute | solution.py:234
  231.8 3.3 %collective-permute-start.33 = (bf16[96,768]{1,0:T(8,128)(2,1)S(1)}, bf16[96,768]{1,0:T(8,128)(2,1)S(1)}, u32[]{:S(2)}, u32[]{:S(2)}) collective-permute-start(bf16[96,768]{1,0:T(8,128)(2,1)S(1)} %get-tuple-element.186), channel_id=1, source_target_pairs={{0,24},{4,28},{8,16},{12,20},{16,8},{20,12},{24,0},{28,4},{1,25},{... | collective-permute-start | bytes 442376 | tf_op jit(solution)/shard_map/ppermute | solution.py:234
  238.1 2.3 collective-permute-done.33
  240.4 7.5 %collective-permute-done.32 = bf16[96,768]{1,0:T(8,128)(2,1)S(1)} collective-permute-done((bf16[96,768]{1,0:T(8,128)(2,1)S(1)}, bf16[96,768]{1,0:T(8,128)(2,1)S(1)}, u32[]{:S(2)}, u32[]{:S(2)}) %collective-permute-start.32) | collective-permute-done | bytes 147488 | tf_op jit(solution)/shard_map/ppermute | solution.py:234
  249.6 2.2 collective-permute-start.35
  252.6 5.2 %collective-permute-done.34 = bf16[104,768]{1,0:T(8,128)(2,1)S(1)} collective-permute-done((bf16[104,768]{1,0:T(8,128)(2,1)S(1)}, bf16[104,768]{1,0:T(8,128)(2,1)S(1)}, u32[]{:S(2)}, u32[]{:S(2)}) %collective-permute-start.34) | collective-permute-done | bytes 159776 | tf_op jit(solution)/shard_map/ppermute | solution.py:234
  257.9 7.9 %collective-permute-done.35 = bf16[104,768]{1,0:T(8,128)(2,1)S(1)} collective-permute-done((bf16[104,768]{1,0:T(8,128)(2,1)S(1)}, bf16[104,768]{1,0:T(8,128)(2,1)S(1)}, u32[]{:S(2)}, u32[]{:S(2)}) %collective-permute-start.35) | collective-permute-done | bytes 159776 | tf_op jit(solution)/shard_map/ppermute | solution.py:234
  (206 shorter events, 69.5 us)
Async XLA Ops:
  4.6 7.3 %collective-permute-start.1 = (bf16[104,768]{1,0:T(8,128)(2,1)}, bf16[104,768]{1,0:T(8,128)(2,1)S(1)}, u32[]{:S(2)}, u32[]{:S(2)}) collective-permute-start(bf16[104,768]{1,0:T(8,128)(2,1)} %get-tuple-element.72), channel_id=1, source_target_pairs={{0,8},{4,12},{8,0},{12,4},{16,24},{20,28},{24,16},{28,20},{1,9},{5... | collective-permute-start | bytes 479240 | tf_op jit(solution)/shard_map/ppermute | solution.py:234
  12.9 7.1 %collective-permute-start.2 = (bf16[2,104,768]{2,1,0:T(8,128)(2,1)S(1)}, bf16[2,104,768]{2,1,0:T(8,128)(2,1)S(1)}, u32[]{:S(2)}, u32[]{:S(2)}) collective-permute-start(bf16[2,104,768]{2,1,0:T(8,128)(2,1)S(1)} %pad_maximum_fusion.5.refs_0_), channel_id=1, source_target_pairs={{0,2},{1,5},{2,0},{3,7},{4,6},{5,1},{6,4},{7,3},{8,10},{9,13},{10,... | collective-permute-start | bytes 958472 | tf_op jit(solution)/shard_map/ppermute | solution.py:245
  14.6 16.0 %collective-permute-start.3 = (bf16[2,104,768]{2,1,0:T(8,128)(2,1)S(1)}, bf16[2,104,768]{2,1,0:T(8,128)(2,1)S(1)}, u32[]{:S(2)}, u32[]{:S(2)}) collective-permute-start(bf16[2,104,768]{2,1,0:T(8,128)(2,1)S(1)} %pad_maximum_fusion.5.refs_0_), channel_id=1, source_target_pairs={{0,16},{4,20},{8,24},{12,28},{16,0},{20,4},{24,8},{28,12},{1,17},{... | collective-permute-start | bytes 958472 | tf_op jit(solution)/shard_map/ppermute | solution.py:234
  21.1 16.6 %collective-permute-start.6 = (bf16[4,104,768]{2,1,0:T(8,128)(2,1)S(1)}, bf16[4,104,768]{2,1,0:T(8,128)(2,1)S(1)}, u32[]{:S(2)}, u32[]{:S(2)}) collective-permute-start(bf16[4,104,768]{2,1,0:T(8,128)(2,1)S(1)} %pad_maximum_fusion.2), channel_id=1, source_target_pairs={{0,4},{1,3},{2,6},{3,1},{4,0},{5,7},{6,2},{7,5},{8,12},{9,11},{10,... | collective-permute-start | bytes 1916936 | tf_op jit(solution)/shard_map/ppermute | solution.py:245
  22.8 12.4 %collective-permute-start.5 = (bf16[2,96,768]{2,1,0:T(8,128)(2,1)S(1)}, bf16[2,96,768]{2,1,0:T(8,128)(2,1)S(1)}, u32[]{:S(2)}, u32[]{:S(2)}) collective-permute-start(bf16[2,96,768]{2,1,0:T(8,128)(2,1)S(1)} %copy-done.30), channel_id=1, source_target_pairs={{0,8},{4,12},{8,0},{12,4},{16,24},{20,28},{24,16},{28,20},{1,9},{5... | collective-permute-start | bytes 884744 | tf_op jit(solution)/shard_map/ppermute | solution.py:234
  30.6 7.0 %collective-permute-start.4 = (bf16[2,104,768]{2,1,0:T(8,128)(2,1)S(1)}, bf16[2,104,768]{2,1,0:T(8,128)(2,1)S(1)}, u32[]{:S(2)}, u32[]{:S(2)}) collective-permute-start(bf16[2,104,768]{2,1,0:T(8,128)(2,1)S(1)} %collective-permute-done.3.refs_3_), channel_id=1, source_target_pairs={{0,2},{1,5},{2,0},{3,7},{4,6},{5,1},{6,4},{7,3},{8,10},{9,13},{10,... | collective-permute-start | bytes 958472 | tf_op jit(solution)/shard_map/ppermute | solution.py:245
  32.1 10.2 %collective-permute-start = (bf16[512,768]{1,0:T(8,128)(2,1)S(1)}, bf16[512,768]{1,0:T(8,128)(2,1)S(1)}, u32[]{:S(2)}, u32[]{:S(2)}) collective-permute-start(bf16[512,768]{1,0:T(8,128)(2,1)S(1)} %copy-done.3), channel_id=1, source_target_pairs={{0,1},{1,0},{2,3},{3,2},{4,5},{5,4},{6,7},{7,6},{8,9},{9,8},{10,11... | collective-permute-start | bytes 2359304 | tf_op jit(solution)/shard_map/ppermute | solution.py:229
  38.6 16.8 %collective-permute-start.7 = (bf16[4,104,768]{2,1,0:T(8,128)(2,1)}, bf16[4,104,768]{2,1,0:T(8,128)(2,1)}, u32[]{:S(2)}, u32[]{:S(2)}) collective-permute-start(bf16[4,104,768]{2,1,0:T(8,128)(2,1)} %pad_maximum_fusion.3), channel_id=1, source_target_pairs={{0,4},{1,3},{2,6},{3,1},{4,0},{5,7},{6,2},{7,5},{8,12},{9,11},{10,... | collective-permute-start | bytes 1916936 | tf_op jit(solution)/shard_map/ppermute | solution.py:245
  39.4 27.4 %collective-permute-start.9 = (bf16[2,2,96,768]{3,2,1,0:T(8,128)(2,1)S(1)}, bf16[2,2,96,768]{3,2,1,0:T(8,128)(2,1)S(1)}, u32[]{:S(2)}, u32[]{:S(2)}) collective-permute-start(bf16[2,2,96,768]{3,2,1,0:T(8,128)(2,1)S(1)} %pad_maximum_fusion.4.refs_0_), channel_id=1, source_target_pairs={{0,16},{4,20},{8,24},{12,28},{16,0},{20,4},{24,8},{28,12},{1,17},{... | collective-permute-start | bytes 1769480 | tf_op jit(solution)/shard_map/ppermute | solution.py:234
  40.2 26.5 %collective-permute-start.8 = (bf16[2,2,96,768]{3,2,1,0:T(8,128)(2,1)S(1)}, bf16[2,2,96,768]{3,2,1,0:T(8,128)(2,1)S(1)}, u32[]{:S(2)}, u32[]{:S(2)}) collective-permute-start(bf16[2,2,96,768]{3,2,1,0:T(8,128)(2,1)S(1)} %pad_maximum_fusion.4.refs_0_), channel_id=1, source_target_pairs={{0,2},{1,5},{2,0},{3,7},{4,6},{5,1},{6,4},{7,3},{8,10},{9,13},{10,... | collective-permute-start | bytes 1769480 | tf_op jit(solution)/shard_map/ppermute | solution.py:245
  68.0 19.9 %collective-permute-start.10 = (bf16[4,2,96,768]{3,2,1,0:T(8,128)(2,1)}, bf16[4,2,96,768]{3,2,1,0:T(8,128)(2,1)}, u32[]{:S(2)}, u32[]{:S(2)}) collective-permute-start(bf16[4,2,96,768]{3,2,1,0:T(8,128)(2,1)} %pad_maximum_fusion), channel_id=1, source_target_pairs={{0,4},{1,3},{2,6},{3,1},{4,0},{5,7},{6,2},{7,5},{8,12},{9,11},{10,... | collective-permute-start | bytes 3538952 | tf_op jit(solution)/shard_map/ppermute | solution.py:245
  69.1 16.3 %collective-permute-start.11 = (bf16[2,2,96,768]{3,2,1,0:T(8,128)(2,1)S(1)}, bf16[2,2,96,768]{3,2,1,0:T(8,128)(2,1)S(1)}, u32[]{:S(2)}, u32[]{:S(2)}) collective-permute-start(bf16[2,2,96,768]{3,2,1,0:T(8,128)(2,1)S(1)} %collective-permute-done.9.refs_3_), channel_id=1, source_target_pairs={{0,2},{1,5},{2,0},{3,7},{4,6},{5,1},{6,4},{7,3},{8,10},{9,13},{10,... | collective-permute-start | bytes 1769480 | tf_op jit(solution)/shard_map/ppermute | solution.py:245
  89.0 16.5 %collective-permute-start.13 = (bf16[4,2,96,768]{3,2,1,0:T(8,128)(2,1)}, bf16[4,2,96,768]{3,2,1,0:T(8,128)(2,1)}, u32[]{:S(2)}, u32[]{:S(2)}) collective-permute-start(bf16[4,2,96,768]{3,2,1,0:T(8,128)(2,1)} %pad_maximum_fusion.1), channel_id=1, source_target_pairs={{0,4},{1,3},{2,6},{3,1},{4,0},{5,7},{6,2},{7,5},{8,12},{9,11},{10,... | collective-permute-start | bytes 3538952 | tf_op jit(solution)/shard_map/ppermute | solution.py:245
  91.1 3.2 %collective-permute-start.12 = (bf16[512,768]{1,0:T(8,128)(2,1)S(1)}, bf16[512,768]{1,0:T(8,128)(2,1)}, u32[]{:S(2)}, u32[]{:S(2)}) collective-permute-start(bf16[512,768]{1,0:T(8,128)(2,1)S(1)} %convolution_convert_fusion), channel_id=1, source_target_pairs={{0,1},{1,0},{2,3},{3,2},{4,5},{5,4},{6,7},{7,6},{8,9},{9,8},{10,11... | collective-permute-start | bytes 2359304 | tf_op jit(solution)/shard_map/ppermute | solution.py:229
  123.4 2.6 collective-permute-start.16
  156.8 3.2 %collective-permute-start.18 = (bf16[512,768]{1,0:T(8,128)(2,1)}, bf16[512,768]{1,0:T(8,128)(2,1)}, u32[]{:S(2)}, u32[]{:S(2)}) collective-permute-start(bf16[512,768]{1,0:T(8,128)(2,1)} %get-tuple-element.97), channel_id=1, source_target_pairs={{0,1},{1,0},{2,3},{3,2},{4,5},{5,4},{6,7},{7,6},{8,9},{9,8},{10,11... | collective-permute-start | bytes 2359304 | tf_op jit(solution)/shard_map/ppermute | solution.py:229
  157.9 33.8 %collective-permute-start.21 = (bf16[8,96,768]{2,1,0:T(8,128)(2,1)}, bf16[8,96,768]{2,1,0:T(8,128)(2,1)}, u32[]{:S(2)}, u32[]{:S(2)}) collective-permute-start(bf16[8,96,768]{2,1,0:T(8,128)(2,1)} %get-tuple-element.101), channel_id=1, source_target_pairs={{0,2},{1,5},{2,0},{3,7},{4,6},{5,1},{6,4},{7,3},{8,10},{9,13},{10,... | collective-permute-start | bytes 3538952 | tf_op jit(solution)/shard_map/ppermute | solution.py:245
  159.5 32.1 %collective-permute-start.22 = (bf16[8,96,768]{2,1,0:T(8,128)(2,1)}, bf16[8,96,768]{2,1,0:T(8,128)(2,1)}, u32[]{:S(2)}, u32[]{:S(2)}) collective-permute-start(bf16[8,96,768]{2,1,0:T(8,128)(2,1)} %get-tuple-element.102), channel_id=1, source_target_pairs={{0,2},{1,5},{2,0},{3,7},{4,6},{5,1},{6,4},{7,3},{8,10},{9,13},{10,... | collective-permute-start | bytes 3538952 | tf_op jit(solution)/shard_map/ppermute | solution.py:245
  193.0 12.1 %collective-permute-start.24 = (bf16[4,96,768]{2,1,0:T(8,128)(2,1)S(1)}, bf16[4,96,768]{2,1,0:T(8,128)(2,1)S(1)}, u32[]{:S(2)}, u32[]{:S(2)}) collective-permute-start(bf16[4,96,768]{2,1,0:T(8,128)(2,1)S(1)} %add_convert_fusion.8), channel_id=1, source_target_pairs={{0,4},{1,3},{2,6},{3,1},{4,0},{5,7},{6,2},{7,5},{8,12},{9,11},{10,... | collective-permute-start | bytes 1769480 | tf_op jit(solution)/shard_map/ppermute | solution.py:245
  195.8 13.6 %collective-permute-start.23 = (bf16[4,96,768]{2,1,0:T(8,128)(2,1)S(1)}, bf16[4,96,768]{2,1,0:T(8,128)(2,1)}, u32[]{:S(2)}, u32[]{:S(2)}) collective-permute-start(bf16[4,96,768]{2,1,0:T(8,128)(2,1)S(1)} %add_convert_fusion.9), channel_id=1, source_target_pairs={{0,4},{1,3},{2,6},{3,1},{4,0},{5,7},{6,2},{7,5},{8,12},{9,11},{10,... | collective-permute-start | bytes 1769480 | tf_op jit(solution)/shard_map/ppermute | solution.py:245
  209.4 20.2 %collective-permute-start.25 = (bf16[8,104,768]{2,1,0:T(8,128)(2,1)}, bf16[8,104,768]{2,1,0:T(8,128)(2,1)S(1)}, u32[]{:S(2)}, u32[]{:S(2)}) collective-permute-start(bf16[8,104,768]{2,1,0:T(8,128)(2,1)} %get-tuple-element.112), channel_id=1, source_target_pairs={{0,2},{1,5},{2,0},{3,7},{4,6},{5,1},{6,4},{7,3},{8,10},{9,13},{10,... | collective-permute-start | bytes 3833864 | tf_op jit(solution)/shard_map/ppermute | solution.py:245
  213.4 11.9 %collective-permute-start.28 = (bf16[96,768]{1,0:T(8,128)(2,1)}, bf16[96,768]{1,0:T(8,128)(2,1)S(1)}, u32[]{:S(2)}, u32[]{:S(2)}) collective-permute-start(bf16[96,768]{1,0:T(8,128)(2,1)} %get-tuple-element.189), channel_id=1, source_target_pairs={{0,24},{4,28},{8,16},{12,20},{16,8},{20,12},{24,0},{28,4},{1,25},{... | collective-permute-start | bytes 442376 | tf_op jit(solution)/shard_map/ppermute | solution.py:234
  218.1 11.5 %collective-permute-start.27 = (bf16[96,768]{1,0:T(8,128)(2,1)}, bf16[96,768]{1,0:T(8,128)(2,1)S(1)}, u32[]{:S(2)}, u32[]{:S(2)}) collective-permute-start(bf16[96,768]{1,0:T(8,128)(2,1)} %get-tuple-element.190), channel_id=1, source_target_pairs={{0,16},{4,20},{8,24},{12,28},{16,0},{20,4},{24,8},{28,12},{1,17},{... | collective-permute-start | bytes 442376 | tf_op jit(solution)/shard_map/ppermute | solution.py:234
  218.1 11.5 %collective-permute-start.26 = (bf16[96,768]{1,0:T(8,128)(2,1)}, bf16[96,768]{1,0:T(8,128)(2,1)S(1)}, u32[]{:S(2)}, u32[]{:S(2)}) collective-permute-start(bf16[96,768]{1,0:T(8,128)(2,1)} %get-tuple-element.191), channel_id=1, source_target_pairs={{0,8},{4,12},{8,0},{12,4},{16,24},{20,28},{24,16},{28,20},{1,9},{5... | collective-permute-start | bytes 442376 | tf_op jit(solution)/shard_map/ppermute | solution.py:234
  229.5 7.5 %collective-permute-start.30 = (bf16[512,768]{1,0:T(8,128)(2,1)}, bf16[512,768]{1,0:T(8,128)(2,1)S(1)}, u32[]{:S(2)}, u32[]{:S(2)}) collective-permute-start(bf16[512,768]{1,0:T(8,128)(2,1)} %get-tuple-element.120), channel_id=1, source_target_pairs={{0,1},{1,0},{2,3},{3,2},{4,5},{5,4},{6,7},{7,6},{8,9},{9,8},{10,11... | collective-permute-start | bytes 2359304 | tf_op jit(solution)/shard_map/ppermute | solution.py:229
  231.3 16.7 %collective-permute-start.29 = (bf16[4,104,768]{2,1,0:T(8,128)(2,1)S(1)}, bf16[4,104,768]{2,1,0:T(8,128)(2,1)S(1)}, u32[]{:S(2)}, u32[]{:S(2)}) collective-permute-start(bf16[4,104,768]{2,1,0:T(8,128)(2,1)S(1)} %add_convert_fusion.3), channel_id=1, source_target_pairs={{0,4},{1,3},{2,6},{3,1},{4,0},{5,7},{6,2},{7,5},{8,12},{9,11},{10,... | collective-permute-start | bytes 1916936 | tf_op jit(solution)/shard_map/ppermute | solution.py:245
  231.8 8.6 %collective-permute-start.33 = (bf16[96,768]{1,0:T(8,128)(2,1)S(1)}, bf16[96,768]{1,0:T(8,128)(2,1)S(1)}, u32[]{:S(2)}, u32[]{:S(2)}) collective-permute-start(bf16[96,768]{1,0:T(8,128)(2,1)S(1)} %get-tuple-element.186), channel_id=1, source_target_pairs={{0,24},{4,28},{8,16},{12,20},{16,8},{20,12},{24,0},{28,4},{1,25},{... | collective-permute-start | bytes 442376 | tf_op jit(solution)/shard_map/ppermute | solution.py:234
  235.2 12.7 %collective-permute-start.32 = (bf16[96,768]{1,0:T(8,128)(2,1)S(1)}, bf16[96,768]{1,0:T(8,128)(2,1)S(1)}, u32[]{:S(2)}, u32[]{:S(2)}) collective-permute-start(bf16[96,768]{1,0:T(8,128)(2,1)S(1)} %get-tuple-element.187), channel_id=1, source_target_pairs={{0,16},{4,20},{8,24},{12,28},{16,0},{20,4},{24,8},{28,12},{1,17},{... | collective-permute-start | bytes 442376 | tf_op jit(solution)/shard_map/ppermute | solution.py:234
  235.2 12.7 %collective-permute-start.31 = (bf16[96,768]{1,0:T(8,128)(2,1)S(1)}, bf16[96,768]{1,0:T(8,128)(2,1)S(1)}, u32[]{:S(2)}, u32[]{:S(2)}) collective-permute-start(bf16[96,768]{1,0:T(8,128)(2,1)S(1)} %get-tuple-element.188), channel_id=1, source_target_pairs={{0,8},{4,12},{8,0},{12,4},{16,24},{20,28},{24,16},{28,20},{1,9},{5... | collective-permute-start | bytes 442376 | tf_op jit(solution)/shard_map/ppermute | solution.py:234
  248.2 9.5 %collective-permute-start.34 = (bf16[104,768]{1,0:T(8,128)(2,1)S(1)}, bf16[104,768]{1,0:T(8,128)(2,1)S(1)}, u32[]{:S(2)}, u32[]{:S(2)}) collective-permute-start(bf16[104,768]{1,0:T(8,128)(2,1)S(1)} %get-tuple-element.183), channel_id=1, source_target_pairs={{0,8},{4,12},{8,0},{12,4},{16,24},{20,28},{24,16},{28,20},{1,9},{5... | collective-permute-start | bytes 479240 | tf_op jit(solution)/shard_map/ppermute | solution.py:234
  248.3 9.6 %collective-permute-start.36 = (bf16[104,768]{1,0:T(8,128)(2,1)S(1)}, bf16[104,768]{1,0:T(8,128)(2,1)S(1)}, u32[]{:S(2)}, u32[]{:S(2)}) collective-permute-start(bf16[104,768]{1,0:T(8,128)(2,1)S(1)} %get-tuple-element.184), channel_id=1, source_target_pairs={{0,24},{4,28},{8,16},{12,20},{16,8},{20,12},{24,0},{28,4},{1,25},{... | collective-permute-start | bytes 479240 | tf_op jit(solution)/shard_map/ppermute | solution.py:234
  249.6 16.3 %collective-permute-start.35 = (bf16[104,768]{1,0:T(8,128)(2,1)S(1)}, bf16[104,768]{1,0:T(8,128)(2,1)S(1)}, u32[]{:S(2)}, u32[]{:S(2)}) collective-permute-start(bf16[104,768]{1,0:T(8,128)(2,1)S(1)} %get-tuple-element.185), channel_id=1, source_target_pairs={{0,16},{4,20},{8,24},{12,28},{16,0},{20,4},{24,8},{28,12},{1,17},{... | collective-permute-start | bytes 479240 | tf_op jit(solution)/shard_map/ppermute | solution.py:234
  (38 other events, 408.7 us)
where the time goes:
time: 270 us; the launch traced here: 269 us
  Pallas kernels  93.5 us (35%)
  waiting for transfers between devices  89.7 us (33%)
  starting transfers between devices  39.8 us (15%)
  other arithmetic  26.8 us (10%)
  local copies, waits for them, and re-layouts  13.5 us (5%)
  matrix products  5.08 us (2%)
    ppermute x13, waiting for transfers between devices, flip(): return lax.ppermute(a, axis, [(i, i ^ bit) for i in range(n)])  45 us
    ppermute x14, waiting for transfers between devices, turn(): return lax.ppermute(a, ('dp', 'x', 'c'), pairs)  36.1 us
    ppermute x13, starting transfers between devices, flip(): return lax.ppermute(a, axis, [(i, i ^ bit) for i in range(n)])  21.3 us
    pallas_call x1, Pallas kernels, attention_backward(): pl.pallas_call(functools.partial(attention_backward_kernel, width, halves...  21 us
    pallas_call x1, Pallas kernels, feed_back(): pl.pallas_call(functools.partial(feed_back_kernel, 256, piece), grid_spec...  21 us
    ppermute x14, starting transfers between devices, turn(): return lax.ppermute(a, ('dp', 'x', 'c'), pairs)  16.7 us
    pallas_call x1, Pallas kernels, feed(): pl.pallas_call(functools.partial(feed_kernel, index, moves, halves), grid...  13.7 us
    pallas_call x1, Pallas kernels, attention_forward(): pl.pallas_call(functools.partial(attention_forward_kernel, width), grid=(...  12.9 us
  transfers between devices with their start and end apart: 37, of which 22 were waited for; matrix products, arithmetic and copies ran while one was open for 9% of the time, Pallas kernels for 21%

commit v1 on v0

--- a/solution.py
+++ b/solution.py
@@ -265,7 +265,7 @@
     return jnp.concatenate(parts[1:]) if len(parts) > 2 else parts[1]
 
 
-OPT = {'bc': None, 'bn1': 'qkv', 'bz2': 'qkv', 'bf1': 'ctx', 'bn2': 'ctx', 'bf2': 'attn', 'c1': 'P3', 'c2': 'P4', 'b1': 'P3', 'b2': 'P4', 'c3': 'P5', 'b3': 'P6', 'an2': 'f1', 'bz1': 'f1'}
+OPT = {'bc': None, 'bn1': 'f2', 'bz2': 'qkv', 'bf1': 'ctx', 'bn2': 'ctx', 'bf2': 'attn', 'c1': 'P3', 'c2': 'P4', 'c3': 'P5', 'b1': 'P3', 'b2': 'P5', 'b3': 'P6', 'an2': 'f1', 'bz1': 'f1'}
 
 
 def stage(name, *values, **items):

time: 270 us -> 263 us (0.974)
  waiting for transfers between devices: 89.7 us -> 80.6 us
    ppermute x13, waiting for transfers between devices: 45 us -> 39.4 us  [flip(): return lax.ppermute(a, axis, [(i, i ^ bit) for i in range(n)])]
    ppermute x14, waiting for transfers between devices: 36.1 us -> 32.6 us  [turn(): return lax.ppermute(a, ('dp', 'x', 'c'), pairs)]
    unnamed x69 -> x75, local copies, waits for them, and re-layouts: 7.09 us -> 8.69 us
  transfers between devices with their start and end apart: 37 -> 37, of which waited for: 22 -> 21; matrix products, arithmetic and copies ran while one was open for 9% -> 10% of each run, Pallas kernels for 21% -> 22%
where the time goes in v1:
time: 263 us
  Pallas kernels  93.7 us (36%)
  waiting for transfers between devices  80.6 us (31%)
  starting transfers between devices  39.8 us (15%)
  other arithmetic  27.2 us (10%)
  local copies, waits for them, and re-layouts  15.1 us (6%)
  matrix products  5.07 us (2%)
    ppermute x13, waiting for transfers between devices, flip(): return lax.ppermute(a, axis, [(i, i ^ bit) for i in range(n)])  39.4 us
    ppermute x14, waiting for transfers between devices, turn(): return lax.ppermute(a, ('dp', 'x', 'c'), pairs)  32.6 us
    pallas_call x1, Pallas kernels, attention_backward(): pl.pallas_call(functools.partial(attention_backward_kernel, width, halves...  21 us
    pallas_call x1, Pallas kernels, feed_back(): pl.pallas_call(functools.partial(feed_back_kernel, 256, piece), grid_spec...  21 us
    ppermute x13, starting transfers between devices, flip(): return lax.ppermute(a, axis, [(i, i ^ bit) for i in range(n)])  20.7 us
    ppermute x14, starting transfers between devices, turn(): return lax.ppermute(a, ('dp', 'x', 'c'), pairs)  17.3 us
    pallas_call x1, Pallas kernels, feed(): pl.pallas_call(functools.partial(feed_kernel, index, moves, halves), grid...  13.7 us
    pallas_call x1, Pallas kernels, attention_forward(): pl.pallas_call(functools.partial(attention_forward_kernel, width), grid=(...  12.9 us
  transfers between devices with their start and end apart: 37, of which 21 were waited for; matrix products, arithmetic and copies ran while one was open for 10% of the time, Pallas kernels for 22%

profile of v1, /device:TPU:0, one launch (start us, length us, event | category | flops | bytes accessed | tf_op | source)
XLA Modules:
  0.0 262.7 jit_solution(12718440643072976646)
XLA Ops:
  2.4 2.1 prepare_units.1
  4.5 3.0 %collective-permute-start.1 = (bf16[104,768]{1,0:T(8,128)(2,1)}, bf16[104,768]{1,0:T(8,128)(2,1)S(1)}, u32[]{:S(2)}, u32[]{:S(2)}) collective-permute-start(bf16[104,768]{1,0:T(8,128)(2,1)} %get-tuple-element.73), channel_id=1, source_target_pairs={{0,8},{4,12},{8,0},{12,4},{16,24},{20,28},{24,16},{28,20},{1,9},{5... | collective-permute-start | bytes 479240 | tf_op jit(solution)/shard_map/ppermute | solution.py:234
  7.6 4.3 %collective-permute-done.1 = bf16[104,768]{1,0:T(8,128)(2,1)S(1)} collective-permute-done((bf16[104,768]{1,0:T(8,128)(2,1)}, bf16[104,768]{1,0:T(8,128)(2,1)S(1)}, u32[]{:S(2)}, u32[]{:S(2)}) %collective-permute-start.1) | collective-permute-done | bytes 159776 | tf_op jit(solution)/shard_map/ppermute | solution.py:234
  14.6 2.6 collective-permute-start.3
  17.2 2.7 %collective-permute-done.2.refs_1_ = bf16[2,104,768]{2,1,0:T(8,128)(2,1)S(1)} collective-permute-done((bf16[2,104,768]{2,1,0:T(8,128)(2,1)S(1)}, bf16[2,104,768]{2,1,0:T(8,128)(2,1)S(1)}, u32[]{:S(2)}, u32[]{:S(2)}) %collective-permute-start.2) | collective-permute-done | bytes 319520 | tf_op jit(solution)/shard_map/ppermute | solution.py:245
  24.3 6.2 %collective-permute-done.3.refs_3_ = bf16[2,104,768]{2,1,0:T(8,128)(2,1)S(1)} collective-permute-done((bf16[2,104,768]{2,1,0:T(8,128)(2,1)S(1)}, bf16[2,104,768]{2,1,0:T(8,128)(2,1)S(1)}, u32[]{:S(2)}, u32[]{:S(2)}) %collective-permute-start.3) | collective-permute-done | bytes 319520 | tf_op jit(solution)/shard_map/ppermute | solution.py:234
  32.1 3.1 %collective-permute-done.5 = bf16[2,96,768]{2,1,0:T(8,128)(2,1)S(1)} collective-permute-done((bf16[2,96,768]{2,1,0:T(8,128)(2,1)S(1)}, bf16[2,96,768]{2,1,0:T(8,128)(2,1)S(1)}, u32[]{:S(2)}, u32[]{:S(2)}) %collective-permute-start.5) | collective-permute-done | bytes 294944 | tf_op jit(solution)/shard_map/ppermute | solution.py:234
  35.3 2.3 collective-permute-done.4.refs_4_
  40.8 10.7 %collective-permute-done.8.refs_1_ = bf16[2,2,96,768]{3,2,1,0:T(8,128)(2,1)S(1)} collective-permute-done((bf16[2,2,96,768]{3,2,1,0:T(8,128)(2,1)S(1)}, bf16[2,2,96,768]{3,2,1,0:T(8,128)(2,1)S(1)}, u32[]{:S(2)}, u32[]{:S(2)}) %collective-permute-start.8) | collective-permute-done | bytes 589856 | tf_op jit(solution)/shard_map/ppermute | solution.py:245
  56.5 7.5 %project_kernel.1 = (bf16[1024,1152]{1,0:T(8,128)(2,1)}, bf16[768,1152]{1,0:T(8,128)(2,1)}, bf16[768,384]{1,0:T(8,128)(2,1)}, bf16[8,8,768]{2,1,0:T(8,128)(2,1)}) custom-call(s32[2]{0:T(128)} %pad_add_fusion.1.where_ref, bf16[512,768]{1,0:T(8,128)(2,1)} %refs_0_.1, bf16[512,768]{1,0:T(8,128)(2,1)} %copy-done.8, bf16[2,104,768]{2,1,0:T(8,128)(2,1)} %copy-done.21, ...), custom_call_target="tpu_custom_call" | custom-call | flops 1000 | bytes 1000 | tf_op jit(solution)/shard_map/project_kernel/pallas_call | solution.py:590
  64.0 5.0 %collective-permute-done.9.refs_3_ = bf16[2,2,96,768]{3,2,1,0:T(8,128)(2,1)S(1)} collective-permute-done((bf16[2,2,96,768]{3,2,1,0:T(8,128)(2,1)S(1)}, bf16[2,2,96,768]{3,2,1,0:T(8,128)(2,1)S(1)}, u32[]{:S(2)}, u32[]{:S(2)}) %collective-permute-start.9) | collective-permute-done | bytes 589856 | tf_op jit(solution)/shard_map/ppermute | solution.py:234
  70.8 12.9 %attention_forward.1 = (bf16[1024,384]{1,0:T(8,128)(2,1)}, f32[8,1024]{1,0:T(8,128)}) custom-call(s32[1024,1]{1,0:T(8,128)} %copy.33.seg_q_ref.seg_k_ref, s32[1,1024]{1,0:T(1,128)} %bitcast.93, bf16[1024,1152]{1,0:T(8,128)(2,1)} %get-tuple-element.80.q_ref.k_ref.v_ref, bf16[1024,1152]{1,0:T(8,128)(2,1)} %get-tuple-element.80.q_ref.k_ref.v_ref, ...), custom_call_target="tpu_custom_call" | custom-call | flops 1000 | bytes 1000 | tf_op jit(solution)/shard_map/attention_forward/pallas_call | solution.py:66
  91.9 9.6 %collective-permute-done.13.refs_5_ = bf16[4,2,96,768]{3,2,1,0:T(8,128)(2,1)} collective-permute-done((bf16[4,2,96,768]{3,2,1,0:T(8,128)(2,1)}, bf16[4,2,96,768]{3,2,1,0:T(8,128)(2,1)}, u32[]{:S(2)}, u32[]{:S(2)}) %collective-permute-start.13) | collective-permute-done | bytes 1179680 | tf_op jit(solution)/shard_map/ppermute | solution.py:245
  105.6 13.7 %feed_kernel.1 = (bf16[1024,1536]{1,0:T(8,128)(2,1)}, bf16[1024,1536]{1,0:T(8,128)(2,1)}, f32[512,768]{1,0:T(8,128)}, bf16[512,768]{1,0:T(8,128)(2,1)}, bf16[768...) custom-call(s32[2]{0:T(128)} %pad_add_fusion.1.where_ref, bf16[512,768]{1,0:T(8,128)(2,1)} %copy-done.5, ...), custom_call_target="tpu_custom_call" | custom-call | flops 1000 | bytes 1000 | tf_op jit(solution)/shard_map/feed_kernel/pallas_call | solution.py:623
  119.7 2.2 collective-permute-done.16
  122.8 2.3 fusion.21
  128.6 2.1 collective-permute-done.17.refs_1_
  131.6 21.0 %feed_back.1 = (f32[512,768]{1,0:T(8,128)}, bf16[512,768]{1,0:T(8,128)(2,1)}, f32[1,1536]{1,0:T(1,128)}, bf16[8,96,768]{2,1,0:T(8,128)(2,1)}, bf16[8,96,768]{2,1...) custom-call(s32[2]{0:T(128)} %pad_add_fusion.1.where_ref, bf16[512,768]{1,0:T(8,128)(2,1)} %copy-done.9, ...), custom_call_target="tpu_custom_call" | custom-call | flops 1000 | bytes 1000 | tf_op jit(solution)/shard_map/feed_back/pallas_call | solution.py:531
  155.8 3.7 %multiply_reduce_fusion = (f32[768]{0:T(1024)S(1)}, f32[512]{0:T(512)S(1)}, f32[512]{0:T(512)S(1)}, f32[768]{0:T(1024)S(1)}, f32[512,768]{1,0:T(8,128)S(1)}, /*index=5*/bf16[512,768]{1,0:T(8,128)(2,1)}) fusion(f32[512,768]{1,0:T(8,128)S(1)} %get-tuple-element.183, f32[512]{0:T(512)S(1)} %add_rsqrt_fusion.1, f32[512]{0:T(512)S(1)} %broadcast_multiply_fusion.5, ...), kind=kLoop, calls=%fused_computation.11 | loop fusion | flops 9041408 | bytes 8682496 | tf_op jit(solution)/shard_map/reduce_sum | solution.py:972
  166.4 21.0 %attention_backward.1 = (bf16[1024,1152]{1,0:T(8,128)(2,1)}, f32[1,768]{1,0:T(1,128)}) custom-call(s32[1024,1]{1,0:T(8,128)} %copy.33.seg_q_ref.seg_k_ref, s32[1,1024]{1,0:T(1,128)} %bitcast.94, bf16[1024,1152]{1,0:T(8,128)(2,1)} %get-tuple-element.80.q_ref.k_ref.v_ref, bf16[1024,1152]{1,0:T(8,128)(2,1)} %get-tuple-element.80.q_ref.k_ref.v_ref, ...), custom_call_target="tpu_custom_call" | custom-call | flops 1000 | bytes 1000 | tf_op jit(solution)/shard_map/attention_backward/pallas_call | solution.py:162
  190.2 8.8 %sum_units.1 = (bf16[8,104,768]{2,1,0:T(8,128)(2,1)}, bf16[8,104,768]{2,1,0:T(8,128)(2,1)}) custom-call(s32[2]{0:T(128)} %pad_add_fusion.1.where_ref, bf16[512,768]{1,0:T(8,128)(2,1)} %refs_0_.1, bf16[512,768]{1,0:T(8,128)(2,1)} %copy-done.8, bf16[1024,1152]{1,0:T(8,128)(2,1)} %get-tuple-element.113.refs_2_.d_ref, bf16[512,768]{1,0:T(8,128)(2,1)} %copy-done.10, ...), custom_call_target="tpu_custom_call" | custom-call | flops 1000 | bytes 1000 | tf_op jit(solution)/shard_map/sum_units/pallas_call | solution.py:761
  201.3 2.1 add_convert_fusion.6
  208.0 2.9 %collective-permute-start.25 = (bf16[96,768]{1,0:T(8,128)(2,1)}, bf16[96,768]{1,0:T(8,128)(2,1)}, u32[]{:S(2)}, u32[]{:S(2)}) collective-permute-start(bf16[96,768]{1,0:T(8,128)(2,1)} %get-tuple-element.193), channel_id=1, source_target_pairs={{0,8},{4,12},{8,0},{12,4},{16,24},{20,28},{24,16},{28,20},{1,9},{5... | collective-permute-start | bytes 442376 | tf_op jit(solution)/shard_map/ppermute | solution.py:234
  211.0 6.7 %input_gradient.1 = (f32[512,768]{1,0:T(8,128)}, bf16[512,768]{1,0:T(8,128)(2,1)}) custom-call(bf16[1024,1152]{1,0:T(8,128)(2,1)} %get-tuple-element.113.refs_2_.d_ref, f32[512,768]{1,0:T(8,128)} %get-tuple-element.178.first_ref, bf16[768,1152]{1,0:T(8,128)(2,1)} %get-tuple-element.114.w_ref), custom_call_target="tpu_custom_call" | custom-call | flops 1000 | bytes 1000 | tf_op jit(solution)/shard_map/input_gradient/pallas_call | solution.py:202
  217.7 2.3 collective-permute-done.28
  220.0 3.6 %collective-permute-done.24 = bf16[8,104,768]{2,1,0:T(8,128)(2,1)S(1)} collective-permute-done((bf16[8,104,768]{2,1,0:T(8,128)(2,1)}, bf16[8,104,768]{2,1,0:T(8,128)(2,1)S(1)}, u32[]{:S(2)}, u32[]{:S(2)}) %collective-permute-start.24) | collective-permute-done | bytes 1277984 | tf_op jit(solution)/shard_map/ppermute | solution.py:245
  227.9 3.1 %collective-permute-start.31 = (bf16[96,768]{1,0:T(8,128)(2,1)S(1)}, bf16[96,768]{1,0:T(8,128)(2,1)S(1)}, u32[]{:S(2)}, u32[]{:S(2)}) collective-permute-start(bf16[96,768]{1,0:T(8,128)(2,1)S(1)} %get-tuple-element.190), channel_id=1, source_target_pairs={{0,8},{4,12},{8,0},{12,4},{16,24},{20,28},{24,16},{28,20},{1,9},{5... | collective-permute-start | bytes 442376 | tf_op jit(solution)/shard_map/ppermute | solution.py:234
  235.2 5.9 %collective-permute-done.32 = bf16[96,768]{1,0:T(8,128)(2,1)S(1)} collective-permute-done((bf16[96,768]{1,0:T(8,128)(2,1)S(1)}, bf16[96,768]{1,0:T(8,128)(2,1)S(1)}, u32[]{:S(2)}, u32[]{:S(2)}) %collective-permute-start.32) | collective-permute-done | bytes 147488 | tf_op jit(solution)/shard_map/ppermute | solution.py:234
  241.5 2.1 collective-permute-start.36
  245.8 2.8 %collective-permute-done.34 = bf16[104,768]{1,0:T(8,128)(2,1)S(1)} collective-permute-done((bf16[104,768]{1,0:T(8,128)(2,1)S(1)}, bf16[104,768]{1,0:T(8,128)(2,1)S(1)}, u32[]{:S(2)}, u32[]{:S(2)}) %collective-permute-start.34) | collective-permute-done | bytes 159776 | tf_op jit(solution)/shard_map/ppermute | solution.py:234
  248.6 3.4 %collective-permute-done.36 = bf16[104,768]{1,0:T(8,128)(2,1)S(1)} collective-permute-done((bf16[104,768]{1,0:T(8,128)(2,1)S(1)}, bf16[104,768]{1,0:T(8,128)(2,1)S(1)}, u32[]{:S(2)}, u32[]{:S(2)}) %collective-permute-start.36) | collective-permute-done | bytes 159776 | tf_op jit(solution)/shard_map/ppermute | solution.py:234
  252.1 7.0 %collective-permute-done.35 = bf16[104,768]{1,0:T(8,128)(2,1)S(1)} collective-permute-done((bf16[104,768]{1,0:T(8,128)(2,1)S(1)}, bf16[104,768]{1,0:T(8,128)(2,1)S(1)}, u32[]{:S(2)}, u32[]{:S(2)}) %collective-permute-start.35) | collective-permute-done | bytes 159776 | tf_op jit(solution)/shard_map/ppermute | solution.py:234
  (212 shorter events, 72.6 us)
Async XLA Ops:
  4.5 7.3 %collective-permute-start.1 = (bf16[104,768]{1,0:T(8,128)(2,1)}, bf16[104,768]{1,0:T(8,128)(2,1)S(1)}, u32[]{:S(2)}, u32[]{:S(2)}) collective-permute-start(bf16[104,768]{1,0:T(8,128)(2,1)} %get-tuple-element.73), channel_id=1, source_target_pairs={{0,8},{4,12},{8,0},{12,4},{16,24},{20,28},{24,16},{28,20},{1,9},{5... | collective-permute-start | bytes 479240 | tf_op jit(solution)/shard_map/ppermute | solution.py:234
  12.8 7.1 %collective-permute-start.2 = (bf16[2,104,768]{2,1,0:T(8,128)(2,1)S(1)}, bf16[2,104,768]{2,1,0:T(8,128)(2,1)S(1)}, u32[]{:S(2)}, u32[]{:S(2)}) collective-permute-start(bf16[2,104,768]{2,1,0:T(8,128)(2,1)S(1)} %pad_maximum_fusion.5.refs_0_), channel_id=1, source_target_pairs={{0,2},{1,5},{2,0},{3,7},{4,6},{5,1},{6,4},{7,3},{8,10},{9,13},{10,... | collective-permute-start | bytes 958472 | tf_op jit(solution)/shard_map/ppermute | solution.py:245
  14.6 16.0 %collective-permute-start.3 = (bf16[2,104,768]{2,1,0:T(8,128)(2,1)S(1)}, bf16[2,104,768]{2,1,0:T(8,128)(2,1)S(1)}, u32[]{:S(2)}, u32[]{:S(2)}) collective-permute-start(bf16[2,104,768]{2,1,0:T(8,128)(2,1)S(1)} %pad_maximum_fusion.5.refs_0_), channel_id=1, source_target_pairs={{0,16},{4,20},{8,24},{12,28},{16,0},{20,4},{24,8},{28,12},{1,17},{... | collective-permute-start | bytes 958472 | tf_op jit(solution)/shard_map/ppermute | solution.py:234
  21.0 16.6 %collective-permute-start.6 = (bf16[4,104,768]{2,1,0:T(8,128)(2,1)S(1)}, bf16[4,104,768]{2,1,0:T(8,128)(2,1)S(1)}, u32[]{:S(2)}, u32[]{:S(2)}) collective-permute-start(bf16[4,104,768]{2,1,0:T(8,128)(2,1)S(1)} %pad_maximum_fusion.2), channel_id=1, source_target_pairs={{0,4},{1,3},{2,6},{3,1},{4,0},{5,7},{6,2},{7,5},{8,12},{9,11},{10,... | collective-permute-start | bytes 1916936 | tf_op jit(solution)/shard_map/ppermute | solution.py:245
  22.8 12.4 %collective-permute-start.5 = (bf16[2,96,768]{2,1,0:T(8,128)(2,1)S(1)}, bf16[2,96,768]{2,1,0:T(8,128)(2,1)S(1)}, u32[]{:S(2)}, u32[]{:S(2)}) collective-permute-start(bf16[2,96,768]{2,1,0:T(8,128)(2,1)S(1)} %copy-done.33), channel_id=1, source_target_pairs={{0,8},{4,12},{8,0},{12,4},{16,24},{20,28},{24,16},{28,20},{1,9},{5... | collective-permute-start | bytes 884744 | tf_op jit(solution)/shard_map/ppermute | solution.py:234
  30.6 7.0 %collective-permute-start.4 = (bf16[2,104,768]{2,1,0:T(8,128)(2,1)S(1)}, bf16[2,104,768]{2,1,0:T(8,128)(2,1)S(1)}, u32[]{:S(2)}, u32[]{:S(2)}) collective-permute-start(bf16[2,104,768]{2,1,0:T(8,128)(2,1)S(1)} %collective-permute-done.3.refs_3_), channel_id=1, source_target_pairs={{0,2},{1,5},{2,0},{3,7},{4,6},{5,1},{6,4},{7,3},{8,10},{9,13},{10,... | collective-permute-start | bytes 958472 | tf_op jit(solution)/shard_map/ppermute | solution.py:245
  37.6 15.2 %collective-permute-start.7 = (bf16[4,104,768]{2,1,0:T(8,128)(2,1)S(1)}, bf16[4,104,768]{2,1,0:T(8,128)(2,1)}, u32[]{:S(2)}, u32[]{:S(2)}) collective-permute-start(bf16[4,104,768]{2,1,0:T(8,128)(2,1)S(1)} %pad_maximum_fusion.3), channel_id=1, source_target_pairs={{0,4},{1,3},{2,6},{3,1},{4,0},{5,7},{6,2},{7,5},{8,12},{9,11},{10,... | collective-permute-start | bytes 1916936 | tf_op jit(solution)/shard_map/ppermute | solution.py:245
  38.4 13.1 %collective-permute-start.8 = (bf16[2,2,96,768]{3,2,1,0:T(8,128)(2,1)S(1)}, bf16[2,2,96,768]{3,2,1,0:T(8,128)(2,1)S(1)}, u32[]{:S(2)}, u32[]{:S(2)}) collective-permute-start(bf16[2,2,96,768]{3,2,1,0:T(8,128)(2,1)S(1)} %pad_maximum_fusion.4.refs_0_), channel_id=1, source_target_pairs={{0,2},{1,5},{2,0},{3,7},{4,6},{5,1},{6,4},{7,3},{8,10},{9,13},{10,... | collective-permute-start | bytes 1769480 | tf_op jit(solution)/shard_map/ppermute | solution.py:245
  39.7 16.0 %collective-permute-start = (bf16[512,768]{1,0:T(8,128)(2,1)S(1)}, bf16[512,768]{1,0:T(8,128)(2,1)S(1)}, u32[]{:S(2)}, u32[]{:S(2)}) collective-permute-start(bf16[512,768]{1,0:T(8,128)(2,1)S(1)} %copy-done.3), channel_id=1, source_target_pairs={{0,1},{1,0},{2,3},{3,2},{4,5},{5,4},{6,7},{7,6},{8,9},{9,8},{10,11... | collective-permute-start | bytes 2359304 | tf_op jit(solution)/shard_map/ppermute | solution.py:229
  39.7 29.3 %collective-permute-start.9 = (bf16[2,2,96,768]{3,2,1,0:T(8,128)(2,1)S(1)}, bf16[2,2,96,768]{3,2,1,0:T(8,128)(2,1)S(1)}, u32[]{:S(2)}, u32[]{:S(2)}) collective-permute-start(bf16[2,2,96,768]{3,2,1,0:T(8,128)(2,1)S(1)} %pad_maximum_fusion.4.refs_0_), channel_id=1, source_target_pairs={{0,16},{4,20},{8,24},{12,28},{16,0},{20,4},{24,8},{28,12},{1,17},{... | collective-permute-start | bytes 1769480 | tf_op jit(solution)/shard_map/ppermute | solution.py:234
  54.0 29.7 %collective-permute-start.10 = (bf16[4,2,96,768]{3,2,1,0:T(8,128)(2,1)}, bf16[4,2,96,768]{3,2,1,0:T(8,128)(2,1)}, u32[]{:S(2)}, u32[]{:S(2)}) collective-permute-start(bf16[4,2,96,768]{3,2,1,0:T(8,128)(2,1)} %pad_maximum_fusion), channel_id=1, source_target_pairs={{0,4},{1,3},{2,6},{3,1},{4,0},{5,7},{6,2},{7,5},{8,12},{9,11},{10,... | collective-permute-start | bytes 3538952 | tf_op jit(solution)/shard_map/ppermute | solution.py:245
  69.0 14.7 %collective-permute-start.11 = (bf16[2,2,96,768]{3,2,1,0:T(8,128)(2,1)S(1)}, bf16[2,2,96,768]{3,2,1,0:T(8,128)(2,1)S(1)}, u32[]{:S(2)}, u32[]{:S(2)}) collective-permute-start(bf16[2,2,96,768]{3,2,1,0:T(8,128)(2,1)S(1)} %collective-permute-done.9.refs_3_), channel_id=1, source_target_pairs={{0,2},{1,5},{2,0},{3,7},{4,6},{5,1},{6,4},{7,3},{8,10},{9,13},{10,... | collective-permute-start | bytes 1769480 | tf_op jit(solution)/shard_map/ppermute | solution.py:245
  84.9 16.5 %collective-permute-start.13 = (bf16[4,2,96,768]{3,2,1,0:T(8,128)(2,1)}, bf16[4,2,96,768]{3,2,1,0:T(8,128)(2,1)}, u32[]{:S(2)}, u32[]{:S(2)}) collective-permute-start(bf16[4,2,96,768]{3,2,1,0:T(8,128)(2,1)} %pad_maximum_fusion.1), channel_id=1, source_target_pairs={{0,4},{1,3},{2,6},{3,1},{4,0},{5,7},{6,2},{7,5},{8,12},{9,11},{10,... | collective-permute-start | bytes 3538952 | tf_op jit(solution)/shard_map/ppermute | solution.py:245
  86.9 3.2 %collective-permute-start.12 = (bf16[512,768]{1,0:T(8,128)(2,1)S(1)}, bf16[512,768]{1,0:T(8,128)(2,1)}, u32[]{:S(2)}, u32[]{:S(2)}) collective-permute-start(bf16[512,768]{1,0:T(8,128)(2,1)S(1)} %convolution_convert_fusion), channel_id=1, source_target_pairs={{0,1},{1,0},{2,3},{3,2},{4,5},{5,4},{6,7},{7,6},{8,9},{9,8},{10,11... | collective-permute-start | bytes 2359304 | tf_op jit(solution)/shard_map/ppermute | solution.py:229
  119.3 2.6 collective-permute-start.16
  152.6 3.2 %collective-permute-start.18 = (bf16[512,768]{1,0:T(8,128)(2,1)}, bf16[512,768]{1,0:T(8,128)(2,1)}, u32[]{:S(2)}, u32[]{:S(2)}) collective-permute-start(bf16[512,768]{1,0:T(8,128)(2,1)} %get-tuple-element.99), channel_id=1, source_target_pairs={{0,1},{1,0},{2,3},{3,2},{4,5},{5,4},{6,7},{7,6},{8,9},{9,8},{10,11... | collective-permute-start | bytes 2359304 | tf_op jit(solution)/shard_map/ppermute | solution.py:229
  153.7 33.8 %collective-permute-start.21 = (bf16[8,96,768]{2,1,0:T(8,128)(2,1)}, bf16[8,96,768]{2,1,0:T(8,128)(2,1)}, u32[]{:S(2)}, u32[]{:S(2)}) collective-permute-start(bf16[8,96,768]{2,1,0:T(8,128)(2,1)} %get-tuple-element.103), channel_id=1, source_target_pairs={{0,2},{1,5},{2,0},{3,7},{4,6},{5,1},{6,4},{7,3},{8,10},{9,13},{10,... | collective-permute-start | bytes 3538952 | tf_op jit(solution)/shard_map/ppermute | solution.py:245
  155.1 32.4 %collective-permute-start.22 = (bf16[8,96,768]{2,1,0:T(8,128)(2,1)}, bf16[8,96,768]{2,1,0:T(8,128)(2,1)}, u32[]{:S(2)}, u32[]{:S(2)}) collective-permute-start(bf16[8,96,768]{2,1,0:T(8,128)(2,1)} %get-tuple-element.104), channel_id=1, source_target_pairs={{0,2},{1,5},{2,0},{3,7},{4,6},{5,1},{6,4},{7,3},{8,10},{9,13},{10,... | collective-permute-start | bytes 3538952 | tf_op jit(solution)/shard_map/ppermute | solution.py:245
  188.8 10.3 %collective-permute-start.23 = (bf16[4,96,768]{2,1,0:T(8,128)(2,1)S(1)}, bf16[4,96,768]{2,1,0:T(8,128)(2,1)S(1)}, u32[]{:S(2)}, u32[]{:S(2)}) collective-permute-start(bf16[4,96,768]{2,1,0:T(8,128)(2,1)S(1)} %add_convert_fusion.9), channel_id=1, source_target_pairs={{0,4},{1,3},{2,6},{3,1},{4,0},{5,7},{6,2},{7,5},{8,12},{9,11},{10,... | collective-permute-start | bytes 1769480 | tf_op jit(solution)/shard_map/ppermute | solution.py:245
  199.9 23.8 %collective-permute-start.24 = (bf16[8,104,768]{2,1,0:T(8,128)(2,1)}, bf16[8,104,768]{2,1,0:T(8,128)(2,1)S(1)}, u32[]{:S(2)}, u32[]{:S(2)}) collective-permute-start(bf16[8,104,768]{2,1,0:T(8,128)(2,1)} %get-tuple-element.112), channel_id=1, source_target_pairs={{0,2},{1,5},{2,0},{3,7},{4,6},{5,1},{6,4},{7,3},{8,10},{9,13},{10,... | collective-permute-start | bytes 3833864 | tf_op jit(solution)/shard_map/ppermute | solution.py:245
  203.4 16.6 %collective-permute-start.28 = (bf16[4,96,768]{2,1,0:T(8,128)(2,1)}, bf16[4,96,768]{2,1,0:T(8,128)(2,1)}, u32[]{:S(2)}, u32[]{:S(2)}) collective-permute-start(bf16[4,96,768]{2,1,0:T(8,128)(2,1)} %add_convert_fusion.6), channel_id=1, source_target_pairs={{0,4},{1,3},{2,6},{3,1},{4,0},{5,7},{6,2},{7,5},{8,12},{9,11},{10,... | collective-permute-start | bytes 1769480 | tf_op jit(solution)/shard_map/ppermute | solution.py:245
  206.6 13.4 %collective-permute-start.27 = (bf16[96,768]{1,0:T(8,128)(2,1)}, bf16[96,768]{1,0:T(8,128)(2,1)S(1)}, u32[]{:S(2)}, u32[]{:S(2)}) collective-permute-start(bf16[96,768]{1,0:T(8,128)(2,1)} %get-tuple-element.191), channel_id=1, source_target_pairs={{0,24},{4,28},{8,16},{12,20},{16,8},{20,12},{24,0},{28,4},{1,25},{... | collective-permute-start | bytes 442376 | tf_op jit(solution)/shard_map/ppermute | solution.py:234
  208.0 12.0 %collective-permute-start.26 = (bf16[96,768]{1,0:T(8,128)(2,1)}, bf16[96,768]{1,0:T(8,128)(2,1)S(1)}, u32[]{:S(2)}, u32[]{:S(2)}) collective-permute-start(bf16[96,768]{1,0:T(8,128)(2,1)} %get-tuple-element.192), channel_id=1, source_target_pairs={{0,16},{4,20},{8,24},{12,28},{16,0},{20,4},{24,8},{28,12},{1,17},{... | collective-permute-start | bytes 442376 | tf_op jit(solution)/shard_map/ppermute | solution.py:234
  208.0 12.0 %collective-permute-start.25 = (bf16[96,768]{1,0:T(8,128)(2,1)}, bf16[96,768]{1,0:T(8,128)(2,1)}, u32[]{:S(2)}, u32[]{:S(2)}) collective-permute-start(bf16[96,768]{1,0:T(8,128)(2,1)} %get-tuple-element.193), channel_id=1, source_target_pairs={{0,8},{4,12},{8,0},{12,4},{16,24},{20,28},{24,16},{28,20},{1,9},{5... | collective-permute-start | bytes 442376 | tf_op jit(solution)/shard_map/ppermute | solution.py:234
  223.6 9.0 %collective-permute-start.30 = (bf16[512,768]{1,0:T(8,128)(2,1)}, bf16[512,768]{1,0:T(8,128)(2,1)S(1)}, u32[]{:S(2)}, u32[]{:S(2)}) collective-permute-start(bf16[512,768]{1,0:T(8,128)(2,1)} %get-tuple-element.122), channel_id=1, source_target_pairs={{0,1},{1,0},{2,3},{3,2},{4,5},{5,4},{6,7},{7,6},{8,9},{9,8},{10,11... | collective-permute-start | bytes 2359304 | tf_op jit(solution)/shard_map/ppermute | solution.py:229
  223.8 17.3 %collective-permute-start.29 = (bf16[4,104,768]{2,1,0:T(8,128)(2,1)S(1)}, bf16[4,104,768]{2,1,0:T(8,128)(2,1)S(1)}, u32[]{:S(2)}, u32[]{:S(2)}) collective-permute-start(bf16[4,104,768]{2,1,0:T(8,128)(2,1)S(1)} %add_convert_fusion.3), channel_id=1, source_target_pairs={{0,4},{1,3},{2,6},{3,1},{4,0},{5,7},{6,2},{7,5},{8,12},{9,11},{10,... | collective-permute-start | bytes 1916936 | tf_op jit(solution)/shard_map/ppermute | solution.py:245
  226.5 8.7 %collective-permute-start.33 = (bf16[96,768]{1,0:T(8,128)(2,1)S(1)}, bf16[96,768]{1,0:T(8,128)(2,1)S(1)}, u32[]{:S(2)}, u32[]{:S(2)}) collective-permute-start(bf16[96,768]{1,0:T(8,128)(2,1)S(1)} %get-tuple-element.188), channel_id=1, source_target_pairs={{0,24},{4,28},{8,16},{12,20},{16,8},{20,12},{24,0},{28,4},{1,25},{... | collective-permute-start | bytes 442376 | tf_op jit(solution)/shard_map/ppermute | solution.py:234
  227.9 13.3 %collective-permute-start.32 = (bf16[96,768]{1,0:T(8,128)(2,1)S(1)}, bf16[96,768]{1,0:T(8,128)(2,1)S(1)}, u32[]{:S(2)}, u32[]{:S(2)}) collective-permute-start(bf16[96,768]{1,0:T(8,128)(2,1)S(1)} %get-tuple-element.189), channel_id=1, source_target_pairs={{0,16},{4,20},{8,24},{12,28},{16,0},{20,4},{24,8},{28,12},{1,17},{... | collective-permute-start | bytes 442376 | tf_op jit(solution)/shard_map/ppermute | solution.py:234
  227.9 13.3 %collective-permute-start.31 = (bf16[96,768]{1,0:T(8,128)(2,1)S(1)}, bf16[96,768]{1,0:T(8,128)(2,1)S(1)}, u32[]{:S(2)}, u32[]{:S(2)}) collective-permute-start(bf16[96,768]{1,0:T(8,128)(2,1)S(1)} %get-tuple-element.190), channel_id=1, source_target_pairs={{0,8},{4,12},{8,0},{12,4},{16,24},{20,28},{24,16},{28,20},{1,9},{5... | collective-permute-start | bytes 442376 | tf_op jit(solution)/shard_map/ppermute | solution.py:234
  241.4 7.2 %collective-permute-start.34 = (bf16[104,768]{1,0:T(8,128)(2,1)S(1)}, bf16[104,768]{1,0:T(8,128)(2,1)S(1)}, u32[]{:S(2)}, u32[]{:S(2)}) collective-permute-start(bf16[104,768]{1,0:T(8,128)(2,1)S(1)} %get-tuple-element.185), channel_id=1, source_target_pairs={{0,8},{4,12},{8,0},{12,4},{16,24},{20,28},{24,16},{28,20},{1,9},{5... | collective-permute-start | bytes 479240 | tf_op jit(solution)/shard_map/ppermute | solution.py:234
  241.5 10.5 %collective-permute-start.36 = (bf16[104,768]{1,0:T(8,128)(2,1)S(1)}, bf16[104,768]{1,0:T(8,128)(2,1)S(1)}, u32[]{:S(2)}, u32[]{:S(2)}) collective-permute-start(bf16[104,768]{1,0:T(8,128)(2,1)S(1)} %get-tuple-element.186), channel_id=1, source_target_pairs={{0,24},{4,28},{8,16},{12,20},{16,8},{20,12},{24,0},{28,4},{1,25},{... | collective-permute-start | bytes 479240 | tf_op jit(solution)/shard_map/ppermute | solution.py:234
  243.6 15.5 %collective-permute-start.35 = (bf16[104,768]{1,0:T(8,128)(2,1)S(1)}, bf16[104,768]{1,0:T(8,128)(2,1)S(1)}, u32[]{:S(2)}, u32[]{:S(2)}) collective-permute-start(bf16[104,768]{1,0:T(8,128)(2,1)S(1)} %get-tuple-element.187), channel_id=1, source_target_pairs={{0,16},{4,20},{8,24},{12,28},{16,0},{20,4},{24,8},{28,12},{1,17},{... | collective-permute-start | bytes 479240 | tf_op jit(solution)/shard_map/ppermute | solution.py:234
  (41 other events, 390.4 us)

commit v2 on v1

--- a/solution.py
+++ b/solution.py
@@ -84,6 +84,7 @@
         ],
         input_output_aliases={5 + i: i for i in range(len(made))},
         cost_estimate=CHEAP,
+        compiler_params=pltpu.CompilerParams(vmem_limit_bytes=30 * 1024 * 1024),
         name="attention_forward",
     )(seg_col, seg_row, qkv, qkv, qkv, *made)
 
@@ -176,6 +177,7 @@
         out_shape=[jax.ShapeDtypeStruct((rows, triple), BF16), jax.ShapeDtypeStruct((1, 2 * width), F32)],
         scratch_shapes=[pltpu.VMEM((rows, width), F32), pltpu.VMEM((rows, width), F32)],
         cost_estimate=CHEAP,
+        compiler_params=pltpu.CompilerParams(vmem_limit_bytes=30 * 1024 * 1024),
         name="attention_backward",
     )(seg_col, seg_row, qkv, qkv, qkv, ctx, lse, d_own, d_other)
 
@@ -265,7 +267,7 @@
     return jnp.concatenate(parts[1:]) if len(parts) > 2 else parts[1]
 
 
-OPT = {'bc': None, 'bn1': 'f2', 'bz2': 'qkv', 'bf1': 'ctx', 'bn2': 'ctx', 'bf2': 'attn', 'c1': 'P3', 'c2': 'P4', 'c3': 'P5', 'b1': 'P3', 'b2': 'P5', 'b3': 'P6', 'an2': 'f1', 'bz1': 'f1'}
+OPT = {'bc': None, 'bn1': 'f2', 'bz2': 'qkv', 'bf1': 'ctx', 'bn2': 'ctx', 'bf2': 'attn', 'c1': 'P3', 'c2': 'P4', 'c3': 'P5', 'b1': 'P3', 'b2': 'P4', 'b3': 'P6', 'an2': 'f1', 'bz1': 'f1'}
 
 
 def stage(name, *values, **items):
@@ -357,7 +359,7 @@
     rows += jnp.where(line == 2, low, 0.0) + jnp.where(line == 3, row_ref[1:2, :], 0.0)
     a_ref[piece:, :] = rows.astype(BF16)
     bc_ref[0] = up_ref[...]
-    bc_ref[1] = down_ref[...].T
+    bc_ref[1] = down_ref[...]
 
 
 def prepare(w_qkv, w_out, w_up, w_down, b_qv, vectors):
@@ -369,7 +371,7 @@
         def whole(s):
             return pl.BlockSpec(s, lambda i, d: (0,) * len(s))
 
-        given = [w_qkv, w_out, w_up, w_down, b_qv, *[v[None] for v in vectors]]
+        given = [w_qkv, w_out, w_up, w_down.T, b_qv, *[v[None] for v in vectors]]
         shapes = [(piece + 8, model), (2, piece, model)]
         return pl.pallas_call(
             functools.partial(prepare_kernel, piece),
@@ -641,31 +643,6 @@
     return hidden, slope, part[:rows], part[rows:].astype(BF16), b, c
 
 
-def pull(own, other, slope, c, b, block):
-    rows, model = own.shape
-    wide = b.shape[1]
-    halves = rows // block
-
-    def whole(s):
-        return pl.BlockSpec(s, lambda i: (0, 0))
-
-    by_row = pl.BlockSpec((block, wide), lambda i: (i, 0))
-    return pl.pallas_call(
-        functools.partial(pull_kernel, halves),
-        grid=(2 * halves,),
-        in_specs=[*split_specs(block, model, halves), by_row, whole(c.shape), whole(b.shape)],
-        out_specs=[by_row, *split_specs(block, model, halves), whole((1, wide))],
-        out_shape=[
-            jax.ShapeDtypeStruct((2 * rows, wide), BF16),
-            jax.ShapeDtypeStruct((rows, model), F32),
-            jax.ShapeDtypeStruct((rows, model), BF16),
-            jax.ShapeDtypeStruct((1, wide), F32),
-        ],
-        cost_estimate=CHEAP,
-        name="pull_kernel",
-    )(own, other, slope, c, b)
-
-
 def where():
     return jnp.stack([lax.axis_index("dp"), lax.axis_index("c")]).astype(jnp.int32)
 
@@ -673,15 +650,18 @@
 def sum_kernel(parts, piece, extra, part, where_ref, *refs):
     count = 1 + max(max(*p[0], p[1]) for p in parts)
     ins = refs[:count]
-    scratch = refs[count + (2 if extra else 0) :]
+    scratch = refs[count + (3 if extra else 0) :]
     outs, left_ref, acc, ext_ref = scratch[:2], scratch[2], scratch[3], scratch[4]
     dp, step = where_ref[0], pl.program_id(0)
     outer = outs[0].shape[0] // 2
     blocked = parts[0][4]
     if extra:
-        lines_ref, bias_ref = refs[count : count + 2]
-        ext_ref[...] = lines_ref[...].astype(F32)
+        lines_ref, up_ref, bias_ref = refs[count : count + 3]
+        model = lines_ref.shape[1]
         for rx in range(2):
+            ext_ref[rx] = jnp.zeros(ext_ref.shape[1:], F32)
+            ext_ref[rx, 0:1, :] = up_ref[0:1, rx * model : (rx + 1) * model]
+            ext_ref[rx, 1:7, :] = lines_ref[0:6, :]
             for k in range(2):
                 ext_ref[rx, extra - 1 : extra, k * part : (k + 1) * part] = bias_ref[
                     0:1, (2 * k + rx) * part : (2 * k + rx + 1) * part
@@ -740,19 +720,19 @@
             put(rx)
 
 
-def summed(arrays, parts, ext=None, bias=None):
+def summed(arrays, parts, lines=None, bias_up=None, bias=None):
     ndp = lax.axis_size("dp")
     model = arrays[0].shape[1]
     piece = model // ndp
     blocked = parts[0][4]
     width = sum(p[2] if p[4] else arrays[p[1]].shape[1] // 2 for p in parts)
-    extra = 0 if ext is None else ext.shape[1]
+    extra = 0 if lines is None else 8
     if piece % 16 == 0:
 
         def whole(s):
             return pl.BlockSpec(s, lambda i, d: (0,) * len(s))
 
-        given = list(arrays) + ([] if ext is None else [ext, bias])
+        given = list(arrays) + ([] if lines is None else [lines, bias_up, bias])
         specs = [whole(a.shape) for a in given]
         if blocked:
             right = parts[0][1]
@@ -773,14 +753,16 @@
             ),
             out_shape=[jax.ShapeDtypeStruct(shape, BF16)] * 2,
             cost_estimate=CHEAP,
-            name="sum_units",
+        compiler_params=pltpu.CompilerParams(vmem_limit_bytes=40 * 1024 * 1024),
+        name="sum_units",
         )(where(), *given)
     order = jnp.bitwise_xor(jnp.arange(ndp), lax.axis_index("dp"))
     sides = []
     if extra:
         line = jnp.transpose(bias.reshape(2, 2, -1), (1, 0, 2)).reshape(2, -1)
         line = jnp.pad(line, ((0, 0), (0, width - line.shape[1]))).astype(BF16)
-        ext = jnp.concatenate([ext[:, :-1], line[:, None]], axis=1)
+        both = jnp.broadcast_to(lines.astype(BF16)[None], (2, *lines.shape))
+        ext = jnp.concatenate([bias_up.astype(BF16).reshape(2, 1, -1), both, line[:, None]], axis=1)
     for rx in range(2):
         g = []
         for (own, other), right, cols, _, by_block in parts:
@@ -979,14 +961,12 @@
     sums = jnp.stack([d_bias_out, d_bias_down, d_gain_one, d_shift_one, d_gain_two, d_shift_two])
     sums = sums + swap(sums)
     d_ctx_other = dot_nn(da_other, o_t).astype(BF16)
-    spread = jnp.concatenate([d_bias_up.reshape(nx, model), jnp.broadcast_to(sums.reshape(1, -1), (nx, 6 * model))], axis=1)
-    spread = jnp.pad(spread.reshape(nx, 7, model), ((0, 0), (0, 1), (0, 0))).astype(BF16)
-    d_ctx_other, spread = go("P2", d_ctx_other, spread)
+    d_ctx_other = go("P2", d_ctx_other)
     d_qkv, bias = attention_backward(qkv, ctx, lse, d_ctx, d_ctx_other, seg_col, seg_row, block)
     d_qkv = go("P3", d_qkv)
     attention_parts = [((0, 1), 2, part, 0, False), ((3, 4), 5, part, 3 * part, False)]
     given = [tokens, x_other, d_qkv, d_attn, da_other, ctx]
-    sa = Scatter(summed(given, attention_parts, spread, bias))
+    sa = Scatter(summed(given, attention_parts, sums, d_bias_up, bias))
     d_qkv, sa.send = go("P4", d_qkv, sa.send)
     sa.first()
     keep, send = input_gradient(d_qkv, d_first, w_all, block)

time: 263 us -> 252 us (0.958)
  Pallas kernels: 93.7 us -> 84.8 us
  other arithmetic: 27.2 us -> 24.1 us
    pallas_call x1, Pallas kernels: 21 us -> 17.7 us  [attention_backward(): pl.pallas_call(functools.partial(attention_backward_kernel, width, halves...]
    pallas_call x1, Pallas kernels: 8.82 us -> 5.44 us  [summed(): pl.pallas_call(functools.partial(sum_kernel, parts, piece, extra, 0 if bi...]
    ppermute x14, waiting for transfers between devices: 32.6 us -> 29.4 us  [turn(): return lax.ppermute(a, ('dp', 'x', 'c'), pairs)]
    unnamed x75 -> x94, local copies, waits for them, and re-layouts: 8.69 us -> 11.6 us
    ppermute x13, waiting for transfers between devices: 39.4 us -> 42.1 us  [flip(): return lax.ppermute(a, axis, [(i, i ^ bit) for i in range(n)])]
  transfers between devices with their start and end apart: 37 -> 37, of which waited for: 21 -> 25; matrix products, arithmetic and copies ran while one was open for 10% -> 9% of each run, Pallas kernels for 22% -> 19%
where the time goes in v2:
time: 252 us
  Pallas kernels  84.8 us (34%)
  waiting for transfers between devices  82.2 us (33%)
  starting transfers between devices  39.3 us (16%)
  other arithmetic  24.1 us (10%)
  local copies, waits for them, and re-layouts  16.5 us (7%)
  matrix products  3.55 us (1%)
    ppermute x13, waiting for transfers between devices, flip(): return lax.ppermute(a, axis, [(i, i ^ bit) for i in range(n)])  42.1 us
    ppermute x14, waiting for transfers between devices, turn(): return lax.ppermute(a, ('dp', 'x', 'c'), pairs)  29.4 us
    pallas_call x1, Pallas kernels, feed_back(): pl.pallas_call(functools.partial(feed_back_kernel, 256, piece), grid_spec...  21 us
    ppermute x13, starting transfers between devices, flip(): return lax.ppermute(a, axis, [(i, i ^ bit) for i in range(n)])  20.7 us
    pallas_call x1, Pallas kernels, attention_backward(): pl.pallas_call(functools.partial(attention_backward_kernel, width, halves...  17.7 us
    ppermute x14, starting transfers between devices, turn(): return lax.ppermute(a, ('dp', 'x', 'c'), pairs)  17.2 us
    pallas_call x1, Pallas kernels, feed(): pl.pallas_call(functools.partial(feed_kernel, index, moves, halves), grid...  13.7 us
    unnamed x94, local copies, waits for them, and re-layouts  11.6 us
  transfers between devices with their start and end apart: 37, of which 25 were waited for; matrix products, arithmetic and copies ran while one was open for 9% of the time, Pallas kernels for 19%

profile of v2, /device:TPU:0, one launch (start us, length us, event | category | flops | bytes accessed | tf_op | source)
XLA Modules:
  0.0 251.8 jit_solution(17693030317164307563)
XLA Ops:
  0.7 2.0 prepare_units.1
  2.7 3.0 %collective-permute-start.1 = (bf16[104,768]{1,0:T(8,128)(2,1)}, bf16[104,768]{1,0:T(8,128)(2,1)S(1)}, u32[]{:S(2)}, u32[]{:S(2)}) collective-permute-start(bf16[104,768]{1,0:T(8,128)(2,1)} %get-tuple-element.71), channel_id=1, source_target_pairs={{0,8},{4,12},{8,0},{12,4},{16,24},{20,28},{24,16},{28,20},{1,9},{5... | collective-permute-start | bytes 479240 | tf_op jit(solution)/shard_map/ppermute | solution.py:236
  5.7 4.3 %collective-permute-done.1 = bf16[104,768]{1,0:T(8,128)(2,1)S(1)} collective-permute-done((bf16[104,768]{1,0:T(8,128)(2,1)}, bf16[104,768]{1,0:T(8,128)(2,1)S(1)}, u32[]{:S(2)}, u32[]{:S(2)}) %collective-permute-start.1) | collective-permute-done | bytes 159776 | tf_op jit(solution)/shard_map/ppermute | solution.py:236
  12.8 2.6 %collective-permute-start.3 = (bf16[2,104,768]{2,1,0:T(8,128)(2,1)S(1)}, bf16[2,104,768]{2,1,0:T(8,128)(2,1)S(1)}, u32[]{:S(2)}, u32[]{:S(2)}) collective-permute-start(bf16[2,104,768]{2,1,0:T(8,128)(2,1)S(1)} %pad_maximum_fusion.5.refs_0_), channel_id=1, source_target_pairs={{0,16},{4,20},{8,24},{12,28},{16,0},{20,4},{24,8},{28,12},{1,17},{... | collective-permute-start | bytes 958472 | tf_op jit(solution)/shard_map/ppermute | solution.py:236
  15.3 2.7 %collective-permute-done.2.refs_1_ = bf16[2,104,768]{2,1,0:T(8,128)(2,1)S(1)} collective-permute-done((bf16[2,104,768]{2,1,0:T(8,128)(2,1)S(1)}, bf16[2,104,768]{2,1,0:T(8,128)(2,1)S(1)}, u32[]{:S(2)}, u32[]{:S(2)}) %collective-permute-start.2) | collective-permute-done | bytes 319520 | tf_op jit(solution)/shard_map/ppermute | solution.py:247
  22.5 6.2 %collective-permute-done.3.refs_3_ = bf16[2,104,768]{2,1,0:T(8,128)(2,1)S(1)} collective-permute-done((bf16[2,104,768]{2,1,0:T(8,128)(2,1)S(1)}, bf16[2,104,768]{2,1,0:T(8,128)(2,1)S(1)}, u32[]{:S(2)}, u32[]{:S(2)}) %collective-permute-start.3) | collective-permute-done | bytes 319520 | tf_op jit(solution)/shard_map/ppermute | solution.py:236
  30.3 3.1 %collective-permute-done.5 = bf16[2,96,768]{2,1,0:T(8,128)(2,1)S(1)} collective-permute-done((bf16[2,96,768]{2,1,0:T(8,128)(2,1)S(1)}, bf16[2,96,768]{2,1,0:T(8,128)(2,1)S(1)}, u32[]{:S(2)}, u32[]{:S(2)}) %collective-permute-start.5) | collective-permute-done | bytes 294944 | tf_op jit(solution)/shard_map/ppermute | solution.py:236
  33.5 2.3 collective-permute-done.4.refs_4_
  39.1 10.6 %collective-permute-done.8.refs_1_ = bf16[2,2,96,768]{3,2,1,0:T(8,128)(2,1)S(1)} collective-permute-done((bf16[2,2,96,768]{3,2,1,0:T(8,128)(2,1)S(1)}, bf16[2,2,96,768]{3,2,1,0:T(8,128)(2,1)S(1)}, u32[]{:S(2)}, u32[]{:S(2)}) %collective-permute-start.8) | collective-permute-done | bytes 589856 | tf_op jit(solution)/shard_map/ppermute | solution.py:247
  54.7 7.6 %project_kernel.1 = (bf16[1024,1152]{1,0:T(8,128)(2,1)}, bf16[768,1152]{1,0:T(8,128)(2,1)}, bf16[768,384]{1,0:T(8,128)(2,1)}, bf16[8,8,768]{2,1,0:T(8,128)(2,1)}) custom-call(s32[2]{0:T(128)} %pad_add_fusion.1.where_ref, bf16[512,768]{1,0:T(8,128)(2,1)} %refs_0_.1, bf16[512,768]{1,0:T(8,128)(2,1)} %copy-done.10, bf16[2,104,768]{2,1,0:T(8,128)(2,1)} %copy-done.34, ...), custom_call_target="tpu_custom_call" | custom-call | flops 1000 | bytes 1000 | tf_op jit(solution)/shard_map/project_kernel/pallas_call | solution.py:592
  62.3 4.9 %collective-permute-done.9.refs_3_ = bf16[2,2,96,768]{3,2,1,0:T(8,128)(2,1)S(1)} collective-permute-done((bf16[2,2,96,768]{3,2,1,0:T(8,128)(2,1)S(1)}, bf16[2,2,96,768]{3,2,1,0:T(8,128)(2,1)S(1)}, u32[]{:S(2)}, u32[]{:S(2)}) %collective-permute-start.9) | collective-permute-done | bytes 589856 | tf_op jit(solution)/shard_map/ppermute | solution.py:236
  70.0 10.7 %attention_forward.1 = (bf16[1024,384]{1,0:T(8,128)(2,1)S(1)}, f32[8,1024]{1,0:T(8,128)S(1)}) custom-call(s32[1024,1]{1,0:T(8,128)S(1)} %copy.31.seg_q_ref.seg_k_ref, s32[1,1024]{1,0:T(1,128)S(1)} %bitcast.87, bf16[1024,1152]{1,0:T(8,128)(2,1)S(1)} %copy-done.2, bf16[1024,1152]{1,0:T(8,128)(2,1)S(1)} %copy-done.2, bf16[1024,1152]{1,0:T(8,128)(2,1)S(1)} %copy-done.2), custom_call_target="tpu_custom_call" | custom-call | flops 1000 | bytes 1000 | tf_op jit(solution)/shard_map/attention_forward/pallas_call | solution.py:66
  89.0 9.6 %collective-permute-done.13.refs_5_ = bf16[4,2,96,768]{3,2,1,0:T(8,128)(2,1)} collective-permute-done((bf16[4,2,96,768]{3,2,1,0:T(8,128)(2,1)}, bf16[4,2,96,768]{3,2,1,0:T(8,128)(2,1)}, u32[]{:S(2)}, u32[]{:S(2)}) %collective-permute-start.13) | collective-permute-done | bytes 1179680 | tf_op jit(solution)/shard_map/ppermute | solution.py:247
  101.9 13.7 %feed_kernel.1 = (bf16[1024,1536]{1,0:T(8,128)(2,1)}, bf16[1024,1536]{1,0:T(8,128)(2,1)}, f32[512,768]{1,0:T(8,128)}, bf16[512,768]{1,0:T(8,128)(2,1)}, bf16[768...) custom-call(s32[2]{0:T(128)} %pad_add_fusion.1.where_ref, bf16[512,768]{1,0:T(8,128)(2,1)} %copy-done.21, ...), custom_call_target="tpu_custom_call" | custom-call | flops 1000 | bytes 1000 | tf_op jit(solution)/shard_map/feed_kernel/pallas_call | solution.py:625
  116.0 2.2 collective-permute-done.16
  118.2 2.1 fusion.21
  124.4 2.1 collective-permute-done.17.refs_1_
  127.5 21.0 %feed_back.1 = (f32[512,768]{1,0:T(8,128)}, bf16[512,768]{1,0:T(8,128)(2,1)}, f32[1,1536]{1,0:T(1,128)}, bf16[8,96,768]{2,1,0:T(8,128)(2,1)}, bf16[8,96,768]{2,1...) custom-call(s32[2]{0:T(128)} %pad_add_fusion.1.where_ref, bf16[512,768]{1,0:T(8,128)(2,1)} %copy-done.24, ...), custom_call_target="tpu_custom_call" | custom-call | flops 1000 | bytes 1000 | tf_op jit(solution)/shard_map/feed_back/pallas_call | solution.py:533
  151.2 3.8 %multiply_reduce_fusion = (f32[768]{0:T(1024)S(1)}, f32[512]{0:T(512)S(1)}, f32[512]{0:T(512)S(1)}, f32[768]{0:T(1024)S(1)}, f32[512,768]{1,0:T(8,128)S(1)}, /*index=5*/bf16[512,768]{1,0:T(8,128)(2,1)}) fusion(f32[512,768]{1,0:T(8,128)S(1)} %get-tuple-element.179, f32[512]{0:T(512)S(1)} %add_rsqrt_fusion.1, f32[512]{0:T(512)S(1)} %broadcast_multiply_fusion.5, ...), kind=kLoop, calls=%fused_computation.11 | loop fusion | flops 9041408 | bytes 8682496 | tf_op jit(solution)/shard_map/reduce_sum | solution.py:954
  159.9 17.7 %attention_backward.1 = (bf16[1024,1152]{1,0:T(8,128)(2,1)S(1)}, f32[1,768]{1,0:T(1,128)S(1)}) custom-call(s32[1024,1]{1,0:T(8,128)S(1)} %copy-done.9, s32[1,1024]{1,0:T(1,128)S(1)} %bitcast.88, bf16[1024,1152]{1,0:T(8,128)(2,1)S(1)} %copy-done.3, bf16[1024,1152]{1,0:T(8,128)(2,1)S(1)} %copy-done.3, bf16[1024,1152]{1,0:T(8,128)(2,1)S(1)} %copy-done.3, ...), custom_call_target="tpu_custom_call" | custom-call | flops 1000 | bytes 1000 | tf_op jit(solution)/shard_map/attention_backward/pallas_call | solution.py:163
  188.0 5.4 %sum_units.1 = (bf16[8,104,768]{2,1,0:T(8,128)(2,1)S(1)}, bf16[8,104,768]{2,1,0:T(8,128)(2,1)}) custom-call(s32[2]{0:T(128)S(1)} %copy-done.18, bf16[512,768]{1,0:T(8,128)(2,1)S(1)} %copy-done.7, bf16[512,768]{1,0:T(8,128)(2,1)S(1)} %copy-done.11, bf16[1024,1152]{1,0:T(8,128)(2,1)S(1)} %get-tuple-element.111.refs_2_.d_ref, bf16[512,768]{1,0:T(8,128)(2,1)S(1)} %copy-done.13, ...), custom_call_target="tpu_custom_call" | custom-call | flops 1000 | bytes 1000 | tf_op jit(solution)/shard_map/sum_units/pallas_call | solution.py:741
  193.4 2.0 collective-permute-done.23
  198.9 2.0 collective-permute-start.28
  200.9 2.4 collective-permute-start.26
  203.3 6.7 %input_gradient.1 = (f32[512,768]{1,0:T(8,128)}, bf16[512,768]{1,0:T(8,128)(2,1)}) custom-call(bf16[1024,1152]{1,0:T(8,128)(2,1)} %copy-done.4, f32[512,768]{1,0:T(8,128)} %get-tuple-element.174.first_ref, bf16[768,1152]{1,0:T(8,128)(2,1)} %get-tuple-element.112.w_ref), custom_call_target="tpu_custom_call" | custom-call | flops 1000 | bytes 1000 | tf_op jit(solution)/shard_map/input_gradient/pallas_call | solution.py:204
  210.0 2.4 collective-permute-done.27
  217.6 2.9 %collective-permute-start.31 = (bf16[96,768]{1,0:T(8,128)(2,1)S(1)}, bf16[96,768]{1,0:T(8,128)(2,1)S(1)}, u32[]{:S(2)}, u32[]{:S(2)}) collective-permute-start(bf16[96,768]{1,0:T(8,128)(2,1)S(1)} %get-tuple-element.186), channel_id=1, source_target_pairs={{0,8},{4,12},{8,0},{12,4},{16,24},{20,28},{24,16},{28,20},{1,9},{5... | collective-permute-start | bytes 442376 | tf_op jit(solution)/shard_map/ppermute | solution.py:236
  222.4 2.4 collective-permute-done.33
  224.8 5.5 %collective-permute-done.32 = bf16[96,768]{1,0:T(8,128)(2,1)S(1)} collective-permute-done((bf16[96,768]{1,0:T(8,128)(2,1)S(1)}, bf16[96,768]{1,0:T(8,128)(2,1)S(1)}, u32[]{:S(2)}, u32[]{:S(2)}) %collective-permute-start.32) | collective-permute-done | bytes 147488 | tf_op jit(solution)/shard_map/ppermute | solution.py:236
  234.9 2.3 collective-permute-done.34
  237.2 3.9 %collective-permute-done.36 = bf16[104,768]{1,0:T(8,128)(2,1)S(1)} collective-permute-done((bf16[104,768]{1,0:T(8,128)(2,1)S(1)}, bf16[104,768]{1,0:T(8,128)(2,1)S(1)}, u32[]{:S(2)}, u32[]{:S(2)}) %collective-permute-start.36) | collective-permute-done | bytes 159776 | tf_op jit(solution)/shard_map/ppermute | solution.py:236
  241.1 7.0 %collective-permute-done.35 = bf16[104,768]{1,0:T(8,128)(2,1)S(1)} collective-permute-done((bf16[104,768]{1,0:T(8,128)(2,1)S(1)}, bf16[104,768]{1,0:T(8,128)(2,1)S(1)}, u32[]{:S(2)}, u32[]{:S(2)}) %collective-permute-start.35) | collective-permute-done | bytes 159776 | tf_op jit(solution)/shard_map/ppermute | solution.py:236
  (224 shorter events, 73.1 us)
Async XLA Ops:
  2.7 7.3 %collective-permute-start.1 = (bf16[104,768]{1,0:T(8,128)(2,1)}, bf16[104,768]{1,0:T(8,128)(2,1)S(1)}, u32[]{:S(2)}, u32[]{:S(2)}) collective-permute-start(bf16[104,768]{1,0:T(8,128)(2,1)} %get-tuple-element.71), channel_id=1, source_target_pairs={{0,8},{4,12},{8,0},{12,4},{16,24},{20,28},{24,16},{28,20},{1,9},{5... | collective-permute-start | bytes 479240 | tf_op jit(solution)/shard_map/ppermute | solution.py:236
  11.0 7.1 %collective-permute-start.2 = (bf16[2,104,768]{2,1,0:T(8,128)(2,1)S(1)}, bf16[2,104,768]{2,1,0:T(8,128)(2,1)S(1)}, u32[]{:S(2)}, u32[]{:S(2)}) collective-permute-start(bf16[2,104,768]{2,1,0:T(8,128)(2,1)S(1)} %pad_maximum_fusion.5.refs_0_), channel_id=1, source_target_pairs={{0,2},{1,5},{2,0},{3,7},{4,6},{5,1},{6,4},{7,3},{8,10},{9,13},{10,... | collective-permute-start | bytes 958472 | tf_op jit(solution)/shard_map/ppermute | solution.py:247
  12.8 16.0 %collective-permute-start.3 = (bf16[2,104,768]{2,1,0:T(8,128)(2,1)S(1)}, bf16[2,104,768]{2,1,0:T(8,128)(2,1)S(1)}, u32[]{:S(2)}, u32[]{:S(2)}) collective-permute-start(bf16[2,104,768]{2,1,0:T(8,128)(2,1)S(1)} %pad_maximum_fusion.5.refs_0_), channel_id=1, source_target_pairs={{0,16},{4,20},{8,24},{12,28},{16,0},{20,4},{24,8},{28,12},{1,17},{... | collective-permute-start | bytes 958472 | tf_op jit(solution)/shard_map/ppermute | solution.py:236
  19.2 16.6 %collective-permute-start.6 = (bf16[4,104,768]{2,1,0:T(8,128)(2,1)S(1)}, bf16[4,104,768]{2,1,0:T(8,128)(2,1)S(1)}, u32[]{:S(2)}, u32[]{:S(2)}) collective-permute-start(bf16[4,104,768]{2,1,0:T(8,128)(2,1)S(1)} %pad_maximum_fusion.2), channel_id=1, source_target_pairs={{0,4},{1,3},{2,6},{3,1},{4,0},{5,7},{6,2},{7,5},{8,12},{9,11},{10,... | collective-permute-start | bytes 1916936 | tf_op jit(solution)/shard_map/ppermute | solution.py:247
  20.9 12.4 %collective-permute-start.5 = (bf16[2,96,768]{2,1,0:T(8,128)(2,1)S(1)}, bf16[2,96,768]{2,1,0:T(8,128)(2,1)S(1)}, u32[]{:S(2)}, u32[]{:S(2)}) collective-permute-start(bf16[2,96,768]{2,1,0:T(8,128)(2,1)S(1)} %copy-done.44), channel_id=1, source_target_pairs={{0,8},{4,12},{8,0},{12,4},{16,24},{20,28},{24,16},{28,20},{1,9},{5... | collective-permute-start | bytes 884744 | tf_op jit(solution)/shard_map/ppermute | solution.py:236
  28.8 7.0 %collective-permute-start.4 = (bf16[2,104,768]{2,1,0:T(8,128)(2,1)S(1)}, bf16[2,104,768]{2,1,0:T(8,128)(2,1)S(1)}, u32[]{:S(2)}, u32[]{:S(2)}) collective-permute-start(bf16[2,104,768]{2,1,0:T(8,128)(2,1)S(1)} %collective-permute-done.3.refs_3_), channel_id=1, source_target_pairs={{0,2},{1,5},{2,0},{3,7},{4,6},{5,1},{6,4},{7,3},{8,10},{9,13},{10,... | collective-permute-start | bytes 958472 | tf_op jit(solution)/shard_map/ppermute | solution.py:247
  35.8 15.2 %collective-permute-start.7 = (bf16[4,104,768]{2,1,0:T(8,128)(2,1)S(1)}, bf16[4,104,768]{2,1,0:T(8,128)(2,1)}, u32[]{:S(2)}, u32[]{:S(2)}) collective-permute-start(bf16[4,104,768]{2,1,0:T(8,128)(2,1)S(1)} %pad_maximum_fusion.3), channel_id=1, source_target_pairs={{0,4},{1,3},{2,6},{3,1},{4,0},{5,7},{6,2},{7,5},{8,12},{9,11},{10,... | collective-permute-start | bytes 1916936 | tf_op jit(solution)/shard_map/ppermute | solution.py:247
  36.6 13.1 %collective-permute-start.8 = (bf16[2,2,96,768]{3,2,1,0:T(8,128)(2,1)S(1)}, bf16[2,2,96,768]{3,2,1,0:T(8,128)(2,1)S(1)}, u32[]{:S(2)}, u32[]{:S(2)}) collective-permute-start(bf16[2,2,96,768]{3,2,1,0:T(8,128)(2,1)S(1)} %pad_maximum_fusion.4.refs_0_), channel_id=1, source_target_pairs={{0,2},{1,5},{2,0},{3,7},{4,6},{5,1},{6,4},{7,3},{8,10},{9,13},{10,... | collective-permute-start | bytes 1769480 | tf_op jit(solution)/shard_map/ppermute | solution.py:247
  37.9 15.9 %collective-permute-start = (bf16[512,768]{1,0:T(8,128)(2,1)S(1)}, bf16[512,768]{1,0:T(8,128)(2,1)S(1)}, u32[]{:S(2)}, u32[]{:S(2)}) collective-permute-start(bf16[512,768]{1,0:T(8,128)(2,1)S(1)} %copy-done.5), channel_id=1, source_target_pairs={{0,1},{1,0},{2,3},{3,2},{4,5},{5,4},{6,7},{7,6},{8,9},{9,8},{10,11... | collective-permute-start | bytes 2359304 | tf_op jit(solution)/shard_map/ppermute | solution.py:231
  37.9 29.3 %collective-permute-start.9 = (bf16[2,2,96,768]{3,2,1,0:T(8,128)(2,1)S(1)}, bf16[2,2,96,768]{3,2,1,0:T(8,128)(2,1)S(1)}, u32[]{:S(2)}, u32[]{:S(2)}) collective-permute-start(bf16[2,2,96,768]{3,2,1,0:T(8,128)(2,1)S(1)} %pad_maximum_fusion.4.refs_0_), channel_id=1, source_target_pairs={{0,16},{4,20},{8,24},{12,28},{16,0},{20,4},{24,8},{28,12},{1,17},{... | collective-permute-start | bytes 1769480 | tf_op jit(solution)/shard_map/ppermute | solution.py:236
  52.2 28.7 %collective-permute-start.10 = (bf16[4,2,96,768]{3,2,1,0:T(8,128)(2,1)}, bf16[4,2,96,768]{3,2,1,0:T(8,128)(2,1)}, u32[]{:S(2)}, u32[]{:S(2)}) collective-permute-start(bf16[4,2,96,768]{3,2,1,0:T(8,128)(2,1)} %pad_maximum_fusion), channel_id=1, source_target_pairs={{0,4},{1,3},{2,6},{3,1},{4,0},{5,7},{6,2},{7,5},{8,12},{9,11},{10,... | collective-permute-start | bytes 3538952 | tf_op jit(solution)/shard_map/ppermute | solution.py:247
  67.2 13.7 %collective-permute-start.11 = (bf16[2,2,96,768]{3,2,1,0:T(8,128)(2,1)S(1)}, bf16[2,2,96,768]{3,2,1,0:T(8,128)(2,1)S(1)}, u32[]{:S(2)}, u32[]{:S(2)}) collective-permute-start(bf16[2,2,96,768]{3,2,1,0:T(8,128)(2,1)S(1)} %collective-permute-done.9.refs_3_), channel_id=1, source_target_pairs={{0,2},{1,5},{2,0},{3,7},{4,6},{5,1},{6,4},{7,3},{8,10},{9,13},{10,... | collective-permute-start | bytes 1769480 | tf_op jit(solution)/shard_map/ppermute | solution.py:247
  82.0 16.5 %collective-permute-start.13 = (bf16[4,2,96,768]{3,2,1,0:T(8,128)(2,1)}, bf16[4,2,96,768]{3,2,1,0:T(8,128)(2,1)}, u32[]{:S(2)}, u32[]{:S(2)}) collective-permute-start(bf16[4,2,96,768]{3,2,1,0:T(8,128)(2,1)} %pad_maximum_fusion.1), channel_id=1, source_target_pairs={{0,4},{1,3},{2,6},{3,1},{4,0},{5,7},{6,2},{7,5},{8,12},{9,11},{10,... | collective-permute-start | bytes 3538952 | tf_op jit(solution)/shard_map/ppermute | solution.py:247
  84.0 3.2 %collective-permute-start.12 = (bf16[512,768]{1,0:T(8,128)(2,1)S(1)}, bf16[512,768]{1,0:T(8,128)(2,1)}, u32[]{:S(2)}, u32[]{:S(2)}) collective-permute-start(bf16[512,768]{1,0:T(8,128)(2,1)S(1)} %convolution_convert_fusion), channel_id=1, source_target_pairs={{0,1},{1,0},{2,3},{3,2},{4,5},{5,4},{6,7},{7,6},{8,9},{9,8},{10,11... | collective-permute-start | bytes 2359304 | tf_op jit(solution)/shard_map/ppermute | solution.py:231
  115.6 2.6 %collective-permute-start.16 = (bf16[512,768]{1,0:T(8,128)(2,1)}, bf16[512,768]{1,0:T(8,128)(2,1)S(1)}, u32[]{:S(2)}, u32[]{:S(2)}) collective-permute-start(bf16[512,768]{1,0:T(8,128)(2,1)} %get-tuple-element.90), channel_id=1, source_target_pairs={{0,1},{1,0},{2,3},{3,2},{4,5},{5,4},{6,7},{7,6},{8,9},{9,8},{10,11... | collective-permute-start | bytes 2359304 | tf_op jit(solution)/shard_map/ppermute | solution.py:231
  148.5 2.7 %collective-permute-start.18 = (bf16[512,768]{1,0:T(8,128)(2,1)}, bf16[512,768]{1,0:T(8,128)(2,1)}, u32[]{:S(2)}, u32[]{:S(2)}) collective-permute-start(bf16[512,768]{1,0:T(8,128)(2,1)} %get-tuple-element.97), channel_id=1, source_target_pairs={{0,1},{1,0},{2,3},{3,2},{4,5},{5,4},{6,7},{7,6},{8,9},{9,8},{10,11... | collective-permute-start | bytes 2359304 | tf_op jit(solution)/shard_map/ppermute | solution.py:231
  148.7 28.8 %collective-permute-start.20 = (bf16[8,96,768]{2,1,0:T(8,128)(2,1)}, bf16[8,96,768]{2,1,0:T(8,128)(2,1)S(1)}, u32[]{:S(2)}, u32[]{:S(2)}) collective-permute-start(bf16[8,96,768]{2,1,0:T(8,128)(2,1)} %get-tuple-element.99), channel_id=1, source_target_pairs={{0,2},{1,5},{2,0},{3,7},{4,6},{5,1},{6,4},{7,3},{8,10},{9,13},{10,... | collective-permute-start | bytes 3538952 | tf_op jit(solution)/shard_map/ppermute | solution.py:247
  150.2 27.7 %collective-permute-start.21 = (bf16[8,96,768]{2,1,0:T(8,128)(2,1)}, bf16[8,96,768]{2,1,0:T(8,128)(2,1)S(1)}, u32[]{:S(2)}, u32[]{:S(2)}) collective-permute-start(bf16[8,96,768]{2,1,0:T(8,128)(2,1)} %get-tuple-element.100), channel_id=1, source_target_pairs={{0,2},{1,5},{2,0},{3,7},{4,6},{5,1},{6,4},{7,3},{8,10},{9,13},{10,... | collective-permute-start | bytes 3538952 | tf_op jit(solution)/shard_map/ppermute | solution.py:247
  178.9 14.5 %collective-permute-start.24 = (bf16[4,96,768]{2,1,0:T(8,128)(2,1)}, bf16[4,96,768]{2,1,0:T(8,128)(2,1)}, u32[]{:S(2)}, u32[]{:S(2)}) collective-permute-start(bf16[4,96,768]{2,1,0:T(8,128)(2,1)} %add_convert_fusion.8), channel_id=1, source_target_pairs={{0,4},{1,3},{2,6},{3,1},{4,0},{5,7},{6,2},{7,5},{8,12},{9,11},{10,... | collective-permute-start | bytes 1769480 | tf_op jit(solution)/shard_map/ppermute | solution.py:247
  181.3 14.2 %collective-permute-start.23 = (bf16[4,96,768]{2,1,0:T(8,128)(2,1)}, bf16[4,96,768]{2,1,0:T(8,128)(2,1)}, u32[]{:S(2)}, u32[]{:S(2)}) collective-permute-start(bf16[4,96,768]{2,1,0:T(8,128)(2,1)} %add_convert_fusion.9), channel_id=1, source_target_pairs={{0,4},{1,3},{2,6},{3,1},{4,0},{5,7},{6,2},{7,5},{8,12},{9,11},{10,... | collective-permute-start | bytes 1769480 | tf_op jit(solution)/shard_map/ppermute | solution.py:247
  195.4 17.5 %collective-permute-start.25 = (bf16[8,104,768]{2,1,0:T(8,128)(2,1)}, bf16[8,104,768]{2,1,0:T(8,128)(2,1)S(1)}, u32[]{:S(2)}, u32[]{:S(2)}) collective-permute-start(bf16[8,104,768]{2,1,0:T(8,128)(2,1)} %get-tuple-element.110), channel_id=1, source_target_pairs={{0,2},{1,5},{2,0},{3,7},{4,6},{5,1},{6,4},{7,3},{8,10},{9,13},{10,... | collective-permute-start | bytes 3833864 | tf_op jit(solution)/shard_map/ppermute | solution.py:247
  198.9 11.1 %collective-permute-start.28 = (bf16[96,768]{1,0:T(8,128)(2,1)}, bf16[96,768]{1,0:T(8,128)(2,1)S(1)}, u32[]{:S(2)}, u32[]{:S(2)}) collective-permute-start(bf16[96,768]{1,0:T(8,128)(2,1)} %get-tuple-element.187), channel_id=1, source_target_pairs={{0,24},{4,28},{8,16},{12,20},{16,8},{20,12},{24,0},{28,4},{1,25},{... | collective-permute-start | bytes 442376 | tf_op jit(solution)/shard_map/ppermute | solution.py:236
  200.9 11.5 %collective-permute-start.27 = (bf16[96,768]{1,0:T(8,128)(2,1)}, bf16[96,768]{1,0:T(8,128)(2,1)S(1)}, u32[]{:S(2)}, u32[]{:S(2)}) collective-permute-start(bf16[96,768]{1,0:T(8,128)(2,1)} %get-tuple-element.188), channel_id=1, source_target_pairs={{0,16},{4,20},{8,24},{12,28},{16,0},{20,4},{24,8},{28,12},{1,17},{... | collective-permute-start | bytes 442376 | tf_op jit(solution)/shard_map/ppermute | solution.py:236
  200.9 11.5 %collective-permute-start.26 = (bf16[96,768]{1,0:T(8,128)(2,1)}, bf16[96,768]{1,0:T(8,128)(2,1)S(1)}, u32[]{:S(2)}, u32[]{:S(2)}) collective-permute-start(bf16[96,768]{1,0:T(8,128)(2,1)} %get-tuple-element.189), channel_id=1, source_target_pairs={{0,8},{4,12},{8,0},{12,4},{16,24},{20,28},{24,16},{28,20},{1,9},{5... | collective-permute-start | bytes 442376 | tf_op jit(solution)/shard_map/ppermute | solution.py:236
  212.9 8.4 %collective-permute-start.30 = (bf16[512,768]{1,0:T(8,128)(2,1)}, bf16[512,768]{1,0:T(8,128)(2,1)S(1)}, u32[]{:S(2)}, u32[]{:S(2)}) collective-permute-start(bf16[512,768]{1,0:T(8,128)(2,1)} %get-tuple-element.118), channel_id=1, source_target_pairs={{0,1},{1,0},{2,3},{3,2},{4,5},{5,4},{6,7},{7,6},{8,9},{9,8},{10,11... | collective-permute-start | bytes 2359304 | tf_op jit(solution)/shard_map/ppermute | solution.py:231
  214.6 15.7 %collective-permute-start.29 = (bf16[4,104,768]{2,1,0:T(8,128)(2,1)S(1)}, bf16[4,104,768]{2,1,0:T(8,128)(2,1)S(1)}, u32[]{:S(2)}, u32[]{:S(2)}) collective-permute-start(bf16[4,104,768]{2,1,0:T(8,128)(2,1)S(1)} %add_convert_fusion.3), channel_id=1, source_target_pairs={{0,4},{1,3},{2,6},{3,1},{4,0},{5,7},{6,2},{7,5},{8,12},{9,11},{10,... | collective-permute-start | bytes 1916936 | tf_op jit(solution)/shard_map/ppermute | solution.py:247
  216.1 8.7 %collective-permute-start.33 = (bf16[96,768]{1,0:T(8,128)(2,1)S(1)}, bf16[96,768]{1,0:T(8,128)(2,1)S(1)}, u32[]{:S(2)}, u32[]{:S(2)}) collective-permute-start(bf16[96,768]{1,0:T(8,128)(2,1)S(1)} %get-tuple-element.184), channel_id=1, source_target_pairs={{0,24},{4,28},{8,16},{12,20},{16,8},{20,12},{24,0},{28,4},{1,25},{... | collective-permute-start | bytes 442376 | tf_op jit(solution)/shard_map/ppermute | solution.py:236
  217.6 12.7 %collective-permute-start.32 = (bf16[96,768]{1,0:T(8,128)(2,1)S(1)}, bf16[96,768]{1,0:T(8,128)(2,1)S(1)}, u32[]{:S(2)}, u32[]{:S(2)}) collective-permute-start(bf16[96,768]{1,0:T(8,128)(2,1)S(1)} %get-tuple-element.185), channel_id=1, source_target_pairs={{0,16},{4,20},{8,24},{12,28},{16,0},{20,4},{24,8},{28,12},{1,17},{... | collective-permute-start | bytes 442376 | tf_op jit(solution)/shard_map/ppermute | solution.py:236
  217.6 12.7 %collective-permute-start.31 = (bf16[96,768]{1,0:T(8,128)(2,1)S(1)}, bf16[96,768]{1,0:T(8,128)(2,1)S(1)}, u32[]{:S(2)}, u32[]{:S(2)}) collective-permute-start(bf16[96,768]{1,0:T(8,128)(2,1)S(1)} %get-tuple-element.186), channel_id=1, source_target_pairs={{0,8},{4,12},{8,0},{12,4},{16,24},{20,28},{24,16},{28,20},{1,9},{5... | collective-permute-start | bytes 442376 | tf_op jit(solution)/shard_map/ppermute | solution.py:236
  230.6 6.6 %collective-permute-start.34 = (bf16[104,768]{1,0:T(8,128)(2,1)S(1)}, bf16[104,768]{1,0:T(8,128)(2,1)S(1)}, u32[]{:S(2)}, u32[]{:S(2)}) collective-permute-start(bf16[104,768]{1,0:T(8,128)(2,1)S(1)} %get-tuple-element.181), channel_id=1, source_target_pairs={{0,8},{4,12},{8,0},{12,4},{16,24},{20,28},{24,16},{28,20},{1,9},{5... | collective-permute-start | bytes 479240 | tf_op jit(solution)/shard_map/ppermute | solution.py:236
  230.8 10.3 %collective-permute-start.36 = (bf16[104,768]{1,0:T(8,128)(2,1)S(1)}, bf16[104,768]{1,0:T(8,128)(2,1)S(1)}, u32[]{:S(2)}, u32[]{:S(2)}) collective-permute-start(bf16[104,768]{1,0:T(8,128)(2,1)S(1)} %get-tuple-element.182), channel_id=1, source_target_pairs={{0,24},{4,28},{8,16},{12,20},{16,8},{20,12},{24,0},{28,4},{1,25},{... | collective-permute-start | bytes 479240 | tf_op jit(solution)/shard_map/ppermute | solution.py:236
  232.7 15.5 %collective-permute-start.35 = (bf16[104,768]{1,0:T(8,128)(2,1)S(1)}, bf16[104,768]{1,0:T(8,128)(2,1)S(1)}, u32[]{:S(2)}, u32[]{:S(2)}) collective-permute-start(bf16[104,768]{1,0:T(8,128)(2,1)S(1)} %get-tuple-element.183), channel_id=1, source_target_pairs={{0,16},{4,20},{8,24},{12,28},{16,0},{20,4},{24,8},{28,12},{1,17},{... | collective-permute-start | bytes 479240 | tf_op jit(solution)/shard_map/ppermute | solution.py:236
  (51 other events, 406.3 us)

commit v3 on v2

--- a/solution.py
+++ b/solution.py
@@ -553,6 +553,7 @@
         ]
         + [jax.ShapeDtypeStruct(units, BF16)] * 4,
         cost_estimate=CHEAP,
+        compiler_params=pltpu.CompilerParams(vmem_limit_bytes=52 * 1024 * 1024),
         name="feed_back",
     )(where(), d_own, d_other, n_own, n_other, slope, hidden, c, b)
 
@@ -961,7 +962,7 @@
     sums = jnp.stack([d_bias_out, d_bias_down, d_gain_one, d_shift_one, d_gain_two, d_shift_two])
     sums = sums + swap(sums)
     d_ctx_other = dot_nn(da_other, o_t).astype(BF16)
-    d_ctx_other = go("P2", d_ctx_other)
+    d_ctx_other, sums = go("P2", d_ctx_other, sums)
     d_qkv, bias = attention_backward(qkv, ctx, lse, d_ctx, d_ctx_other, seg_col, seg_row, block)
     d_qkv = go("P3", d_qkv)
     attention_parts = [((0, 1), 2, part, 0, False), ((3, 4), 5, part, 3 * part, False)]

time: 252 us -> 253 us (level)
  local copies, waits for them, and re-layouts: 16.5 us -> 10.8 us
  matrix products: 3.55 us -> 6.22 us
  waiting for transfers between devices: 82.2 us -> 84.8 us
    unnamed x94 -> x82, local copies, waits for them, and re-layouts: 11.6 us -> 5.95 us
    ppermute x14, waiting for transfers between devices: 29.4 us -> 34.7 us  [turn(): return lax.ppermute(a, ('dp', 'x', 'c'), pairs)]
    ppermute x10, waiting for transfers between devices: 10.7 us -> 7.7 us  [swap(): return lax.ppermute(a, 'c', [(0, 1), (1, 0)])]
    dot_general x4, matrix products: 3.55 us -> 6.22 us  [dot(): return lax.dot_general(a, b, (dims, ((), ())), preferred_element_type=F32)]
  transfers between devices with their start and end apart: 37 -> 37, of which waited for: 25 -> 23; matrix products, arithmetic and copies ran while one was open for 9% -> 10% of each run, Pallas kernels for 19% -> 19%
where the time goes in v3:
time: 253 us; the launch traced here: 252 us
  waiting for transfers between devices  84.8 us (34%)
  Pallas kernels  84 us (33%)
  starting transfers between devices  39.5 us (16%)
  other arithmetic  25.3 us (10%)
  local copies, waits for them, and re-layouts  10.8 us (4%)
  matrix products  6.22 us (2%)
    ppermute x13, waiting for transfers between devices, flip(): return lax.ppermute(a, axis, [(i, i ^ bit) for i in range(n)])  42.5 us
    ppermute x14, waiting for transfers between devices, turn(): return lax.ppermute(a, ('dp', 'x', 'c'), pairs)  34.7 us
    ppermute x13, starting transfers between devices, flip(): return lax.ppermute(a, axis, [(i, i ^ bit) for i in range(n)])  20.5 us
    pallas_call x1, Pallas kernels, feed_back(): pl.pallas_call(functools.partial(feed_back_kernel, 256, piece), grid_spec...  20.2 us
    pallas_call x1, Pallas kernels, attention_backward(): pl.pallas_call(functools.partial(attention_backward_kernel, width, halves...  17.7 us
    ppermute x14, starting transfers between devices, turn(): return lax.ppermute(a, ('dp', 'x', 'c'), pairs)  17.2 us
    pallas_call x1, Pallas kernels, feed(): pl.pallas_call(functools.partial(feed_kernel, index, moves, halves), grid...  13.7 us
    pallas_call x1, Pallas kernels, attention_forward(): pl.pallas_call(functools.partial(attention_forward_kernel, width), grid=(...  10.7 us
  transfers between devices with their start and end apart: 37, of which 23 were waited for; matrix products, arithmetic and copies ran while one was open for 10% of the time, Pallas kernels for 19%

profile of v3, /device:TPU:0, one launch (start us, length us, event | category | flops | bytes accessed | tf_op | source)
XLA Modules:
  0.0 252.1 jit_solution(18401214664181949126)
XLA Ops:
  0.7 2.0 prepare_units.1
  2.7 3.0 %collective-permute-start.1 = (bf16[104,768]{1,0:T(8,128)(2,1)}, bf16[104,768]{1,0:T(8,128)(2,1)S(1)}, u32[]{:S(2)}, u32[]{:S(2)}) collective-permute-start(bf16[104,768]{1,0:T(8,128)(2,1)} %get-tuple-element.73), channel_id=1, source_target_pairs={{0,8},{4,12},{8,0},{12,4},{16,24},{20,28},{24,16},{28,20},{1,9},{5... | collective-permute-start | bytes 479240 | tf_op jit(solution)/shard_map/ppermute | solution.py:236
  5.7 4.3 %collective-permute-done.1 = bf16[104,768]{1,0:T(8,128)(2,1)S(1)} collective-permute-done((bf16[104,768]{1,0:T(8,128)(2,1)}, bf16[104,768]{1,0:T(8,128)(2,1)S(1)}, u32[]{:S(2)}, u32[]{:S(2)}) %collective-permute-start.1) | collective-permute-done | bytes 159776 | tf_op jit(solution)/shard_map/ppermute | solution.py:236
  12.8 2.6 %collective-permute-start.3 = (bf16[2,104,768]{2,1,0:T(8,128)(2,1)S(1)}, bf16[2,104,768]{2,1,0:T(8,128)(2,1)S(1)}, u32[]{:S(2)}, u32[]{:S(2)}) collective-permute-start(bf16[2,104,768]{2,1,0:T(8,128)(2,1)S(1)} %pad_maximum_fusion.5.refs_0_), channel_id=1, source_target_pairs={{0,16},{4,20},{8,24},{12,28},{16,0},{20,4},{24,8},{28,12},{1,17},{... | collective-permute-start | bytes 958472 | tf_op jit(solution)/shard_map/ppermute | solution.py:236
  15.3 2.7 %collective-permute-done.2.refs_1_ = bf16[2,104,768]{2,1,0:T(8,128)(2,1)S(1)} collective-permute-done((bf16[2,104,768]{2,1,0:T(8,128)(2,1)S(1)}, bf16[2,104,768]{2,1,0:T(8,128)(2,1)S(1)}, u32[]{:S(2)}, u32[]{:S(2)}) %collective-permute-start.2) | collective-permute-done | bytes 319520 | tf_op jit(solution)/shard_map/ppermute | solution.py:247
  22.5 6.2 %collective-permute-done.3.refs_3_ = bf16[2,104,768]{2,1,0:T(8,128)(2,1)S(1)} collective-permute-done((bf16[2,104,768]{2,1,0:T(8,128)(2,1)S(1)}, bf16[2,104,768]{2,1,0:T(8,128)(2,1)S(1)}, u32[]{:S(2)}, u32[]{:S(2)}) %collective-permute-start.3) | collective-permute-done | bytes 319520 | tf_op jit(solution)/shard_map/ppermute | solution.py:236
  30.3 3.1 %collective-permute-done.5 = bf16[2,96,768]{2,1,0:T(8,128)(2,1)S(1)} collective-permute-done((bf16[2,96,768]{2,1,0:T(8,128)(2,1)S(1)}, bf16[2,96,768]{2,1,0:T(8,128)(2,1)S(1)}, u32[]{:S(2)}, u32[]{:S(2)}) %collective-permute-start.5) | collective-permute-done | bytes 294944 | tf_op jit(solution)/shard_map/ppermute | solution.py:236
  33.5 2.3 collective-permute-done.4.refs_4_
  39.1 10.6 %collective-permute-done.8.refs_1_ = bf16[2,2,96,768]{3,2,1,0:T(8,128)(2,1)S(1)} collective-permute-done((bf16[2,2,96,768]{3,2,1,0:T(8,128)(2,1)S(1)}, bf16[2,2,96,768]{3,2,1,0:T(8,128)(2,1)S(1)}, u32[]{:S(2)}, u32[]{:S(2)}) %collective-permute-start.8) | collective-permute-done | bytes 589856 | tf_op jit(solution)/shard_map/ppermute | solution.py:247
  54.7 7.4 %project_kernel.1 = (bf16[1024,1152]{1,0:T(8,128)(2,1)}, bf16[768,1152]{1,0:T(8,128)(2,1)}, bf16[768,384]{1,0:T(8,128)(2,1)}, bf16[8,8,768]{2,1,0:T(8,128)(2,1)}) custom-call(s32[2]{0:T(128)} %pad_add_fusion.1.where_ref, bf16[512,768]{1,0:T(8,128)(2,1)} %refs_0_.1, bf16[512,768]{1,0:T(8,128)(2,1)} %copy-done.10, bf16[2,104,768]{2,1,0:T(8,128)(2,1)} %copy-done.31, ...), custom_call_target="tpu_custom_call" | custom-call | flops 1000 | bytes 1000 | tf_op jit(solution)/shard_map/project_kernel/pallas_call | solution.py:593
  62.2 5.2 %collective-permute-done.9.refs_3_ = bf16[2,2,96,768]{3,2,1,0:T(8,128)(2,1)S(1)} collective-permute-done((bf16[2,2,96,768]{3,2,1,0:T(8,128)(2,1)S(1)}, bf16[2,2,96,768]{3,2,1,0:T(8,128)(2,1)S(1)}, u32[]{:S(2)}, u32[]{:S(2)}) %collective-permute-start.9) | collective-permute-done | bytes 589856 | tf_op jit(solution)/shard_map/ppermute | solution.py:236
  70.1 10.7 %attention_forward.1 = (bf16[1024,384]{1,0:T(8,128)(2,1)S(1)}, f32[8,1024]{1,0:T(8,128)S(1)}) custom-call(s32[1024,1]{1,0:T(8,128)S(1)} %copy.31.seg_q_ref.seg_k_ref, s32[1,1024]{1,0:T(1,128)S(1)} %bitcast.87, bf16[1024,1152]{1,0:T(8,128)(2,1)S(1)} %copy-done.2, bf16[1024,1152]{1,0:T(8,128)(2,1)S(1)} %copy-done.2, bf16[1024,1152]{1,0:T(8,128)(2,1)S(1)} %copy-done.2), custom_call_target="tpu_custom_call" | custom-call | flops 1000 | bytes 1000 | tf_op jit(solution)/shard_map/attention_forward/pallas_call | solution.py:66
  89.0 9.6 %collective-permute-done.13.refs_5_ = bf16[4,2,96,768]{3,2,1,0:T(8,128)(2,1)} collective-permute-done((bf16[4,2,96,768]{3,2,1,0:T(8,128)(2,1)}, bf16[4,2,96,768]{3,2,1,0:T(8,128)(2,1)}, u32[]{:S(2)}, u32[]{:S(2)}) %collective-permute-start.13) | collective-permute-done | bytes 1179680 | tf_op jit(solution)/shard_map/ppermute | solution.py:247
  102.0 13.7 %feed_kernel.1 = (bf16[1024,1536]{1,0:T(8,128)(2,1)}, bf16[1024,1536]{1,0:T(8,128)(2,1)}, f32[512,768]{1,0:T(8,128)}, bf16[512,768]{1,0:T(8,128)(2,1)}, bf16[768...) custom-call(s32[2]{0:T(128)} %pad_add_fusion.1.where_ref, bf16[512,768]{1,0:T(8,128)(2,1)} %copy-done.20, ...), custom_call_target="tpu_custom_call" | custom-call | flops 1000 | bytes 1000 | tf_op jit(solution)/shard_map/feed_kernel/pallas_call | solution.py:626
  116.1 2.2 collective-permute-done.16
  118.3 2.1 fusion.21
  123.7 2.1 collective-permute-done.17.refs_1_
  126.7 20.2 %feed_back.1 = (f32[512,768]{1,0:T(8,128)}, bf16[512,768]{1,0:T(8,128)(2,1)S(1)}, f32[1,1536]{1,0:T(1,128)S(1)}, bf16[8,96,768]{2,1,0:T(8,128)(2,1)}, bf16[8,96,...) custom-call(s32[2]{0:T(128)S(1)} %copy-done.18, ...), custom_call_target="tpu_custom_call" | custom-call | flops 1000 | bytes 1000 | tf_op jit(solution)/shard_map/feed_back/pallas_call | solution.py:533
  149.4 3.9 %multiply_reduce_fusion = (f32[768]{0:T(1024)S(1)}, f32[512]{0:T(512)S(1)}, f32[512]{0:T(512)S(1)}, f32[768]{0:T(1024)S(1)}, f32[512,768]{1,0:T(8,128)S(1)}, /*index=5*/bf16[512,768]{1,0:T(8,128)(2,1)}) fusion(f32[512,768]{1,0:T(8,128)S(1)} %get-tuple-element.183, f32[512]{0:T(512)S(1)} %add_rsqrt_fusion.1, f32[512]{0:T(512)S(1)} %broadcast_multiply_fusion.5, ...), kind=kLoop, calls=%fused_computation.11 | loop fusion | flops 9041408 | bytes 8682496 | tf_op jit(solution)/shard_map/reduce_sum | solution.py:955
  159.6 17.7 %attention_backward.1 = (bf16[1024,1152]{1,0:T(8,128)(2,1)S(1)}, f32[1,768]{1,0:T(1,128)S(1)}) custom-call(s32[1024,1]{1,0:T(8,128)S(1)} %copy-done.9, s32[1,1024]{1,0:T(1,128)S(1)} %bitcast.88, bf16[1024,1152]{1,0:T(8,128)(2,1)S(1)} %copy-done.3, bf16[1024,1152]{1,0:T(8,128)(2,1)S(1)} %copy-done.3, bf16[1024,1152]{1,0:T(8,128)(2,1)S(1)} %copy-done.3, ...), custom_call_target="tpu_custom_call" | custom-call | flops 1000 | bytes 1000 | tf_op jit(solution)/shard_map/attention_backward/pallas_call | solution.py:163
  182.8 5.4 %sum_units.1 = (bf16[8,104,768]{2,1,0:T(8,128)(2,1)S(1)}, bf16[8,104,768]{2,1,0:T(8,128)(2,1)}) custom-call(s32[2]{0:T(128)S(1)} %copy-done.18, bf16[512,768]{1,0:T(8,128)(2,1)S(1)} %copy-done.7, bf16[512,768]{1,0:T(8,128)(2,1)S(1)} %copy-done.11, bf16[1024,1152]{1,0:T(8,128)(2,1)S(1)} %get-tuple-element.115.refs_2_.d_ref, bf16[512,768]{1,0:T(8,128)(2,1)S(1)} %copy-done.13, ...), custom_call_target="tpu_custom_call" | custom-call | flops 1000 | bytes 1000 | tf_op jit(solution)/shard_map/sum_units/pallas_call | solution.py:742
  189.3 6.3 %collective-permute-done.23 = bf16[4,96,768]{2,1,0:T(8,128)(2,1)S(1)} collective-permute-done((bf16[4,96,768]{2,1,0:T(8,128)(2,1)S(1)}, bf16[4,96,768]{2,1,0:T(8,128)(2,1)S(1)}, u32[]{:S(2)}, u32[]{:S(2)}) %collective-permute-start.23) | collective-permute-done | bytes 589856 | tf_op jit(solution)/shard_map/ppermute | solution.py:247
  201.0 2.6 %collective-permute-start.26 = (bf16[96,768]{1,0:T(8,128)(2,1)}, bf16[96,768]{1,0:T(8,128)(2,1)S(1)}, u32[]{:S(2)}, u32[]{:S(2)}) collective-permute-start(bf16[96,768]{1,0:T(8,128)(2,1)} %get-tuple-element.193), channel_id=1, source_target_pairs={{0,8},{4,12},{8,0},{12,4},{16,24},{20,28},{24,16},{28,20},{1,9},{5... | collective-permute-start | bytes 442376 | tf_op jit(solution)/shard_map/ppermute | solution.py:236
  203.6 6.7 %input_gradient.1 = (f32[512,768]{1,0:T(8,128)}, bf16[512,768]{1,0:T(8,128)(2,1)}) custom-call(bf16[1024,1152]{1,0:T(8,128)(2,1)} %copy-done.4, f32[512,768]{1,0:T(8,128)} %get-tuple-element.178.first_ref, bf16[768,1152]{1,0:T(8,128)(2,1)} %get-tuple-element.116.w_ref), custom_call_target="tpu_custom_call" | custom-call | flops 1000 | bytes 1000 | tf_op jit(solution)/shard_map/input_gradient/pallas_call | solution.py:204
  210.3 2.2 collective-permute-done.27
  217.7 2.9 %collective-permute-start.31 = (bf16[96,768]{1,0:T(8,128)(2,1)S(1)}, bf16[96,768]{1,0:T(8,128)(2,1)S(1)}, u32[]{:S(2)}, u32[]{:S(2)}) collective-permute-start(bf16[96,768]{1,0:T(8,128)(2,1)S(1)} %get-tuple-element.190), channel_id=1, source_target_pairs={{0,8},{4,12},{8,0},{12,4},{16,24},{20,28},{24,16},{28,20},{1,9},{5... | collective-permute-start | bytes 442376 | tf_op jit(solution)/shard_map/ppermute | solution.py:236
  222.5 2.4 collective-permute-done.33
  224.8 5.7 %collective-permute-done.32 = bf16[96,768]{1,0:T(8,128)(2,1)S(1)} collective-permute-done((bf16[96,768]{1,0:T(8,128)(2,1)S(1)}, bf16[96,768]{1,0:T(8,128)(2,1)S(1)}, u32[]{:S(2)}, u32[]{:S(2)}) %collective-permute-start.32) | collective-permute-done | bytes 147488 | tf_op jit(solution)/shard_map/ppermute | solution.py:236
  231.0 2.1 collective-permute-start.36
  235.2 2.6 %collective-permute-done.34 = bf16[104,768]{1,0:T(8,128)(2,1)S(1)} collective-permute-done((bf16[104,768]{1,0:T(8,128)(2,1)S(1)}, bf16[104,768]{1,0:T(8,128)(2,1)S(1)}, u32[]{:S(2)}, u32[]{:S(2)}) %collective-permute-start.34) | collective-permute-done | bytes 159776 | tf_op jit(solution)/shard_map/ppermute | solution.py:236
  237.8 3.7 %collective-permute-done.36 = bf16[104,768]{1,0:T(8,128)(2,1)S(1)} collective-permute-done((bf16[104,768]{1,0:T(8,128)(2,1)S(1)}, bf16[104,768]{1,0:T(8,128)(2,1)S(1)}, u32[]{:S(2)}, u32[]{:S(2)}) %collective-permute-start.36) | collective-permute-done | bytes 159776 | tf_op jit(solution)/shard_map/ppermute | solution.py:236
  241.5 7.0 %collective-permute-done.35 = bf16[104,768]{1,0:T(8,128)(2,1)S(1)} collective-permute-done((bf16[104,768]{1,0:T(8,128)(2,1)S(1)}, bf16[104,768]{1,0:T(8,128)(2,1)S(1)}, u32[]{:S(2)}, u32[]{:S(2)}) %collective-permute-start.35) | collective-permute-done | bytes 159776 | tf_op jit(solution)/shard_map/ppermute | solution.py:236
  (212 shorter events, 69.1 us)
Async XLA Ops:
  2.7 7.3 %collective-permute-start.1 = (bf16[104,768]{1,0:T(8,128)(2,1)}, bf16[104,768]{1,0:T(8,128)(2,1)S(1)}, u32[]{:S(2)}, u32[]{:S(2)}) collective-permute-start(bf16[104,768]{1,0:T(8,128)(2,1)} %get-tuple-element.73), channel_id=1, source_target_pairs={{0,8},{4,12},{8,0},{12,4},{16,24},{20,28},{24,16},{28,20},{1,9},{5... | collective-permute-start | bytes 479240 | tf_op jit(solution)/shard_map/ppermute | solution.py:236
  11.0 7.1 %collective-permute-start.2 = (bf16[2,104,768]{2,1,0:T(8,128)(2,1)S(1)}, bf16[2,104,768]{2,1,0:T(8,128)(2,1)S(1)}, u32[]{:S(2)}, u32[]{:S(2)}) collective-permute-start(bf16[2,104,768]{2,1,0:T(8,128)(2,1)S(1)} %pad_maximum_fusion.5.refs_0_), channel_id=1, source_target_pairs={{0,2},{1,5},{2,0},{3,7},{4,6},{5,1},{6,4},{7,3},{8,10},{9,13},{10,... | collective-permute-start | bytes 958472 | tf_op jit(solution)/shard_map/ppermute | solution.py:247
  12.8 16.0 %collective-permute-start.3 = (bf16[2,104,768]{2,1,0:T(8,128)(2,1)S(1)}, bf16[2,104,768]{2,1,0:T(8,128)(2,1)S(1)}, u32[]{:S(2)}, u32[]{:S(2)}) collective-permute-start(bf16[2,104,768]{2,1,0:T(8,128)(2,1)S(1)} %pad_maximum_fusion.5.refs_0_), channel_id=1, source_target_pairs={{0,16},{4,20},{8,24},{12,28},{16,0},{20,4},{24,8},{28,12},{1,17},{... | collective-permute-start | bytes 958472 | tf_op jit(solution)/shard_map/ppermute | solution.py:236
  19.2 16.6 %collective-permute-start.6 = (bf16[4,104,768]{2,1,0:T(8,128)(2,1)S(1)}, bf16[4,104,768]{2,1,0:T(8,128)(2,1)S(1)}, u32[]{:S(2)}, u32[]{:S(2)}) collective-permute-start(bf16[4,104,768]{2,1,0:T(8,128)(2,1)S(1)} %pad_maximum_fusion.2), channel_id=1, source_target_pairs={{0,4},{1,3},{2,6},{3,1},{4,0},{5,7},{6,2},{7,5},{8,12},{9,11},{10,... | collective-permute-start | bytes 1916936 | tf_op jit(solution)/shard_map/ppermute | solution.py:247
  20.9 12.4 %collective-permute-start.5 = (bf16[2,96,768]{2,1,0:T(8,128)(2,1)S(1)}, bf16[2,96,768]{2,1,0:T(8,128)(2,1)S(1)}, u32[]{:S(2)}, u32[]{:S(2)}) collective-permute-start(bf16[2,96,768]{2,1,0:T(8,128)(2,1)S(1)} %copy-done.38), channel_id=1, source_target_pairs={{0,8},{4,12},{8,0},{12,4},{16,24},{20,28},{24,16},{28,20},{1,9},{5... | collective-permute-start | bytes 884744 | tf_op jit(solution)/shard_map/ppermute | solution.py:236
  28.8 7.0 %collective-permute-start.4 = (bf16[2,104,768]{2,1,0:T(8,128)(2,1)S(1)}, bf16[2,104,768]{2,1,0:T(8,128)(2,1)S(1)}, u32[]{:S(2)}, u32[]{:S(2)}) collective-permute-start(bf16[2,104,768]{2,1,0:T(8,128)(2,1)S(1)} %collective-permute-done.3.refs_3_), channel_id=1, source_target_pairs={{0,2},{1,5},{2,0},{3,7},{4,6},{5,1},{6,4},{7,3},{8,10},{9,13},{10,... | collective-permute-start | bytes 958472 | tf_op jit(solution)/shard_map/ppermute | solution.py:247
  35.8 15.2 %collective-permute-start.7 = (bf16[4,104,768]{2,1,0:T(8,128)(2,1)S(1)}, bf16[4,104,768]{2,1,0:T(8,128)(2,1)}, u32[]{:S(2)}, u32[]{:S(2)}) collective-permute-start(bf16[4,104,768]{2,1,0:T(8,128)(2,1)S(1)} %pad_maximum_fusion.3), channel_id=1, source_target_pairs={{0,4},{1,3},{2,6},{3,1},{4,0},{5,7},{6,2},{7,5},{8,12},{9,11},{10,... | collective-permute-start | bytes 1916936 | tf_op jit(solution)/shard_map/ppermute | solution.py:247
  36.6 13.1 %collective-permute-start.8 = (bf16[2,2,96,768]{3,2,1,0:T(8,128)(2,1)S(1)}, bf16[2,2,96,768]{3,2,1,0:T(8,128)(2,1)S(1)}, u32[]{:S(2)}, u32[]{:S(2)}) collective-permute-start(bf16[2,2,96,768]{3,2,1,0:T(8,128)(2,1)S(1)} %pad_maximum_fusion.4.refs_0_), channel_id=1, source_target_pairs={{0,2},{1,5},{2,0},{3,7},{4,6},{5,1},{6,4},{7,3},{8,10},{9,13},{10,... | collective-permute-start | bytes 1769480 | tf_op jit(solution)/shard_map/ppermute | solution.py:247
  38.1 15.7 %collective-permute-start = (bf16[512,768]{1,0:T(8,128)(2,1)S(1)}, bf16[512,768]{1,0:T(8,128)(2,1)S(1)}, u32[]{:S(2)}, u32[]{:S(2)}) collective-permute-start(bf16[512,768]{1,0:T(8,128)(2,1)S(1)} %copy-done.5), channel_id=1, source_target_pairs={{0,1},{1,0},{2,3},{3,2},{4,5},{5,4},{6,7},{7,6},{8,9},{9,8},{10,11... | collective-permute-start | bytes 2359304 | tf_op jit(solution)/shard_map/ppermute | solution.py:231
  38.1 29.3 %collective-permute-start.9 = (bf16[2,2,96,768]{3,2,1,0:T(8,128)(2,1)S(1)}, bf16[2,2,96,768]{3,2,1,0:T(8,128)(2,1)S(1)}, u32[]{:S(2)}, u32[]{:S(2)}) collective-permute-start(bf16[2,2,96,768]{3,2,1,0:T(8,128)(2,1)S(1)} %pad_maximum_fusion.4.refs_0_), channel_id=1, source_target_pairs={{0,16},{4,20},{8,24},{12,28},{16,0},{20,4},{24,8},{28,12},{1,17},{... | collective-permute-start | bytes 1769480 | tf_op jit(solution)/shard_map/ppermute | solution.py:236
  52.2 28.7 %collective-permute-start.10 = (bf16[4,2,96,768]{3,2,1,0:T(8,128)(2,1)}, bf16[4,2,96,768]{3,2,1,0:T(8,128)(2,1)}, u32[]{:S(2)}, u32[]{:S(2)}) collective-permute-start(bf16[4,2,96,768]{3,2,1,0:T(8,128)(2,1)} %pad_maximum_fusion), channel_id=1, source_target_pairs={{0,4},{1,3},{2,6},{3,1},{4,0},{5,7},{6,2},{7,5},{8,12},{9,11},{10,... | collective-permute-start | bytes 3538952 | tf_op jit(solution)/shard_map/ppermute | solution.py:247
  67.4 13.5 %collective-permute-start.11 = (bf16[2,2,96,768]{3,2,1,0:T(8,128)(2,1)S(1)}, bf16[2,2,96,768]{3,2,1,0:T(8,128)(2,1)S(1)}, u32[]{:S(2)}, u32[]{:S(2)}) collective-permute-start(bf16[2,2,96,768]{3,2,1,0:T(8,128)(2,1)S(1)} %collective-permute-done.9.refs_3_), channel_id=1, source_target_pairs={{0,2},{1,5},{2,0},{3,7},{4,6},{5,1},{6,4},{7,3},{8,10},{9,13},{10,... | collective-permute-start | bytes 1769480 | tf_op jit(solution)/shard_map/ppermute | solution.py:247
  82.1 16.5 %collective-permute-start.13 = (bf16[4,2,96,768]{3,2,1,0:T(8,128)(2,1)}, bf16[4,2,96,768]{3,2,1,0:T(8,128)(2,1)}, u32[]{:S(2)}, u32[]{:S(2)}) collective-permute-start(bf16[4,2,96,768]{3,2,1,0:T(8,128)(2,1)} %pad_maximum_fusion.1), channel_id=1, source_target_pairs={{0,4},{1,3},{2,6},{3,1},{4,0},{5,7},{6,2},{7,5},{8,12},{9,11},{10,... | collective-permute-start | bytes 3538952 | tf_op jit(solution)/shard_map/ppermute | solution.py:247
  84.0 3.2 %collective-permute-start.12 = (bf16[512,768]{1,0:T(8,128)(2,1)S(1)}, bf16[512,768]{1,0:T(8,128)(2,1)}, u32[]{:S(2)}, u32[]{:S(2)}) collective-permute-start(bf16[512,768]{1,0:T(8,128)(2,1)S(1)} %convolution_convert_fusion), channel_id=1, source_target_pairs={{0,1},{1,0},{2,3},{3,2},{4,5},{5,4},{6,7},{7,6},{8,9},{9,8},{10,11... | collective-permute-start | bytes 2359304 | tf_op jit(solution)/shard_map/ppermute | solution.py:231
  115.8 2.6 %collective-permute-start.16 = (bf16[512,768]{1,0:T(8,128)(2,1)}, bf16[512,768]{1,0:T(8,128)(2,1)S(1)}, u32[]{:S(2)}, u32[]{:S(2)}) collective-permute-start(bf16[512,768]{1,0:T(8,128)(2,1)} %get-tuple-element.92), channel_id=1, source_target_pairs={{0,1},{1,0},{2,3},{3,2},{4,5},{5,4},{6,7},{7,6},{8,9},{9,8},{10,11... | collective-permute-start | bytes 2359304 | tf_op jit(solution)/shard_map/ppermute | solution.py:231
  147.2 30.2 %collective-permute-start.21 = (bf16[8,96,768]{2,1,0:T(8,128)(2,1)}, bf16[8,96,768]{2,1,0:T(8,128)(2,1)}, u32[]{:S(2)}, u32[]{:S(2)}) collective-permute-start(bf16[8,96,768]{2,1,0:T(8,128)(2,1)} %get-tuple-element.102), channel_id=1, source_target_pairs={{0,2},{1,5},{2,0},{3,7},{4,6},{5,1},{6,4},{7,3},{8,10},{9,13},{10,... | collective-permute-start | bytes 3538952 | tf_op jit(solution)/shard_map/ppermute | solution.py:247
  148.7 28.7 %collective-permute-start.22 = (bf16[8,96,768]{2,1,0:T(8,128)(2,1)}, bf16[8,96,768]{2,1,0:T(8,128)(2,1)}, u32[]{:S(2)}, u32[]{:S(2)}) collective-permute-start(bf16[8,96,768]{2,1,0:T(8,128)(2,1)} %get-tuple-element.103), channel_id=1, source_target_pairs={{0,2},{1,5},{2,0},{3,7},{4,6},{5,1},{6,4},{7,3},{8,10},{9,13},{10,... | collective-permute-start | bytes 3538952 | tf_op jit(solution)/shard_map/ppermute | solution.py:247
  155.0 2.6 %collective-permute-start.19 = (bf16[512,768]{1,0:T(8,128)(2,1)S(1)}, bf16[512,768]{1,0:T(8,128)(2,1)S(1)}, u32[]{:S(2)}, u32[]{:S(2)}) collective-permute-start(bf16[512,768]{1,0:T(8,128)(2,1)S(1)} %get-tuple-element.177.refs_3_), channel_id=1, source_target_pairs={{0,1},{1,0},{2,3},{3,2},{4,5},{5,4},{6,7},{7,6},{8,9},{9,8},{10,11... | collective-permute-start | bytes 2359304 | tf_op jit(solution)/shard_map/ppermute | solution.py:231
  179.3 9.9 %collective-permute-start.24 = (bf16[4,96,768]{2,1,0:T(8,128)(2,1)S(1)}, bf16[4,96,768]{2,1,0:T(8,128)(2,1)S(1)}, u32[]{:S(2)}, u32[]{:S(2)}) collective-permute-start(bf16[4,96,768]{2,1,0:T(8,128)(2,1)S(1)} %add_convert_fusion.8), channel_id=1, source_target_pairs={{0,4},{1,3},{2,6},{3,1},{4,0},{5,7},{6,2},{7,5},{8,12},{9,11},{10,... | collective-permute-start | bytes 1769480 | tf_op jit(solution)/shard_map/ppermute | solution.py:247
  182.0 13.6 %collective-permute-start.23 = (bf16[4,96,768]{2,1,0:T(8,128)(2,1)S(1)}, bf16[4,96,768]{2,1,0:T(8,128)(2,1)S(1)}, u32[]{:S(2)}, u32[]{:S(2)}) collective-permute-start(bf16[4,96,768]{2,1,0:T(8,128)(2,1)S(1)} %add_convert_fusion.9), channel_id=1, source_target_pairs={{0,4},{1,3},{2,6},{3,1},{4,0},{5,7},{6,2},{7,5},{8,12},{9,11},{10,... | collective-permute-start | bytes 1769480 | tf_op jit(solution)/shard_map/ppermute | solution.py:247
  195.6 17.5 %collective-permute-start.25 = (bf16[8,104,768]{2,1,0:T(8,128)(2,1)}, bf16[8,104,768]{2,1,0:T(8,128)(2,1)S(1)}, u32[]{:S(2)}, u32[]{:S(2)}) collective-permute-start(bf16[8,104,768]{2,1,0:T(8,128)(2,1)} %get-tuple-element.114), channel_id=1, source_target_pairs={{0,2},{1,5},{2,0},{3,7},{4,6},{5,1},{6,4},{7,3},{8,10},{9,13},{10,... | collective-permute-start | bytes 3833864 | tf_op jit(solution)/shard_map/ppermute | solution.py:247
  199.2 11.1 %collective-permute-start.28 = (bf16[96,768]{1,0:T(8,128)(2,1)}, bf16[96,768]{1,0:T(8,128)(2,1)S(1)}, u32[]{:S(2)}, u32[]{:S(2)}) collective-permute-start(bf16[96,768]{1,0:T(8,128)(2,1)} %get-tuple-element.191), channel_id=1, source_target_pairs={{0,24},{4,28},{8,16},{12,20},{16,8},{20,12},{24,0},{28,4},{1,25},{... | collective-permute-start | bytes 442376 | tf_op jit(solution)/shard_map/ppermute | solution.py:236
  201.0 11.5 %collective-permute-start.27 = (bf16[96,768]{1,0:T(8,128)(2,1)}, bf16[96,768]{1,0:T(8,128)(2,1)S(1)}, u32[]{:S(2)}, u32[]{:S(2)}) collective-permute-start(bf16[96,768]{1,0:T(8,128)(2,1)} %get-tuple-element.192), channel_id=1, source_target_pairs={{0,16},{4,20},{8,24},{12,28},{16,0},{20,4},{24,8},{28,12},{1,17},{... | collective-permute-start | bytes 442376 | tf_op jit(solution)/shard_map/ppermute | solution.py:236
  201.0 11.5 %collective-permute-start.26 = (bf16[96,768]{1,0:T(8,128)(2,1)}, bf16[96,768]{1,0:T(8,128)(2,1)S(1)}, u32[]{:S(2)}, u32[]{:S(2)}) collective-permute-start(bf16[96,768]{1,0:T(8,128)(2,1)} %get-tuple-element.193), channel_id=1, source_target_pairs={{0,8},{4,12},{8,0},{12,4},{16,24},{20,28},{24,16},{28,20},{1,9},{5... | collective-permute-start | bytes 442376 | tf_op jit(solution)/shard_map/ppermute | solution.py:236
  213.1 8.4 %collective-permute-start.30 = (bf16[512,768]{1,0:T(8,128)(2,1)}, bf16[512,768]{1,0:T(8,128)(2,1)S(1)}, u32[]{:S(2)}, u32[]{:S(2)}) collective-permute-start(bf16[512,768]{1,0:T(8,128)(2,1)} %get-tuple-element.122), channel_id=1, source_target_pairs={{0,1},{1,0},{2,3},{3,2},{4,5},{5,4},{6,7},{7,6},{8,9},{9,8},{10,11... | collective-permute-start | bytes 2359304 | tf_op jit(solution)/shard_map/ppermute | solution.py:231
  214.8 15.8 %collective-permute-start.29 = (bf16[4,104,768]{2,1,0:T(8,128)(2,1)S(1)}, bf16[4,104,768]{2,1,0:T(8,128)(2,1)S(1)}, u32[]{:S(2)}, u32[]{:S(2)}) collective-permute-start(bf16[4,104,768]{2,1,0:T(8,128)(2,1)S(1)} %add_convert_fusion.3), channel_id=1, source_target_pairs={{0,4},{1,3},{2,6},{3,1},{4,0},{5,7},{6,2},{7,5},{8,12},{9,11},{10,... | collective-permute-start | bytes 1916936 | tf_op jit(solution)/shard_map/ppermute | solution.py:247
  216.2 8.7 %collective-permute-start.33 = (bf16[96,768]{1,0:T(8,128)(2,1)S(1)}, bf16[96,768]{1,0:T(8,128)(2,1)S(1)}, u32[]{:S(2)}, u32[]{:S(2)}) collective-permute-start(bf16[96,768]{1,0:T(8,128)(2,1)S(1)} %get-tuple-element.188), channel_id=1, source_target_pairs={{0,24},{4,28},{8,16},{12,20},{16,8},{20,12},{24,0},{28,4},{1,25},{... | collective-permute-start | bytes 442376 | tf_op jit(solution)/shard_map/ppermute | solution.py:236
  217.7 12.9 %collective-permute-start.32 = (bf16[96,768]{1,0:T(8,128)(2,1)S(1)}, bf16[96,768]{1,0:T(8,128)(2,1)S(1)}, u32[]{:S(2)}, u32[]{:S(2)}) collective-permute-start(bf16[96,768]{1,0:T(8,128)(2,1)S(1)} %get-tuple-element.189), channel_id=1, source_target_pairs={{0,16},{4,20},{8,24},{12,28},{16,0},{20,4},{24,8},{28,12},{1,17},{... | collective-permute-start | bytes 442376 | tf_op jit(solution)/shard_map/ppermute | solution.py:236
  217.7 12.9 %collective-permute-start.31 = (bf16[96,768]{1,0:T(8,128)(2,1)S(1)}, bf16[96,768]{1,0:T(8,128)(2,1)S(1)}, u32[]{:S(2)}, u32[]{:S(2)}) collective-permute-start(bf16[96,768]{1,0:T(8,128)(2,1)S(1)} %get-tuple-element.190), channel_id=1, source_target_pairs={{0,8},{4,12},{8,0},{12,4},{16,24},{20,28},{24,16},{28,20},{1,9},{5... | collective-permute-start | bytes 442376 | tf_op jit(solution)/shard_map/ppermute | solution.py:236
  230.9 6.9 %collective-permute-start.34 = (bf16[104,768]{1,0:T(8,128)(2,1)S(1)}, bf16[104,768]{1,0:T(8,128)(2,1)S(1)}, u32[]{:S(2)}, u32[]{:S(2)}) collective-permute-start(bf16[104,768]{1,0:T(8,128)(2,1)S(1)} %get-tuple-element.185), channel_id=1, source_target_pairs={{0,8},{4,12},{8,0},{12,4},{16,24},{20,28},{24,16},{28,20},{1,9},{5... | collective-permute-start | bytes 479240 | tf_op jit(solution)/shard_map/ppermute | solution.py:236
  231.0 10.5 %collective-permute-start.36 = (bf16[104,768]{1,0:T(8,128)(2,1)S(1)}, bf16[104,768]{1,0:T(8,128)(2,1)S(1)}, u32[]{:S(2)}, u32[]{:S(2)}) collective-permute-start(bf16[104,768]{1,0:T(8,128)(2,1)S(1)} %get-tuple-element.186), channel_id=1, source_target_pairs={{0,24},{4,28},{8,16},{12,20},{16,8},{20,12},{24,0},{28,4},{1,25},{... | collective-permute-start | bytes 479240 | tf_op jit(solution)/shard_map/ppermute | solution.py:236
  233.0 15.5 %collective-permute-start.35 = (bf16[104,768]{1,0:T(8,128)(2,1)S(1)}, bf16[104,768]{1,0:T(8,128)(2,1)S(1)}, u32[]{:S(2)}, u32[]{:S(2)}) collective-permute-start(bf16[104,768]{1,0:T(8,128)(2,1)S(1)} %get-tuple-element.187), channel_id=1, source_target_pairs={{0,16},{4,20},{8,24},{12,28},{16,0},{20,4},{24,8},{28,12},{1,17},{... | collective-permute-start | bytes 479240 | tf_op jit(solution)/shard_map/ppermute | solution.py:236
  (45 other events, 410.0 us)

commit v4 on v3

--- a/solution.py
+++ b/solution.py
@@ -225,6 +225,58 @@
     first = jnp.mean(d_hat, axis=-1, keepdims=True)
     second = jnp.mean(d_hat * hat, axis=-1, keepdims=True)
     return inv * (d_hat - first - hat * second)
+
+
+def column_sums(sum_ref, *rows):
+    @pl.when(pl.program_id(0) == 0)
+    def _():
+        sum_ref[...] = jnp.zeros_like(sum_ref)
+
+    for k, r in enumerate(rows):
+        sum_ref[k : k + 1, :] += jnp.sum(r, axis=0, keepdims=True)
+
+
+def second_norm_kernel(keep_ref, got_ref, hat_ref, grad_ref, vec_ref, out_ref, low_ref, d_ref, sum_ref):
+    vec = vec_ref[...]
+    bias, gain_one, shift_one, gain, shift = [vec[k : k + 1] for k in range(1, 6)]
+    second = hat_ref[...] * gain_one + shift_one + keep_ref[...] + got_ref[...].astype(F32) + bias
+    hat, inv = normalize(second)
+    out_ref[...] = (hat * gain + shift).astype(BF16)
+    grad = grad_ref[...].astype(F32)
+    d = normalize_back(hat, inv, gain, grad)
+    d_ref[...] = d
+    low = d.astype(BF16)
+    low_ref[...] = low
+    column_sums(sum_ref, low.astype(F32), grad * hat, grad)
+
+
+def first_norm_kernel(keep_ref, got_ref, d_ref, hat_ref, inv_ref, vec_ref, low_ref, out_ref, sum_ref):
+    hat = hat_ref[...]
+    d_normed = d_ref[...] + keep_ref[...] + got_ref[...].astype(F32)
+    d = normalize_back(hat, inv_ref[...], vec_ref[2:3, :], d_normed)
+    out_ref[...] = d
+    low = d.astype(BF16)
+    low_ref[...] = low
+    column_sums(sum_ref, low.astype(F32), d_normed * hat, d_normed)
+
+
+def norm_call(kernel, block, arrays, vectors, types):
+    rows, model = arrays[0].shape
+
+    def by_row(n):
+        return pl.BlockSpec((block, n), lambda i: (i, 0))
+
+    fixed = pl.BlockSpec((8, model), lambda i: (0, 0))
+    return pl.pallas_call(
+        kernel,
+        grid=(rows // block,),
+        in_specs=[by_row(a.shape[1]) for a in arrays] + [fixed],
+        out_specs=[by_row(model) for _ in types] + [fixed],
+        out_shape=[jax.ShapeDtypeStruct((rows, model), t) for t in types] + [jax.ShapeDtypeStruct((8, model), F32)],
+        cost_estimate=CHEAP,
+        compiler_params=pltpu.CompilerParams(vmem_limit_bytes=30 * 1024 * 1024),
+        name=kernel.__name__,
+    )(*arrays, vectors)
 
 
 def swap(a):
@@ -908,17 +960,10 @@
     normed_other = swap(normed_low)
     normed_other = advance("feed", normed_other)
     hidden, slope, keep, send, b_all, c_all = feed([bc_near, bc_far], normed_low, normed_other, bias_up, piece, block)
-    branch = keep + swap(send).astype(F32)
-    second = normed + branch + bdown_f
-    hat_two, inv_two = normalize(second)
-    layer_out = (hat_two * gtwo_f + stwo_f).astype(BF16)
-
-    g_in = grad_out.astype(F32)
-    d_gain_two = jnp.sum(g_in * hat_two, axis=0)
-    d_shift_two = jnp.sum(g_in, axis=0)
-    d_second = normalize_back(hat_two, inv_two, gtwo_f, g_in)
-    d_branch = d_second.astype(BF16)
-    d_bias_down = jnp.sum(d_branch.astype(F32), axis=0)
+    vectors = jnp.pad(vectors, ((0, 2), (0, 0)))
+    layer_out, d_branch, d_second, sums_two = norm_call(
+        second_norm_kernel, block, [keep, swap(send), hat_one, grad_out], vectors, [BF16, BF16, F32]
+    )
     db_other = swap(d_branch)
 
     sc = sb = sa = None
@@ -950,16 +995,13 @@
     )
     sc, sb = Scatter(pairs[:2]), Scatter(pairs[2:])
     go("P0")
-    d_normed = d_second + keep + swap(send).astype(F32)
-    d_normed = go("P1", d_normed)
-    d_gain_one = jnp.sum(d_normed * hat_one, axis=0)
-    d_shift_one = jnp.sum(d_normed, axis=0)
-    d_first = normalize_back(hat_one, inv_one, gone_f, d_normed)
-    d_attn = d_first.astype(BF16)
-    d_bias_out = jnp.sum(d_attn.astype(F32), axis=0)
+    send = go("P1", swap(send))
+    d_attn, d_first, sums_one = norm_call(
+        first_norm_kernel, block, [keep, send, d_second, hat_one, inv_one], vectors, [BF16, F32]
+    )
     da_other = swap(d_attn)
     d_ctx = dot_nn(d_attn, o_t).astype(BF16)
-    sums = jnp.stack([d_bias_out, d_bias_down, d_gain_one, d_shift_one, d_gain_two, d_shift_two])
+    sums = jnp.concatenate([sums_one[:1], sums_two[:1], sums_one[1:3], sums_two[1:3]])
     sums = sums + swap(sums)
     d_ctx_other = dot_nn(da_other, o_t).astype(BF16)
     d_ctx_other, sums = go("P2", d_ctx_other, sums)

time: 253 us -> 255 us (level)
  other arithmetic: 25.3 us -> 17.1 us
  Pallas kernels: 84 us -> 89.1 us
  local copies, waits for them, and re-layouts: 10.8 us -> 15.7 us
    reduce_sum x4 -> x0, other arithmetic: 6.94 us -> none  [the longest x1 3.91 us: local(): d_gain_one = jnp.sum(d_normed * hat_one, axis=0)]
    unnamed x82 -> x84, local copies, waits for them, and re-layouts: 5.95 us -> 11 us
    pallas_call x0 -> x2, Pallas kernels: none -> 4.81 us  [norm_call(): pl.pallas_call(kernel, grid=(rows // block,), in_specs=[by_row(a.shape[1]...]
  transfers between devices with their start and end apart: 37 -> 37, of which waited for: 23 -> 24; matrix products, arithmetic and copies ran while one was open for 10% -> 7% of each run, Pallas kernels for 19% -> 19%
where the time goes in v4:
time: 255 us; the launch traced here: 254 us
  Pallas kernels  89.1 us (35%)
  waiting for transfers between devices  85.9 us (34%)
  starting transfers between devices  41 us (16%)
  other arithmetic  17.1 us (7%)
  local copies, waits for them, and re-layouts  15.7 us (6%)
  matrix products  4.42 us (2%)
    ppermute x13, waiting for transfers between devices, flip(): return lax.ppermute(a, axis, [(i, i ^ bit) for i in range(n)])  42.4 us
    ppermute x14, waiting for transfers between devices, turn(): return lax.ppermute(a, ('dp', 'x', 'c'), pairs)  34.2 us
    ppermute x13, starting transfers between devices, flip(): return lax.ppermute(a, axis, [(i, i ^ bit) for i in range(n)])  22.3 us
    pallas_call x1, Pallas kernels, feed_back(): pl.pallas_call(functools.partial(feed_back_kernel, 256, piece), grid_spec...  20.4 us
    pallas_call x1, Pallas kernels, attention_backward(): pl.pallas_call(functools.partial(attention_backward_kernel, width, halves...  17.7 us
    ppermute x14, starting transfers between devices, turn(): return lax.ppermute(a, ('dp', 'x', 'c'), pairs)  17.1 us
    pallas_call x1, Pallas kernels, feed(): pl.pallas_call(functools.partial(feed_kernel, index, moves, halves), grid...  13.7 us
    unnamed x84, local copies, waits for them, and re-layouts  11 us
  transfers between devices with their start and end apart: 37, of which 24 were waited for; matrix products, arithmetic and copies ran while one was open for 7% of the time, Pallas kernels for 19%

profile of v4, /device:TPU:0, one launch (start us, length us, event | category | flops | bytes accessed | tf_op | source)
XLA Modules:
  0.0 254.4 jit_solution(17073821546114926825)
XLA Ops:
  0.7 2.0 prepare_units.1
  2.7 3.0 %collective-permute-start.1 = (bf16[104,768]{1,0:T(8,128)(2,1)}, bf16[104,768]{1,0:T(8,128)(2,1)S(1)}, u32[]{:S(2)}, u32[]{:S(2)}) collective-permute-start(bf16[104,768]{1,0:T(8,128)(2,1)} %get-tuple-element.80), channel_id=1, source_target_pairs={{0,8},{4,12},{8,0},{12,4},{16,24},{20,28},{24,16},{28,20},{1,9},{5... | collective-permute-start | bytes 479240 | tf_op jit(solution)/shard_map/ppermute | solution.py:288
  5.7 4.3 %collective-permute-done.1 = bf16[104,768]{1,0:T(8,128)(2,1)S(1)} collective-permute-done((bf16[104,768]{1,0:T(8,128)(2,1)}, bf16[104,768]{1,0:T(8,128)(2,1)S(1)}, u32[]{:S(2)}, u32[]{:S(2)}) %collective-permute-start.1) | collective-permute-done | bytes 159776 | tf_op jit(solution)/shard_map/ppermute | solution.py:288
  12.7 2.6 %collective-permute-start.3 = (bf16[2,104,768]{2,1,0:T(8,128)(2,1)S(1)}, bf16[2,104,768]{2,1,0:T(8,128)(2,1)S(1)}, u32[]{:S(2)}, u32[]{:S(2)}) collective-permute-start(bf16[2,104,768]{2,1,0:T(8,128)(2,1)S(1)} %pad_maximum_fusion.5.refs_0_), channel_id=1, source_target_pairs={{0,16},{4,20},{8,24},{12,28},{16,0},{20,4},{24,8},{28,12},{1,17},{... | collective-permute-start | bytes 958472 | tf_op jit(solution)/shard_map/ppermute | solution.py:288
  15.3 2.7 %collective-permute-done.2.refs_1_ = bf16[2,104,768]{2,1,0:T(8,128)(2,1)S(1)} collective-permute-done((bf16[2,104,768]{2,1,0:T(8,128)(2,1)S(1)}, bf16[2,104,768]{2,1,0:T(8,128)(2,1)S(1)}, u32[]{:S(2)}, u32[]{:S(2)}) %collective-permute-start.2) | collective-permute-done | bytes 319520 | tf_op jit(solution)/shard_map/ppermute | solution.py:299
  22.5 6.2 %collective-permute-done.3.refs_3_ = bf16[2,104,768]{2,1,0:T(8,128)(2,1)S(1)} collective-permute-done((bf16[2,104,768]{2,1,0:T(8,128)(2,1)S(1)}, bf16[2,104,768]{2,1,0:T(8,128)(2,1)S(1)}, u32[]{:S(2)}, u32[]{:S(2)}) %collective-permute-start.3) | collective-permute-done | bytes 319520 | tf_op jit(solution)/shard_map/ppermute | solution.py:288
  30.2 3.1 %collective-permute-done.5 = bf16[2,96,768]{2,1,0:T(8,128)(2,1)S(1)} collective-permute-done((bf16[2,96,768]{2,1,0:T(8,128)(2,1)S(1)}, bf16[2,96,768]{2,1,0:T(8,128)(2,1)S(1)}, u32[]{:S(2)}, u32[]{:S(2)}) %collective-permute-start.5) | collective-permute-done | bytes 294944 | tf_op jit(solution)/shard_map/ppermute | solution.py:288
  33.5 2.3 collective-permute-done.4.refs_4_
  39.1 10.6 %collective-permute-done.8.refs_1_ = bf16[2,2,96,768]{3,2,1,0:T(8,128)(2,1)S(1)} collective-permute-done((bf16[2,2,96,768]{3,2,1,0:T(8,128)(2,1)S(1)}, bf16[2,2,96,768]{3,2,1,0:T(8,128)(2,1)S(1)}, u32[]{:S(2)}, u32[]{:S(2)}) %collective-permute-start.8) | collective-permute-done | bytes 589856 | tf_op jit(solution)/shard_map/ppermute | solution.py:299
  54.7 7.4 %project_kernel.1 = (bf16[1024,1152]{1,0:T(8,128)(2,1)}, bf16[768,1152]{1,0:T(8,128)(2,1)}, bf16[768,384]{1,0:T(8,128)(2,1)}, bf16[8,8,768]{2,1,0:T(8,128)(2,1)}) custom-call(s32[2]{0:T(128)} %pad_add_fusion.1.where_ref, bf16[512,768]{1,0:T(8,128)(2,1)} %refs_0_.1, bf16[512,768]{1,0:T(8,128)(2,1)} %copy-done.11, bf16[2,104,768]{2,1,0:T(8,128)(2,1)} %copy-done.32, ...), custom_call_target="tpu_custom_call" | custom-call | flops 1000 | bytes 1000 | tf_op jit(solution)/shard_map/project_kernel/pallas_call | solution.py:645
  62.2 5.0 %collective-permute-done.9.refs_3_ = bf16[2,2,96,768]{3,2,1,0:T(8,128)(2,1)S(1)} collective-permute-done((bf16[2,2,96,768]{3,2,1,0:T(8,128)(2,1)S(1)}, bf16[2,2,96,768]{3,2,1,0:T(8,128)(2,1)S(1)}, u32[]{:S(2)}, u32[]{:S(2)}) %collective-permute-start.9) | collective-permute-done | bytes 589856 | tf_op jit(solution)/shard_map/ppermute | solution.py:288
  68.2 1.8 copy-done.2
  70.0 10.7 %attention_forward.1 = (bf16[1024,384]{1,0:T(8,128)(2,1)S(1)}, f32[8,1024]{1,0:T(8,128)S(1)}) custom-call(s32[1024,1]{1,0:T(8,128)S(1)} %copy.31.seg_q_ref.seg_k_ref, s32[1,1024]{1,0:T(1,128)S(1)} %bitcast.88, bf16[1024,1152]{1,0:T(8,128)(2,1)S(1)} %copy-done.2, bf16[1024,1152]{1,0:T(8,128)(2,1)S(1)} %copy-done.2, bf16[1024,1152]{1,0:T(8,128)(2,1)S(1)} %copy-done.2), custom_call_target="tpu_custom_call" | custom-call | flops 1000 | bytes 1000 | tf_op jit(solution)/shard_map/attention_forward/pallas_call | solution.py:66
  89.6 8.9 %collective-permute-done.13.refs_5_ = bf16[4,2,96,768]{3,2,1,0:T(8,128)(2,1)} collective-permute-done((bf16[4,2,96,768]{3,2,1,0:T(8,128)(2,1)}, bf16[4,2,96,768]{3,2,1,0:T(8,128)(2,1)}, u32[]{:S(2)}, u32[]{:S(2)}) %collective-permute-start.13) | collective-permute-done | bytes 1179680 | tf_op jit(solution)/shard_map/ppermute | solution.py:299
  101.5 1.9 collective-permute-done.15.other_ref.refs_3_
  103.4 13.7 %feed_kernel.1 = (bf16[1024,1536]{1,0:T(8,128)(2,1)}, bf16[1024,1536]{1,0:T(8,128)(2,1)}, f32[512,768]{1,0:T(8,128)}, bf16[512,768]{1,0:T(8,128)(2,1)}, bf16[768...) custom-call(s32[2]{0:T(128)} %pad_add_fusion.1.where_ref, bf16[512,768]{1,0:T(8,128)(2,1)} %get-tuple-element.177.own_ref.refs_2_, ...), custom_call_target="tpu_custom_call" | custom-call | flops 1000 | bytes 1000 | tf_op jit(solution)/shard_map/feed_kernel/pallas_call | solution.py:678
  117.5 2.3 collective-permute-done.16.got_ref
  121.2 3.5 %second_norm_kernel.1 = (bf16[512,768]{1,0:T(8,128)(2,1)}, bf16[512,768]{1,0:T(8,128)(2,1)S(1)}, f32[512,768]{1,0:T(8,128)S(1)}, f32[8,768]{1,0:T(8,128)S(1)}) custom-call(f32[512,768]{1,0:T(8,128)S(1)} %copy-done.17, bf16[512,768]{1,0:T(8,128)(2,1)} %collective-permute-done.16.got_ref, f32[512,768]{1,0:T(8,128)S(1)} %get-tuple-element.178.hat_ref, ...), custom_call_target="tpu_custom_call" | custom-call | flops 1000 | bytes 1000 | tf_op jit(solution)/shard_map/second_norm_kernel/pallas_call | solution.py:270
  126.0 2.1 collective-permute-done.17.refs_1_
  129.0 20.4 %feed_back.1 = (f32[512,768]{1,0:T(8,128)}, bf16[512,768]{1,0:T(8,128)(2,1)}, f32[1,1536]{1,0:T(1,128)S(1)}, bf16[8,96,768]{2,1,0:T(8,128)(2,1)}, bf16[8,96,768]...) custom-call(s32[2]{0:T(128)S(1)} %copy-done.21, ...), custom_call_target="tpu_custom_call" | custom-call | flops 1000 | bytes 1000 | tf_op jit(solution)/shard_map/feed_back/pallas_call | solution.py:585
  160.2 17.7 %attention_backward.1 = (bf16[1024,1152]{1,0:T(8,128)(2,1)S(1)}, f32[1,768]{1,0:T(1,128)S(1)}) custom-call(s32[1024,1]{1,0:T(8,128)S(1)} %copy-done.10, s32[1,1024]{1,0:T(1,128)S(1)} %bitcast.89, bf16[1024,1152]{1,0:T(8,128)(2,1)S(1)} %copy-done.3, bf16[1024,1152]{1,0:T(8,128)(2,1)S(1)} %copy-done.3, bf16[1024,1152]{1,0:T(8,128)(2,1)S(1)} %copy-done.3, ...), custom_call_target="tpu_custom_call" | custom-call | flops 1000 | bytes 1000 | tf_op jit(solution)/shard_map/attention_backward/pallas_call | solution.py:163
  183.9 5.5 %sum_units.1 = (bf16[8,104,768]{2,1,0:T(8,128)(2,1)S(1)}, bf16[8,104,768]{2,1,0:T(8,128)(2,1)}) custom-call(s32[2]{0:T(128)S(1)} %copy-done.21, bf16[512,768]{1,0:T(8,128)(2,1)S(1)} %copy-done.5, bf16[512,768]{1,0:T(8,128)(2,1)S(1)} %copy-done.12, bf16[1024,1152]{1,0:T(8,128)(2,1)S(1)} %get-tuple-element.128.refs_2_.d_ref, ...), custom_call_target="tpu_custom_call" | custom-call | flops 1000 | bytes 1000 | tf_op jit(solution)/shard_map/sum_units/pallas_call | solution.py:794
  190.4 6.3 %collective-permute-done.24 = bf16[4,96,768]{2,1,0:T(8,128)(2,1)S(1)} collective-permute-done((bf16[4,96,768]{2,1,0:T(8,128)(2,1)S(1)}, bf16[4,96,768]{2,1,0:T(8,128)(2,1)S(1)}, u32[]{:S(2)}, u32[]{:S(2)}) %collective-permute-start.24) | collective-permute-done | bytes 589856 | tf_op jit(solution)/shard_map/ppermute | solution.py:299
  200.2 2.6 %collective-permute-start.27 = (bf16[96,768]{1,0:T(8,128)(2,1)}, bf16[96,768]{1,0:T(8,128)(2,1)S(1)}, u32[]{:S(2)}, u32[]{:S(2)}) collective-permute-start(bf16[96,768]{1,0:T(8,128)(2,1)} %get-tuple-element.186), channel_id=1, source_target_pairs={{0,16},{4,20},{8,24},{12,28},{16,0},{20,4},{24,8},{28,12},{1,17},{... | collective-permute-start | bytes 442376 | tf_op jit(solution)/shard_map/ppermute | solution.py:288
  204.6 6.7 %input_gradient.1 = (f32[512,768]{1,0:T(8,128)}, bf16[512,768]{1,0:T(8,128)(2,1)}) custom-call(bf16[1024,1152]{1,0:T(8,128)(2,1)} %copy-done.6, f32[512,768]{1,0:T(8,128)} %copy-done.13, bf16[768,1152]{1,0:T(8,128)(2,1)} %get-tuple-element.130.w_ref), custom_call_target="tpu_custom_call" | custom-call | flops 1000 | bytes 1000 | tf_op jit(solution)/shard_map/input_gradient/pallas_call | solution.py:204
  211.3 2.7 %collective-permute-done.27 = bf16[96,768]{1,0:T(8,128)(2,1)S(1)} collective-permute-done((bf16[96,768]{1,0:T(8,128)(2,1)}, bf16[96,768]{1,0:T(8,128)(2,1)S(1)}, u32[]{:S(2)}, u32[]{:S(2)}) %collective-permute-start.27) | collective-permute-done | bytes 147488 | tf_op jit(solution)/shard_map/ppermute | solution.py:288
  219.3 2.5 collective-permute-start.33
  223.7 2.0 collective-permute-done.31
  225.7 7.0 %collective-permute-done.32 = bf16[96,768]{1,0:T(8,128)(2,1)S(1)} collective-permute-done((bf16[96,768]{1,0:T(8,128)(2,1)S(1)}, bf16[96,768]{1,0:T(8,128)(2,1)S(1)}, u32[]{:S(2)}, u32[]{:S(2)}) %collective-permute-start.32) | collective-permute-done | bytes 147488 | tf_op jit(solution)/shard_map/ppermute | solution.py:288
  234.6 3.4 %collective-permute-start.35 = (bf16[104,768]{1,0:T(8,128)(2,1)S(1)}, bf16[104,768]{1,0:T(8,128)(2,1)S(1)}, u32[]{:S(2)}, u32[]{:S(2)}) collective-permute-start(bf16[104,768]{1,0:T(8,128)(2,1)S(1)} %get-tuple-element.181), channel_id=1, source_target_pairs={{0,16},{4,20},{8,24},{12,28},{16,0},{20,4},{24,8},{28,12},{1,17},{... | collective-permute-start | bytes 479240 | tf_op jit(solution)/shard_map/ppermute | solution.py:288
  238.8 2.9 %collective-permute-done.36 = bf16[104,768]{1,0:T(8,128)(2,1)S(1)} collective-permute-done((bf16[104,768]{1,0:T(8,128)(2,1)S(1)}, bf16[104,768]{1,0:T(8,128)(2,1)S(1)}, u32[]{:S(2)}, u32[]{:S(2)}) %collective-permute-start.36) | collective-permute-done | bytes 159776 | tf_op jit(solution)/shard_map/ppermute | solution.py:288
  241.7 9.1 %collective-permute-done.35 = bf16[104,768]{1,0:T(8,128)(2,1)S(1)} collective-permute-done((bf16[104,768]{1,0:T(8,128)(2,1)S(1)}, bf16[104,768]{1,0:T(8,128)(2,1)S(1)}, u32[]{:S(2)}, u32[]{:S(2)}) %collective-permute-start.35) | collective-permute-done | bytes 159776 | tf_op jit(solution)/shard_map/ppermute | solution.py:288
  (204 shorter events, 69.9 us)
Async XLA Ops:
  2.7 7.3 %collective-permute-start.1 = (bf16[104,768]{1,0:T(8,128)(2,1)}, bf16[104,768]{1,0:T(8,128)(2,1)S(1)}, u32[]{:S(2)}, u32[]{:S(2)}) collective-permute-start(bf16[104,768]{1,0:T(8,128)(2,1)} %get-tuple-element.80), channel_id=1, source_target_pairs={{0,8},{4,12},{8,0},{12,4},{16,24},{20,28},{24,16},{28,20},{1,9},{5... | collective-permute-start | bytes 479240 | tf_op jit(solution)/shard_map/ppermute | solution.py:288
  11.0 7.1 %collective-permute-start.2 = (bf16[2,104,768]{2,1,0:T(8,128)(2,1)S(1)}, bf16[2,104,768]{2,1,0:T(8,128)(2,1)S(1)}, u32[]{:S(2)}, u32[]{:S(2)}) collective-permute-start(bf16[2,104,768]{2,1,0:T(8,128)(2,1)S(1)} %pad_maximum_fusion.5.refs_0_), channel_id=1, source_target_pairs={{0,2},{1,5},{2,0},{3,7},{4,6},{5,1},{6,4},{7,3},{8,10},{9,13},{10,... | collective-permute-start | bytes 958472 | tf_op jit(solution)/shard_map/ppermute | solution.py:299
  12.7 16.0 %collective-permute-start.3 = (bf16[2,104,768]{2,1,0:T(8,128)(2,1)S(1)}, bf16[2,104,768]{2,1,0:T(8,128)(2,1)S(1)}, u32[]{:S(2)}, u32[]{:S(2)}) collective-permute-start(bf16[2,104,768]{2,1,0:T(8,128)(2,1)S(1)} %pad_maximum_fusion.5.refs_0_), channel_id=1, source_target_pairs={{0,16},{4,20},{8,24},{12,28},{16,0},{20,4},{24,8},{28,12},{1,17},{... | collective-permute-start | bytes 958472 | tf_op jit(solution)/shard_map/ppermute | solution.py:288
  19.2 16.6 %collective-permute-start.6 = (bf16[4,104,768]{2,1,0:T(8,128)(2,1)S(1)}, bf16[4,104,768]{2,1,0:T(8,128)(2,1)S(1)}, u32[]{:S(2)}, u32[]{:S(2)}) collective-permute-start(bf16[4,104,768]{2,1,0:T(8,128)(2,1)S(1)} %pad_maximum_fusion.2), channel_id=1, source_target_pairs={{0,4},{1,3},{2,6},{3,1},{4,0},{5,7},{6,2},{7,5},{8,12},{9,11},{10,... | collective-permute-start | bytes 1916936 | tf_op jit(solution)/shard_map/ppermute | solution.py:299
  20.9 12.4 %collective-permute-start.5 = (bf16[2,96,768]{2,1,0:T(8,128)(2,1)S(1)}, bf16[2,96,768]{2,1,0:T(8,128)(2,1)S(1)}, u32[]{:S(2)}, u32[]{:S(2)}) collective-permute-start(bf16[2,96,768]{2,1,0:T(8,128)(2,1)S(1)} %copy-done.39), channel_id=1, source_target_pairs={{0,8},{4,12},{8,0},{12,4},{16,24},{20,28},{24,16},{28,20},{1,9},{5... | collective-permute-start | bytes 884744 | tf_op jit(solution)/shard_map/ppermute | solution.py:288
  28.8 7.0 %collective-permute-start.4 = (bf16[2,104,768]{2,1,0:T(8,128)(2,1)S(1)}, bf16[2,104,768]{2,1,0:T(8,128)(2,1)S(1)}, u32[]{:S(2)}, u32[]{:S(2)}) collective-permute-start(bf16[2,104,768]{2,1,0:T(8,128)(2,1)S(1)} %collective-permute-done.3.refs_3_), channel_id=1, source_target_pairs={{0,2},{1,5},{2,0},{3,7},{4,6},{5,1},{6,4},{7,3},{8,10},{9,13},{10,... | collective-permute-start | bytes 958472 | tf_op jit(solution)/shard_map/ppermute | solution.py:299
  35.8 15.2 %collective-permute-start.7 = (bf16[4,104,768]{2,1,0:T(8,128)(2,1)S(1)}, bf16[4,104,768]{2,1,0:T(8,128)(2,1)}, u32[]{:S(2)}, u32[]{:S(2)}) collective-permute-start(bf16[4,104,768]{2,1,0:T(8,128)(2,1)S(1)} %pad_maximum_fusion.3), channel_id=1, source_target_pairs={{0,4},{1,3},{2,6},{3,1},{4,0},{5,7},{6,2},{7,5},{8,12},{9,11},{10,... | collective-permute-start | bytes 1916936 | tf_op jit(solution)/shard_map/ppermute | solution.py:299
  36.6 13.1 %collective-permute-start.8 = (bf16[2,2,96,768]{3,2,1,0:T(8,128)(2,1)S(1)}, bf16[2,2,96,768]{3,2,1,0:T(8,128)(2,1)S(1)}, u32[]{:S(2)}, u32[]{:S(2)}) collective-permute-start(bf16[2,2,96,768]{3,2,1,0:T(8,128)(2,1)S(1)} %pad_maximum_fusion.4.refs_0_), channel_id=1, source_target_pairs={{0,2},{1,5},{2,0},{3,7},{4,6},{5,1},{6,4},{7,3},{8,10},{9,13},{10,... | collective-permute-start | bytes 1769480 | tf_op jit(solution)/shard_map/ppermute | solution.py:299
  37.9 15.9 %collective-permute-start = (bf16[512,768]{1,0:T(8,128)(2,1)S(1)}, bf16[512,768]{1,0:T(8,128)(2,1)S(1)}, u32[]{:S(2)}, u32[]{:S(2)}) collective-permute-start(bf16[512,768]{1,0:T(8,128)(2,1)S(1)} %copy-done.4), channel_id=1, source_target_pairs={{0,1},{1,0},{2,3},{3,2},{4,5},{5,4},{6,7},{7,6},{8,9},{9,8},{10,11... | collective-permute-start | bytes 2359304 | tf_op jit(solution)/shard_map/ppermute | solution.py:283
  37.9 29.3 %collective-permute-start.9 = (bf16[2,2,96,768]{3,2,1,0:T(8,128)(2,1)S(1)}, bf16[2,2,96,768]{3,2,1,0:T(8,128)(2,1)S(1)}, u32[]{:S(2)}, u32[]{:S(2)}) collective-permute-start(bf16[2,2,96,768]{3,2,1,0:T(8,128)(2,1)S(1)} %pad_maximum_fusion.4.refs_0_), channel_id=1, source_target_pairs={{0,16},{4,20},{8,24},{12,28},{16,0},{20,4},{24,8},{28,12},{1,17},{... | collective-permute-start | bytes 1769480 | tf_op jit(solution)/shard_map/ppermute | solution.py:288
  52.2 28.7 %collective-permute-start.10 = (bf16[4,2,96,768]{3,2,1,0:T(8,128)(2,1)}, bf16[4,2,96,768]{3,2,1,0:T(8,128)(2,1)}, u32[]{:S(2)}, u32[]{:S(2)}) collective-permute-start(bf16[4,2,96,768]{3,2,1,0:T(8,128)(2,1)} %pad_maximum_fusion), channel_id=1, source_target_pairs={{0,4},{1,3},{2,6},{3,1},{4,0},{5,7},{6,2},{7,5},{8,12},{9,11},{10,... | collective-permute-start | bytes 3538952 | tf_op jit(solution)/shard_map/ppermute | solution.py:299
  67.2 13.7 %collective-permute-start.11 = (bf16[2,2,96,768]{3,2,1,0:T(8,128)(2,1)S(1)}, bf16[2,2,96,768]{3,2,1,0:T(8,128)(2,1)S(1)}, u32[]{:S(2)}, u32[]{:S(2)}) collective-permute-start(bf16[2,2,96,768]{3,2,1,0:T(8,128)(2,1)S(1)} %collective-permute-done.9.refs_3_), channel_id=1, source_target_pairs={{0,2},{1,5},{2,0},{3,7},{4,6},{5,1},{6,4},{7,3},{8,10},{9,13},{10,... | collective-permute-start | bytes 1769480 | tf_op jit(solution)/shard_map/ppermute | solution.py:299
  82.0 16.5 %collective-permute-start.13 = (bf16[4,2,96,768]{3,2,1,0:T(8,128)(2,1)}, bf16[4,2,96,768]{3,2,1,0:T(8,128)(2,1)}, u32[]{:S(2)}, u32[]{:S(2)}) collective-permute-start(bf16[4,2,96,768]{3,2,1,0:T(8,128)(2,1)} %pad_maximum_fusion.1), channel_id=1, source_target_pairs={{0,4},{1,3},{2,6},{3,1},{4,0},{5,7},{6,2},{7,5},{8,12},{9,11},{10,... | collective-permute-start | bytes 3538952 | tf_op jit(solution)/shard_map/ppermute | solution.py:299
  84.9 2.9 %collective-permute-start.12 = (bf16[512,768]{1,0:T(8,128)(2,1)}, bf16[512,768]{1,0:T(8,128)(2,1)}, u32[]{:S(2)}, u32[]{:S(2)}) collective-permute-start(bf16[512,768]{1,0:T(8,128)(2,1)} %convolution_convert_fusion), channel_id=1, source_target_pairs={{0,1},{1,0},{2,3},{3,2},{4,5},{5,4},{6,7},{7,6},{8,9},{9,8},{10,11... | collective-permute-start | bytes 2359304 | tf_op jit(solution)/shard_map/ppermute | solution.py:283
  100.7 2.6 %collective-permute-start.15 = (bf16[512,768]{1,0:T(8,128)(2,1)}, bf16[512,768]{1,0:T(8,128)(2,1)}, u32[]{:S(2)}, u32[]{:S(2)}) collective-permute-start(bf16[512,768]{1,0:T(8,128)(2,1)} %get-tuple-element.177.own_ref.refs_2_), channel_id=1, source_target_pairs={{0,1},{1,0},{2,3},{3,2},{4,5},{5,4},{6,7},{7,6},{8,9},{9,8},{10,11... | collective-permute-start | bytes 2359304 | tf_op jit(solution)/shard_map/ppermute | solution.py:283
  117.1 2.7 %collective-permute-start.16 = (bf16[512,768]{1,0:T(8,128)(2,1)}, bf16[512,768]{1,0:T(8,128)(2,1)}, u32[]{:S(2)}, u32[]{:S(2)}) collective-permute-start(bf16[512,768]{1,0:T(8,128)(2,1)} %get-tuple-element.99), channel_id=1, source_target_pairs={{0,1},{1,0},{2,3},{3,2},{4,5},{5,4},{6,7},{7,6},{8,9},{9,8},{10,11... | collective-permute-start | bytes 2359304 | tf_op jit(solution)/shard_map/ppermute | solution.py:283
  149.6 28.4 %collective-permute-start.21 = (bf16[8,96,768]{2,1,0:T(8,128)(2,1)}, bf16[8,96,768]{2,1,0:T(8,128)(2,1)}, u32[]{:S(2)}, u32[]{:S(2)}) collective-permute-start(bf16[8,96,768]{2,1,0:T(8,128)(2,1)} %get-tuple-element.115), channel_id=1, source_target_pairs={{0,2},{1,5},{2,0},{3,7},{4,6},{5,1},{6,4},{7,3},{8,10},{9,13},{10,... | collective-permute-start | bytes 3538952 | tf_op jit(solution)/shard_map/ppermute | solution.py:299
  150.9 27.8 %collective-permute-start.22 = (bf16[8,96,768]{2,1,0:T(8,128)(2,1)}, bf16[8,96,768]{2,1,0:T(8,128)(2,1)}, u32[]{:S(2)}, u32[]{:S(2)}) collective-permute-start(bf16[8,96,768]{2,1,0:T(8,128)(2,1)} %get-tuple-element.116), channel_id=1, source_target_pairs={{0,2},{1,5},{2,0},{3,7},{4,6},{5,1},{6,4},{7,3},{8,10},{9,13},{10,... | collective-permute-start | bytes 3538952 | tf_op jit(solution)/shard_map/ppermute | solution.py:299
  180.5 9.9 %collective-permute-start.23 = (bf16[4,96,768]{2,1,0:T(8,128)(2,1)S(1)}, bf16[4,96,768]{2,1,0:T(8,128)(2,1)S(1)}, u32[]{:S(2)}, u32[]{:S(2)}) collective-permute-start(bf16[4,96,768]{2,1,0:T(8,128)(2,1)S(1)} %add_convert_fusion.9), channel_id=1, source_target_pairs={{0,4},{1,3},{2,6},{3,1},{4,0},{5,7},{6,2},{7,5},{8,12},{9,11},{10,... | collective-permute-start | bytes 1769480 | tf_op jit(solution)/shard_map/ppermute | solution.py:299
  183.1 13.6 %collective-permute-start.24 = (bf16[4,96,768]{2,1,0:T(8,128)(2,1)S(1)}, bf16[4,96,768]{2,1,0:T(8,128)(2,1)S(1)}, u32[]{:S(2)}, u32[]{:S(2)}) collective-permute-start(bf16[4,96,768]{2,1,0:T(8,128)(2,1)S(1)} %add_convert_fusion.8), channel_id=1, source_target_pairs={{0,4},{1,3},{2,6},{3,1},{4,0},{5,7},{6,2},{7,5},{8,12},{9,11},{10,... | collective-permute-start | bytes 1769480 | tf_op jit(solution)/shard_map/ppermute | solution.py:299
  196.7 17.5 %collective-permute-start.25 = (bf16[8,104,768]{2,1,0:T(8,128)(2,1)}, bf16[8,104,768]{2,1,0:T(8,128)(2,1)S(1)}, u32[]{:S(2)}, u32[]{:S(2)}) collective-permute-start(bf16[8,104,768]{2,1,0:T(8,128)(2,1)} %get-tuple-element.127), channel_id=1, source_target_pairs={{0,2},{1,5},{2,0},{3,7},{4,6},{5,1},{6,4},{7,3},{8,10},{9,13},{10,... | collective-permute-start | bytes 3833864 | tf_op jit(solution)/shard_map/ppermute | solution.py:299
  200.2 11.1 %collective-permute-start.26 = (bf16[96,768]{1,0:T(8,128)(2,1)}, bf16[96,768]{1,0:T(8,128)(2,1)S(1)}, u32[]{:S(2)}, u32[]{:S(2)}) collective-permute-start(bf16[96,768]{1,0:T(8,128)(2,1)} %get-tuple-element.187), channel_id=1, source_target_pairs={{0,8},{4,12},{8,0},{12,4},{16,24},{20,28},{24,16},{28,20},{1,9},{5... | collective-permute-start | bytes 442376 | tf_op jit(solution)/shard_map/ppermute | solution.py:288
  200.2 13.8 %collective-permute-start.27 = (bf16[96,768]{1,0:T(8,128)(2,1)}, bf16[96,768]{1,0:T(8,128)(2,1)S(1)}, u32[]{:S(2)}, u32[]{:S(2)}) collective-permute-start(bf16[96,768]{1,0:T(8,128)(2,1)} %get-tuple-element.186), channel_id=1, source_target_pairs={{0,16},{4,20},{8,24},{12,28},{16,0},{20,4},{24,8},{28,12},{1,17},{... | collective-permute-start | bytes 442376 | tf_op jit(solution)/shard_map/ppermute | solution.py:288
  202.8 11.2 %collective-permute-start.28 = (bf16[96,768]{1,0:T(8,128)(2,1)}, bf16[96,768]{1,0:T(8,128)(2,1)S(1)}, u32[]{:S(2)}, u32[]{:S(2)}) collective-permute-start(bf16[96,768]{1,0:T(8,128)(2,1)} %get-tuple-element.185), channel_id=1, source_target_pairs={{0,24},{4,28},{8,16},{12,20},{16,8},{20,12},{24,0},{28,4},{1,25},{... | collective-permute-start | bytes 442376 | tf_op jit(solution)/shard_map/ppermute | solution.py:288
  214.2 8.4 %collective-permute-start.30 = (bf16[512,768]{1,0:T(8,128)(2,1)}, bf16[512,768]{1,0:T(8,128)(2,1)S(1)}, u32[]{:S(2)}, u32[]{:S(2)}) collective-permute-start(bf16[512,768]{1,0:T(8,128)(2,1)} %get-tuple-element.136), channel_id=1, source_target_pairs={{0,1},{1,0},{2,3},{3,2},{4,5},{5,4},{6,7},{7,6},{8,9},{9,8},{10,11... | collective-permute-start | bytes 2359304 | tf_op jit(solution)/shard_map/ppermute | solution.py:283
  215.9 16.7 %collective-permute-start.29 = (bf16[4,104,768]{2,1,0:T(8,128)(2,1)S(1)}, bf16[4,104,768]{2,1,0:T(8,128)(2,1)S(1)}, u32[]{:S(2)}, u32[]{:S(2)}) collective-permute-start(bf16[4,104,768]{2,1,0:T(8,128)(2,1)S(1)} %add_convert_fusion.3), channel_id=1, source_target_pairs={{0,4},{1,3},{2,6},{3,1},{4,0},{5,7},{6,2},{7,5},{8,12},{9,11},{10,... | collective-permute-start | bytes 1916936 | tf_op jit(solution)/shard_map/ppermute | solution.py:299
  217.4 8.3 %collective-permute-start.31 = (bf16[96,768]{1,0:T(8,128)(2,1)S(1)}, bf16[96,768]{1,0:T(8,128)(2,1)S(1)}, u32[]{:S(2)}, u32[]{:S(2)}) collective-permute-start(bf16[96,768]{1,0:T(8,128)(2,1)S(1)} %get-tuple-element.184), channel_id=1, source_target_pairs={{0,8},{4,12},{8,0},{12,4},{16,24},{20,28},{24,16},{28,20},{1,9},{5... | collective-permute-start | bytes 442376 | tf_op jit(solution)/shard_map/ppermute | solution.py:288
  218.6 14.0 %collective-permute-start.32 = (bf16[96,768]{1,0:T(8,128)(2,1)S(1)}, bf16[96,768]{1,0:T(8,128)(2,1)S(1)}, u32[]{:S(2)}, u32[]{:S(2)}) collective-permute-start(bf16[96,768]{1,0:T(8,128)(2,1)S(1)} %get-tuple-element.183), channel_id=1, source_target_pairs={{0,16},{4,20},{8,24},{12,28},{16,0},{20,4},{24,8},{28,12},{1,17},{... | collective-permute-start | bytes 442376 | tf_op jit(solution)/shard_map/ppermute | solution.py:288
  219.3 13.3 %collective-permute-start.33 = (bf16[96,768]{1,0:T(8,128)(2,1)S(1)}, bf16[96,768]{1,0:T(8,128)(2,1)S(1)}, u32[]{:S(2)}, u32[]{:S(2)}) collective-permute-start(bf16[96,768]{1,0:T(8,128)(2,1)S(1)} %get-tuple-element.182), channel_id=1, source_target_pairs={{0,24},{4,28},{8,16},{12,20},{16,8},{20,12},{24,0},{28,4},{1,25},{... | collective-permute-start | bytes 442376 | tf_op jit(solution)/shard_map/ppermute | solution.py:288
  232.9 8.8 %collective-permute-start.36 = (bf16[104,768]{1,0:T(8,128)(2,1)S(1)}, bf16[104,768]{1,0:T(8,128)(2,1)S(1)}, u32[]{:S(2)}, u32[]{:S(2)}) collective-permute-start(bf16[104,768]{1,0:T(8,128)(2,1)S(1)} %get-tuple-element.180), channel_id=1, source_target_pairs={{0,24},{4,28},{8,16},{12,20},{16,8},{20,12},{24,0},{28,4},{1,25},{... | collective-permute-start | bytes 479240 | tf_op jit(solution)/shard_map/ppermute | solution.py:288
  234.6 16.2 %collective-permute-start.35 = (bf16[104,768]{1,0:T(8,128)(2,1)S(1)}, bf16[104,768]{1,0:T(8,128)(2,1)S(1)}, u32[]{:S(2)}, u32[]{:S(2)}) collective-permute-start(bf16[104,768]{1,0:T(8,128)(2,1)S(1)} %get-tuple-element.181), channel_id=1, source_target_pairs={{0,16},{4,20},{8,24},{12,28},{16,0},{20,4},{24,8},{28,12},{1,17},{... | collective-permute-start | bytes 479240 | tf_op jit(solution)/shard_map/ppermute | solution.py:288
  238.0 12.8 %collective-permute-start.34 = (bf16[104,768]{1,0:T(8,128)(2,1)S(1)}, bf16[104,768]{1,0:T(8,128)(2,1)S(1)}, u32[]{:S(2)}, u32[]{:S(2)}) collective-permute-start(bf16[104,768]{1,0:T(8,128)(2,1)S(1)} %get-tuple-element.179), channel_id=1, source_target_pairs={{0,8},{4,12},{8,0},{12,4},{16,24},{20,28},{24,16},{28,20},{1,9},{5... | collective-permute-start | bytes 479240 | tf_op jit(solution)/shard_map/ppermute | solution.py:288
  (46 other events, 407.6 us)
